TPU v7x, 512 devices: a whole 4x8x8 slice. The times are simulated.
512 devices in a mesh: dp: 32 (over y, x), fsdp: 16 (over z, core).
Axes of the slice: x: 4, y: 8, z: 8, core: 2. Of those that a mesh axis runs over, the one named last changes fastest.
Arguments:
- hidden: bfloat16 [131072, 8192], P(('dp', 'fsdp')), may hold values from -6 to 6
- lengths: int32 [2048], P(('dp', 'fsdp')), may hold values from 16 to 112, as said below
- learner: int32 [2048], P(('dp', 'fsdp')), may hold values from 0 to 31, as said below
- slot_offset: int32 [2048], P(('dp', 'fsdp')), may hold values from 0 to 240, as said below
- norm_gain: bfloat16 [8192], P('fsdp'), may hold values from 0.099609375 to 1.8984375
- query_weight: bfloat16 [8192, 512], P('fsdp'), may hold values from -2 to 2
- keyval_weight: bfloat16 [8192, 256], P('fsdp'), may hold values from -2 to 2
Outputs:
- attended: bfloat16 [131072, 512], P(('dp', 'fsdp'))
Inputs may be any that keep to these rules, and one draw needn't show every extreme that they name: Rows 2k and 2k+1 of one device form a pair whose lengths sum to 128; a device's rows fill its 256 slots in order. Both rows of a pair go to the same learner; every learner receives exactly 2 pairs from the devices of its fsdp index. `slot_offset`: the rows that one learner receives tile its 256 slots without gaps, in some order.
All inputs are finite; a program needn't handle non-finite values.
Results may differ from a plain program's by a relative error of at most 0.0076.
Values may be sent and summed in bfloat16 or wider, within the bound.
No kernel may reach another device: no remote copies, remote signals or barrier semaphores. Data moves between devices by JAX's collectives and lax.ppermute only.
A program may use at most 128 MiB of HBM per device.

v0:
```python
import jax
import jax.numpy as jnp
from jax import lax
from jax.sharding import PartitionSpec as P

HD = 128
QH = 4


rope_base = 500000.0
norm_eps = 1e-05


def rotate(values, positions):
    midpoint = values.shape[-1] // 2
    frequency = rope_base ** (-jnp.arange(midpoint, dtype=jnp.float32) * 2.0 / values.shape[-1])
    angles = positions.astype(jnp.float32)[:, None] * frequency[None, :]
    cosine = jnp.cos(angles)[:, None, :]
    sines = jnp.sin(angles)[:, None, :]
    leading = values[..., :midpoint]
    trailing = values[..., midpoint:]
    return jnp.concatenate(
        [leading * cosine - trailing * sines, trailing * cosine + leading * sines], -1
    )


def project(rows, positions, norm_gain, query_weight, keyval_weight):
    inverse = lax.rsqrt(
        jnp.mean(jnp.square(rows.astype(jnp.float32)), axis=1, keepdims=True) + norm_eps
    )
    gain_piece = lax.all_gather(norm_gain, "fsdp", axis=0, tiled=True)
    query_piece = lax.all_gather(query_weight, "fsdp", axis=0, tiled=True)
    kv_piece = lax.all_gather(keyval_weight, "fsdp", axis=0, tiled=True)
    normed = (rows.astype(jnp.float32) * inverse * gain_piece.astype(jnp.float32)[None, :]).astype(
        jnp.bfloat16
    )
    query = jnp.dot(normed, query_piece, preferred_element_type=jnp.float32)
    key_value = jnp.dot(normed, kv_piece, preferred_element_type=jnp.float32)
    query = rotate(query.reshape(-1, QH, HD), positions).reshape(-1, QH * HD)
    key_part = rotate(key_value[:, :HD].reshape(-1, 1, HD), positions).reshape(-1, HD)
    return jnp.concatenate([query, key_part, key_value[:, HD:]], axis=1).astype(jnp.bfloat16)


def source_positions(lengths, slot_count):
    starts = jnp.cumsum(lengths) - lengths
    places = jnp.arange(slot_count, dtype=jnp.int32)
    relative = places[:, None] - starts[None, :]
    inside = (relative >= 0) & (relative < lengths[None, :])
    return jnp.sum(jnp.where(inside, relative, 0), axis=1)


def route(buffer, tables):
    channels = buffer.shape[1]
    peer_count = lax.axis_size("dp")
    pair_count = tables.shape[1] // (2 * peer_count)
    block_len = buffer.shape[0] // pair_count
    slice_len = block_len // peer_count
    blocks = buffer.reshape(pair_count, peer_count, slice_len, channels)
    spread = lax.all_to_all(blocks, "dp", split_axis=1, concat_axis=0, tiled=True)
    lengths_all = tables[0].reshape(peer_count * pair_count, 2)
    targets = tables[1].reshape(peer_count * pair_count, 2)[:, 0]
    offsets_all = tables[2].reshape(peer_count * pair_count, 2)
    ordering = jnp.argsort(targets, stable=True)
    arranged = jnp.take(spread, ordering, axis=0).reshape(
        peer_count, pair_count, 1, slice_len, channels
    )
    received = lax.all_to_all(arranged, "dp", split_axis=0, concat_axis=2, tiled=True)
    received = received.reshape(pair_count * block_len, channels)
    own_blocks = lax.dynamic_slice_in_dim(ordering, lax.axis_index("dp") * pair_count, pair_count)
    pair_lengths = jnp.take(lengths_all, own_blocks, axis=0)
    sources = jnp.stack([jnp.zeros_like(pair_lengths[:, 0]), pair_lengths[:, 0]], axis=1)
    sources = (sources + (jnp.arange(pair_count, dtype=jnp.int32) * block_len)[:, None]).reshape(-1)
    row_lengths = pair_lengths.reshape(-1)
    row_offsets = jnp.take(offsets_all, own_blocks, axis=0).reshape(-1)
    places = jnp.arange(pair_count * block_len, dtype=jnp.int32)
    relative = places[:, None] - row_offsets[None, :]
    inside = (relative >= 0) & (relative < row_lengths[None, :])
    take_index = jnp.sum(jnp.where(inside, sources[None, :] + relative, 0), axis=1)
    segment = jnp.sum(
        jnp.where(inside, jnp.arange(2 * pair_count, dtype=jnp.int32)[None, :], 0), axis=1
    )
    position = jnp.sum(jnp.where(inside, relative, 0), axis=1)
    return (jnp.take(received, take_index, axis=0), segment, position)


def attend(packed, segment, position):
    query = packed[:, : QH * HD].reshape(-1, QH, HD)
    key_part = packed[:, QH * HD : QH * HD + HD]
    value_part = packed[:, QH * HD + HD :]
    scores = jnp.einsum(
        "qhd,kd->hqk", query, key_part, preferred_element_type=jnp.float32
    ) * HD ** (-0.5)
    allowed = (segment[:, None] == segment[None, :]) & (position[None, :] <= position[:, None])
    scores = jnp.where(allowed[None], scores, -1e30)
    row_max = jnp.max(scores, axis=2, keepdims=True)
    weights = jnp.exp(scores - row_max)
    row_total = jnp.sum(weights, axis=2, keepdims=True)
    probability = (weights / row_total).astype(jnp.bfloat16)
    mixed = jnp.einsum("hqk,kd->qhd", probability, value_part, preferred_element_type=jnp.float32)
    return mixed.reshape(-1, QH * HD).astype(jnp.bfloat16)


def shards(hidden, lengths, learner, slot_offset, norm_gain, query_weight, keyval_weight):
    tables = lax.all_gather(jnp.stack([lengths, learner, slot_offset]), "dp", axis=1, tiled=True)
    positions = source_positions(lengths, hidden.shape[0])
    packed = project(hidden, positions, norm_gain, query_weight, keyval_weight)
    packed, segment, position = route(packed, tables)
    return attend(packed, segment, position)


def solution(mesh):
    placed = (
        P(("dp", "fsdp"), None),
        P(("dp", "fsdp")),
        P(("dp", "fsdp")),
        P(("dp", "fsdp")),
        P("fsdp"),
        P("fsdp", None),
        P("fsdp", None),
    )
    return jax.shard_map(
        shards, mesh=mesh, in_specs=placed, out_specs=P(("dp", "fsdp"), None), check_vma=False
    )
```

profile of v0, /device:TPU:2, one launch (start us, length us, event | category | flops | bytes accessed | tf_op | source)
XLA Modules:
  0.0 184.4 jit_solution(14966020693214738967)
XLA Ops:
  6.5 0.7 all-gather.7.cloned.1.call-update
  7.3 0.7 all-gather.5.cloned.1.call-update
  8.0 0.7 reshape.319
  8.7 23.2 %all-gather.1 = bf16[16,1,512]{2,1,0:T(2,128)(2,1)S(1)} all-gather(bf16[1,1,512]{2,1,0:T(2,128)(2,1)S(1)} %reshape.319), channel_id=1, replica_groups=mesh['dp'=32,'fsdp'=16] {'fsdp'}, dimensions={0}, use_global_device_ids=true | all-gather | bytes 17408 | tf_op jit(solution)/shard_map/all_gather | solution.py:31
  31.9 0.8 reduce-window.9
  32.8 0.7 bitcast_subtract_fusion
  33.4 0.7 select_reduce_fusion.2
  34.2 0.7 add_bitcast_fusion
  35.0 49.0 %all-gather = s32[32,4,3]{2,1,0:T(4,128)S(1)} all-gather(s32[1,4,3]{2,1,0:T(4,128)S(1)} %bitcast.70), channel_id=1, replica_groups=mesh['dp'=32,'fsdp'=16] {'dp'}, dimensions={0}, use_global_device_ids=true | all-gather | bytes 1584 | tf_op jit(solution)/shard_map/all_gather | solution.py:104
  84.3 2.0 %sort.17 = (s32[64]{0:T(128)}, s32[64]{0:T(128)S(1)}) sort(s32[64]{0:T(128)S(1)} %slice_reduce_fusion, s32[64]{0:T(128)S(1)} %iota.26), dimensions={0}, to_apply=%region_0.0 | sort | flops 384 | bytes 1024 | tf_op jit(solution)/shard_map/jit(argsort)/sort | solution.py:63
  86.9 0.6 gather_fusion.2
  88.2 3.2 %fusion.1 = f32[256]{0:T(256)S(1)} fusion(bf16[256,8192]{1,0:T(8,128)(2,1)} %param.9), kind=kLoop, calls=%fused_computation.7 | loop fusion | flops 6291200 | bytes 4195328 | tf_op jit(solution)/shard_map/reduce_sum | solution.py:29
  92.0 5.7 %fusion.8 = f32[256,256]{0,1:T(8,128)S(1)} fusion(bf16[8192,256]{1,0:T(8,128)(2,1)} %all-gather.7.cloned.1.call-done, bf16[256,8192]{1,0:T(8,128)(2,1)} %param.9, f32[8192]{0:T(1024)S(1)} %bitcast.68, f32[256]{0:T(256)S(1)} %add_rsqrt_fusion), kind=kOutput, calls=%fused_computation.16 | convolution fusion | flops 1082130432 | bytes 8684544 | tf_op jit(solution)/shard_map/dot_general | solution.py:38
  98.4 21.0 %all-gather.5.cloned.1.call-done = bf16[8192,512]{1,0:T(8,128)(2,1)} async-done(((bf16[512,512]{1,0:T(8,128)(2,1)}), bf16[8192,512]{1,0:T(8,128)(2,1)}) %all-gather.5.cloned.1.call-update) | async-done | bytes 8388624 | tf_op jit(solution)/shard_map/all_gather | solution.py:32
  119.4 7.0 %fusion.10 = f32[256,512]{1,0:T(8,128)S(1)} fusion(bf16[8192,512]{1,0:T(8,128)(2,1)} %all-gather.5.cloned.1.call-done, bf16[256,8192]{1,0:T(8,128)(2,1)} %param.9, f32[8192]{0:T(1024)S(1)} %bitcast.69, f32[256]{0:T(256)S(1)} %add_rsqrt_fusion), kind=kOutput, calls=%fused_computation.17 | convolution fusion | flops 2155872256 | bytes 13140992 | tf_op jit(solution)/shard_map/dot_general | solution.py:37
  127.8 0.9 copy.55
  128.7 9.9 %all-to-all-start = ((bf16[2,32,4,768]{3,2,0,1:T(4,128)(2,1)}), bf16[2,32,4,768]{3,2,0,1:T(4,128)(2,1)S(1)}, u32[]{:S(2)}, u32[]{:S(2)}) async-start(bf16[2,32,4,768]{3,2,0,1:T(4,128)(2,1)} %copy.55), calls=%async_computation | async-start | bytes 786432 | tf_op jit(solution)/shard_map/all_to_all | solution.py:59
  138.9 14.2 %all-to-all-done = bf16[2,32,4,768]{3,2,0,1:T(4,128)(2,1)S(1)} async-done(((bf16[2,32,4,768]{3,2,0,1:T(4,128)(2,1)}), bf16[2,32,4,768]{3,2,0,1:T(4,128)(2,1)S(1)}, u32[]{:S(2)}, u32[]{:S(2)}) %all-to-all-start) | async-done | bytes 393248 | tf_op jit(solution)/shard_map/all_to_all | solution.py:59
  153.0 0.9 gather_fusion
  153.9 1.0 select_bitcast_fusion
  155.0 5.6 %all-to-all-start.1 = ((bf16[32,2,1,4,768]{4,3,1,2,0:T(4,128)(2,1)}), bf16[32,2,1,4,768]{4,3,1,2,0:T(4,128)(2,1)S(1)}, u32[]{:S(2)}, u32[]{:S(2)}) async-start(bf16[32,2,1,4,768]{4,3,1,2,0:T(4,128)(2,1)} %select_bitcast_fusion), calls=%async_computation.1 | async-start | bytes 786432 | tf_op jit(solution)/shard_map/all_to_all | solution.py:67
  160.7 13.1 %all-to-all-done.1 = bf16[32,2,1,4,768]{4,3,1,2,0:T(4,128)(2,1)S(1)} async-done(((bf16[32,2,1,4,768]{4,3,1,2,0:T(4,128)(2,1)}), bf16[32,2,1,4,768]{4,3,1,2,0:T(4,128)(2,1)S(1)}, u32[]{:S(2)}, u32[]{:S(2)}) %all-to-all-start.1) | async-done | bytes 393248 | tf_op jit(solution)/shard_map/all_to_all | solution.py:67
  174.1 1.2 gather_fusion.1
  176.7 0.8 copy.62
  (53 shorter events, 6.4 us)
Async XLA Ops:
  6.5 85.5 %all-gather.7.cloned.1.call-start = ((), (), s32[]{:S(2)}) async-start(), calls=%async_computation.3 | async-start | bytes 4456448 | tf_op jit(solution)/shard_map/all_gather | solution.py:33
  7.3 112.1 %all-gather.5.cloned.1.call-start = ((), (), s32[]{:S(2)}) async-start(), calls=%async_computation.2 | async-start | bytes 8912896 | tf_op jit(solution)/shard_map/all_gather | solution.py:32
  128.7 24.3 %all-to-all-start = ((bf16[2,32,4,768]{3,2,0,1:T(4,128)(2,1)}), bf16[2,32,4,768]{3,2,0,1:T(4,128)(2,1)S(1)}, u32[]{:S(2)}, u32[]{:S(2)}) async-start(bf16[2,32,4,768]{3,2,0,1:T(4,128)(2,1)} %copy.55), calls=%async_computation | async-start | bytes 786432 | tf_op jit(solution)/shard_map/all_to_all | solution.py:59
  155.0 18.9 %all-to-all-start.1 = ((bf16[32,2,1,4,768]{4,3,1,2,0:T(4,128)(2,1)}), bf16[32,2,1,4,768]{4,3,1,2,0:T(4,128)(2,1)S(1)}, u32[]{:S(2)}, u32[]{:S(2)}) async-start(bf16[32,2,1,4,768]{4,3,1,2,0:T(4,128)(2,1)} %select_bitcast_fusion), calls=%async_computation.1 | async-start | bytes 786432 | tf_op jit(solution)/shard_map/all_to_all | solution.py:67
Sparse Core Ops, SparseCore 0:
  9.5 49.9 all-gather.6
  61.6 57.7 all-gather.4
where the time goes:
time: 185 us; the launch traced here: 184 us
  blocking collectives  72.2 us (39%)
  waiting for transfers between devices  49.7 us (27%)
  starting transfers between devices  15.5 us (8%)
  matrix products  13.9 us (8%)
  between operations  13.7 us (7%)
  other arithmetic  11.8 us (6%)
  local copies, waits for them, and re-layouts  7.6 us (4%)
    all_gather x1, blocking collectives, shards(): lax.all_gather(jnp.stack([lengths, learner, slot_offset]), 'dp', axis=1,...  49 us
    all_gather x1, blocking collectives, project(): gain_piece = lax.all_gather(norm_gain, 'fsdp', axis=0, tiled=True)  23.2 us
    all_gather x1, waiting for transfers between devices, project(): query_piece = lax.all_gather(query_weight, 'fsdp', axis=0, tiled=True)  21 us
    all_to_all x1, waiting for transfers between devices, route(): lax.all_to_all(blocks, 'dp', split_axis=1, concat_axis=0, tiled=True)  14.2 us
    all_to_all x1, waiting for transfers between devices, route(): lax.all_to_all(arranged, 'dp', split_axis=0, concat_axis=2, tiled=True)  13.1 us
    all_to_all x1, starting transfers between devices, route(): lax.all_to_all(blocks, 'dp', split_axis=1, concat_axis=0, tiled=True)  9.85 us
    dot_general x1, matrix products, project(): query = jnp.dot(normed, query_piece, preferred_element_type=jnp.float32)  7.04 us
    dot_general x1, matrix products, project(): key_value = jnp.dot(normed, kv_piece, preferred_element_type=jnp.float32)  5.72 us
  transfers between devices with their start and end apart: 4, of which 3 were waited for; matrix products, arithmetic and copies ran while one was open for 10% of the time, Pallas kernels for 0%

commit v1 on v0

v1 whole, which is shorter than its diff:
```python
import jax
import jax.numpy as jnp
from jax import lax
from jax.experimental import pallas as pl
from jax.experimental.pallas import tpu as pltpu
from jax.sharding import PartitionSpec as P

HD = 128
QH = 4
WIDE = (QH + 2) * HD
PAIR = 128

rope_base = 500000.0
norm_eps = 1e-05


def row_factors(rows, lengths):
    inverse = lax.rsqrt(
        jnp.mean(jnp.square(rows.astype(jnp.float32)), axis=1, keepdims=True) + norm_eps
    )
    lead = jnp.repeat(lengths[0::2], PAIR, total_repeat_length=rows.shape[0])
    place = jnp.arange(rows.shape[0], dtype=jnp.int32) % PAIR
    position = jnp.where(place < lead, place, place - lead)
    lane = jnp.arange(HD, dtype=jnp.int32)
    frequency = rope_base ** (-(lane % (HD // 2)).astype(jnp.float32) * 2.0 / HD)
    angles = position.astype(jnp.float32)[:, None] * frequency[None, :]
    sign = jnp.where(lane < HD // 2, -1.0, 1.0)
    return inverse, jnp.cos(angles) * inverse, jnp.sin(angles) * sign * inverse


def attend_kernel(
    lengths_ref, rows_ref, weight_ref, inverse_ref, cosine_ref, sine_ref, out_ref, total, mixed
):
    step = pl.program_id(0)
    part = jnp.dot(rows_ref[...], weight_ref[...], preferred_element_type=jnp.float32)

    @pl.when(step == 0)
    def _():
        total[...] = part

    @pl.when(step > 0)
    def _():
        total[...] += part

    @pl.when(step == pl.num_programs(0) - 1)
    def _():
        tokens = out_ref.shape[0]
        cosine, sine = cosine_ref[...], sine_ref[...]

        def rotated(head):
            values = total[:, head * HD : (head + 1) * HD]
            return (values * cosine + pltpu.roll(values, HD // 2, 1) * sine).astype(jnp.bfloat16)

        heads = [rotated(h) for h in range(QH)]
        key_part = rotated(QH)
        value_part = (total[:, (QH + 1) * HD :] * inverse_ref[...]).astype(jnp.bfloat16)
        asks = lax.broadcasted_iota(jnp.int32, (PAIR, PAIR), 0)
        keys = lax.broadcasted_iota(jnp.int32, (PAIR, PAIR), 1)
        for pair in range(tokens // PAIR):
            own = slice(pair * PAIR, (pair + 1) * PAIR)
            lead = lengths_ref[2 * pair]
            allowed = (keys <= asks) & ((asks < lead) | (keys >= lead))
            allowed = jnp.concatenate([allowed.astype(jnp.int32)] * QH, axis=0) > 0
            query = jnp.concatenate([h[own] for h in heads], axis=0)
            scores = lax.dot_general(
                query, key_part[own], (((1,), (1,)), ((), ())), preferred_element_type=jnp.float32
            ) * (HD**-0.5)
            scores = jnp.where(allowed, scores, -1e30)
            weights = jnp.exp(scores - jnp.max(scores, axis=1, keepdims=True))
            probability = (weights / jnp.sum(weights, axis=1, keepdims=True)).astype(jnp.bfloat16)
            result = jnp.dot(
                probability, value_part[own], preferred_element_type=jnp.float32
            ).astype(jnp.bfloat16)
            for h in range(QH):
                mixed[own, h * HD : (h + 1) * HD] = result[h * PAIR : (h + 1) * PAIR]
        row = lax.broadcasted_iota(jnp.int32, (tokens, tokens), 0)
        token = lax.broadcasted_iota(jnp.int32, (tokens, tokens), 1)
        source = ((row >> 2) & 1) * PAIR + (row >> 3) * 4 + (row & 3)
        order = jnp.where(token == source, 1.0, 0.0).astype(jnp.bfloat16)
        out_ref[...] = jnp.dot(order, mixed[...], preferred_element_type=jnp.float32).astype(
            out_ref.dtype
        )


def attend(rows, lengths, weight, inverse, cosine, sine):
    tokens, depth = rows.shape
    block = 1024
    return pl.pallas_call(
        attend_kernel,
        out_shape=jax.ShapeDtypeStruct((tokens, QH * HD), jnp.bfloat16),
        grid=(depth // block,),
        in_specs=[
            pl.BlockSpec(memory_space=pltpu.SMEM),
            pl.BlockSpec((tokens, block), lambda k: (0, k)),
            pl.BlockSpec((block, WIDE), lambda k: (k, 0)),
            pl.BlockSpec((tokens, 1), lambda k: (0, 0)),
            pl.BlockSpec((tokens, HD), lambda k: (0, 0)),
            pl.BlockSpec((tokens, HD), lambda k: (0, 0)),
        ],
        out_specs=pl.BlockSpec((tokens, QH * HD), lambda k: (0, 0)),
        scratch_shapes=[
            pltpu.VMEM((tokens, WIDE), jnp.float32),
            pltpu.VMEM((tokens, QH * HD), jnp.bfloat16),
        ],
        compiler_params=pltpu.CompilerParams(vmem_limit_bytes=24 << 20),
        cost_estimate=pl.CostEstimate(
            flops=2 * tokens * depth * WIDE, bytes_accessed=2 * depth * (tokens + WIDE), transcendentals=0
        ),
    )(lengths, rows, weight, inverse, cosine, sine)


def routes(lengths, learner, slot_offset):
    table = jnp.concatenate([lengths, learner, slot_offset]).reshape(3, -1)
    table = lax.all_gather(table, "dp", axis=0).transpose(1, 0, 2).reshape(3, -1, 2)
    lead, target, offset = table[0, :, 0], table[1, :, 0], table[2]
    pairs = target.shape[0]
    number = jnp.arange(pairs, dtype=jnp.int32)
    before = (target[None, :] < target[:, None]) | (
        (target[None, :] == target[:, None]) & (number[None, :] < number[:, None])
    )
    rank = jnp.sum(before.astype(jnp.int32), axis=1)
    rows = 4 * pairs
    row = jnp.arange(rows, dtype=jnp.int32)
    goes = jnp.repeat(rank, 4, total_repeat_length=rows) * 4 + row % 4
    first = (row[:, None] == goes[None, :]).astype(jnp.bfloat16)
    kept = (row // 4) % 2
    mine = (rank[None, :] == (2 * lax.axis_index("dp") + kept)[:, None]).astype(jnp.int32)
    own_lead = jnp.sum(mine * lead[None, :], axis=1)
    own_first = jnp.sum(mine * offset[None, :, 0], axis=1)
    own_second = jnp.sum(mine * offset[None, :, 1], axis=1)
    token = (row // 8) * 4 + row % 4
    slot = jnp.where(token < own_lead, own_first + token, own_second + token - own_lead)
    last = (row[:, None] == slot[None, :]).astype(jnp.bfloat16)
    return first, last


def exchange(rows):
    peers = lax.axis_size("dp")
    blocks = rows.reshape(peers, -1, rows.shape[1])
    return lax.all_to_all(blocks, "dp", split_axis=0, concat_axis=0, tiled=True).reshape(rows.shape)


def shards(hidden, lengths, learner, slot_offset, norm_gain, query_weight, keyval_weight):
    scaled = norm_gain.astype(jnp.float32)[:, None] * jnp.concatenate(
        [query_weight, keyval_weight], axis=1
    ).astype(jnp.float32)
    weight = lax.all_gather(scaled.astype(jnp.bfloat16), "fsdp", axis=0, tiled=True)
    first, last = routes(lengths, learner, slot_offset)
    inverse, cosine, sine = row_factors(hidden, lengths)
    mixed = attend(hidden, lengths, weight, inverse, cosine, sine)
    spread = exchange(mixed)
    arranged = jnp.dot(first, spread, preferred_element_type=jnp.float32).astype(jnp.bfloat16)
    landed = exchange(arranged)
    return jnp.dot(last, landed, preferred_element_type=jnp.float32).astype(jnp.bfloat16)


def solution(mesh):
    placed = (
        P(("dp", "fsdp"), None),
        P(("dp", "fsdp")),
        P(("dp", "fsdp")),
        P(("dp", "fsdp")),
        P("fsdp"),
        P("fsdp", None),
        P("fsdp", None),
    )
    return jax.shard_map(
        shards, mesh=mesh, in_specs=placed, out_specs=P(("dp", "fsdp"), None), check_vma=False
    )
```

time: 185 us -> 156 us (0.84)
  the two profiles are of different devices: /device:TPU:2 before, /device:TPU:8 now
where the time goes in v1:
time: 156 us
  blocking collectives  51.3 us (33%)
  waiting for transfers between devices  45 us (29%)
  starting transfers between devices  14.5 us (9%)
  between operations  13.6 us (9%)
  local copies, waits for them, and re-layouts  12.6 us (8%)
  other arithmetic  8.52 us (5%)
  Pallas kernels  8.18 us (5%)
  matrix products  1.89 us (1%)
    all_gather x1, blocking collectives, routes(): lax.all_gather(table, 'dp', axis=0).transpose(1, 0, 2).reshape(3, -1, 2)  51.3 us
    all_gather x1, waiting for transfers between devices, shards(): lax.all_gather(scaled.astype(jnp.bfloat16), 'fsdp', axis=0, tiled=True)  23.6 us
    all_to_all x2, waiting for transfers between devices, exchange(): lax.all_to_all(blocks, 'dp', split_axis=0, concat_axis=0, tiled=True)  21.5 us
    all_to_all x2, starting transfers between devices, exchange(): lax.all_to_all(blocks, 'dp', split_axis=0, concat_axis=0, tiled=True)  14.5 us
    pallas_call x1, Pallas kernels, attend(): pl.pallas_call(attend_kernel, out_shape=jax.ShapeDtypeStruct((tokens, QH...  8.18 us
    unnamed x12, local copies, waits for them, and re-layouts  6.79 us
  transfers between devices with their start and end apart: 3, of which 3 were waited for; matrix products, arithmetic and copies ran while one was open for 7% of the time, Pallas kernels for 0%

profile of v1, /device:TPU:8, one launch (start us, length us, event | category | flops | bytes accessed | tf_op | source)
XLA Modules:
  0.0 155.6 jit_solution(3435094475886314651)
XLA Ops:
  6.5 0.7 convert_element_type.39
  7.2 2.2 %multiply_convert_fusion = bf16[512,768]{1,0:T(8,128)(2,1)} fusion(bf16[512,256]{1,0:T(8,128)(2,1)} %param.17, bf16[512,512]{1,0:T(8,128)(2,1)} %param.16, f32[512]{0:T(512)S(1)} %convert_element_type.39), kind=kLoop, calls=%fused_computation.2 | loop fusion | flops 2359296 | bytes 1574912 | tf_op jit(solution)/shard_map/convert_element_type | solution.py:147
  9.5 3.1 %multiply_reduce_fusion = f32[256]{0:T(256)S(1)} fusion(bf16[256,8192]{1,0:T(8,128)(2,1)} %rows_ref.1), kind=kLoop, calls=%fused_computation.1 | loop fusion | flops 6291200 | bytes 4195328 | tf_op jit(solution)/shard_map/reduce_sum | solution.py:19
  12.7 0.1 copy.15.inverse_ref
  13.1 51.3 %all_gather.6 = s32[32,3,4]{2,1,0:T(4,128)S(1)} all-gather(s32[1,3,4]{2,1,0:T(4,128)S(1)} %all_gather_reshape.3), channel_id=1, replica_groups=mesh['dp'=32,'fsdp'=16] {'dp'}, dimensions={0}, use_global_device_ids=true | all-gather | bytes 1584 | tf_op jit(solution)/shard_map/all_gather | solution.py:114
  64.4 0.3 copy.14
  64.7 0.6 fusion.29
  65.3 2.4 %slice_reduce_fusion.2 = (s32[64]{0:T(128)S(1)}, s32[64]{0:T(128)S(1)}) fusion(s32[3,64,2]{0,2,1:T(2,128)S(1)} %bitcast.34), kind=kLoop, calls=%fused_computation.25 | loop fusion | bytes 1024 | tf_op jit(solution)/shard_map/slice | solution.py:115
  67.7 1.3 compare_select_fusion.5
  69.2 0.6 fusion.5
  69.7 23.6 %all-gather.2.cloned.1.call-done.weight_ref = bf16[8192,768]{1,0:T(8,128)(2,1)} async-done(((bf16[512,768]{1,0:T(8,128)(2,1)}), bf16[8192,768]{1,0:T(8,128)(2,1)}) %all-gather.2.cloned.1.call-update) | async-done | bytes 12582928 | tf_op jit(solution)/shard_map/all_gather | solution.py:147
  93.3 2.2 %copy-done = bf16[256,8192]{1,0:T(8,128)(2,1)S(1)} copy-done((bf16[256,8192]{1,0:T(8,128)(2,1)S(1)}, bf16[256,8192]{1,0:T(8,128)(2,1)}, u32[]{:S(2)}) %copy-start) | copy-done | bytes 4194328
  95.5 4.6 %copy-done.1 = bf16[8192,768]{1,0:T(8,128)(2,1)S(1)} copy-done((bf16[8192,768]{1,0:T(8,128)(2,1)S(1)}, bf16[8192,768]{1,0:T(8,128)(2,1)}, u32[]{:S(2)}) %copy-start.1) | copy-done | bytes 12582936
  100.1 8.2 %shard_map.73 = bf16[256,512]{1,0:T(8,128)(2,1)} custom-call(s32[4]{0:T(128)S(1)} %copy-done.2, bf16[256,8192]{1,0:T(8,128)(2,1)S(1)} %copy-done, bf16[8192,768]{1,0:T(8,128)(2,1)S(1)} %copy-done.1, f32[256,1]{1,0:T(8,128)S(1)} %copy.15.inverse_ref, f32[256,128]{1,0:T(8,128)S(1)} %get-tuple-element.37.cosine_ref, f32[256,128]{1,0:T(8,128)S(1)} %get-tuple-element.36.sine_ref), custom_call_target="tpu_custom_call" | custom-call | flops 3221225472 | bytes 16777216 | tf_op jit(solution)/shard_map/pallas_call | solution.py:88
  108.2 9.8 %all-to-all-start = ((bf16[32,8,512]{2,1,0:T(8,128)(2,1)}), bf16[32,8,512]{2,1,0:T(8,128)(2,1)S(1)}, u32[]{:S(2)}, u32[]{:S(2)}) async-start(bf16[32,8,512]{2,1,0:T(8,128)(2,1)} %bitcast.15), calls=%async_computation | async-start | bytes 524288 | tf_op jit(solution)/shard_map/all_to_all | solution.py:140
  118.1 0.2 convert_reduce_fusion
  118.3 1.9 %gather_fusion = s32[256]{0:T(256)S(1)} fusion(s32[64]{0:T(128)S(1)} %convert_reduce_fusion, s32[1024]{0:T(1024)S(1)} %pad_clamp_fusion), kind=kCustom, calls=%fused_computation | custom fusion | bytes 3072 | tf_op jit(solution)/shard_map/jit(_take)/gather | solution.py:124
  120.3 10.4 %all-to-all-done = bf16[32,8,512]{2,1,0:T(8,128)(2,1)S(1)} async-done(((bf16[32,8,512]{2,1,0:T(8,128)(2,1)}), bf16[32,8,512]{2,1,0:T(8,128)(2,1)S(1)}, u32[]{:S(2)}, u32[]{:S(2)}) %all-to-all-start) | async-done | bytes 262176 | tf_op jit(solution)/shard_map/all_to_all | solution.py:140
  130.7 0.9 fusion
  131.6 4.6 %all-to-all-start.1 = ((bf16[32,8,512]{2,1,0:T(8,128)(2,1)}), bf16[32,8,512]{2,1,0:T(8,128)(2,1)S(1)}, u32[]{:S(2)}, u32[]{:S(2)}) async-start(bf16[32,8,512]{2,1,0:T(8,128)(2,1)} %fusion), calls=%async_computation.1 | async-start | bytes 524288 | tf_op jit(solution)/shard_map/all_to_all | solution.py:140
  136.3 0.2 slice_reduce_fusion.1
  136.5 0.1 fusion.9
  136.7 11.1 %all-to-all-done.1 = bf16[32,8,512]{2,1,0:T(8,128)(2,1)S(1)} async-done(((bf16[32,8,512]{2,1,0:T(8,128)(2,1)}), bf16[32,8,512]{2,1,0:T(8,128)(2,1)S(1)}, u32[]{:S(2)}, u32[]{:S(2)}) %all-to-all-start.1) | async-done | bytes 262176 | tf_op jit(solution)/shard_map/all_to_all | solution.py:140
  147.8 0.9 convolution_convert_fusion
  (29 shorter events, 0.6 us)
Async XLA Ops:
  6.5 86.8 %all-gather.2.cloned.1.call-start = ((), (), s32[]{:S(2)}) async-start(), calls=%async_computation.2 | async-start | bytes 13369344 | tf_op jit(solution)/shard_map/all_gather | solution.py:147
  9.5 3.3 %copy-start.2 = (s32[4]{0:T(128)S(1)}, s32[4]{0:T(128)}, u32[]{:S(2)}) copy-start(s32[4]{0:T(128)} %lengths_ref.1) | copy-start | bytes 52
  9.5 3.4 %copy-start.4 = (s32[4]{0:T(128)S(1)}, s32[4]{0:T(128)}, u32[]{:S(2)}) copy-start(s32[4]{0:T(128)} %param.14) | copy-start | bytes 52
  9.5 3.4 %copy-start.5 = (s32[4]{0:T(128)S(1)}, s32[4]{0:T(128)}, u32[]{:S(2)}) copy-start(s32[4]{0:T(128)} %param.13) | copy-start | bytes 52
  9.5 59.6 %copy-start.3 = (s32[2,128]{1,0:T(2,128)S(1)}, s32[2,128]{1,0:T(2,128)}, u32[]{:S(2)}) copy-start(s32[2,128]{1,0:T(2,128)} %constant.247.clone.1) | copy-start | bytes 3076
  93.3 2.2 %copy-start = (bf16[256,8192]{1,0:T(8,128)(2,1)S(1)}, bf16[256,8192]{1,0:T(8,128)(2,1)}, u32[]{:S(2)}) copy-start(bf16[256,8192]{1,0:T(8,128)(2,1)} %rows_ref.1) | copy-start | bytes 12582916
  95.5 4.6 %copy-start.1 = (bf16[8192,768]{1,0:T(8,128)(2,1)S(1)}, bf16[8192,768]{1,0:T(8,128)(2,1)}, u32[]{:S(2)}) copy-start(bf16[8192,768]{1,0:T(8,128)(2,1)} %all-gather.2.cloned.1.call-done.weight_ref) | copy-start | bytes 37748740
  108.2 22.4 %all-to-all-start = ((bf16[32,8,512]{2,1,0:T(8,128)(2,1)}), bf16[32,8,512]{2,1,0:T(8,128)(2,1)S(1)}, u32[]{:S(2)}, u32[]{:S(2)}) async-start(bf16[32,8,512]{2,1,0:T(8,128)(2,1)} %bitcast.15), calls=%async_computation | async-start | bytes 524288 | tf_op jit(solution)/shard_map/all_to_all | solution.py:140
  131.6 16.1 %all-to-all-start.1 = ((bf16[32,8,512]{2,1,0:T(8,128)(2,1)}), bf16[32,8,512]{2,1,0:T(8,128)(2,1)S(1)}, u32[]{:S(2)}, u32[]{:S(2)}) async-start(bf16[32,8,512]{2,1,0:T(8,128)(2,1)} %fusion), calls=%async_computation.1 | async-start | bytes 524288 | tf_op jit(solution)/shard_map/all_to_all | solution.py:140
Sparse Core Ops, SparseCore 0:
  9.6 83.6 all-gather.1

commit v2 on v0

v2 whole, which is shorter than its diff:
```python
import jax
import jax.numpy as jnp
from jax import lax
from jax.experimental import pallas as pl
from jax.experimental.pallas import tpu as pltpu
from jax.sharding import PartitionSpec as P

HD = 128
QH = 4
WIDE = (QH + 2) * HD
PAIR = 128

rope_base = 500000.0
norm_eps = 1e-05

f32 = jnp.float32
bf16 = jnp.bfloat16


def whole(shape):
    return pl.BlockSpec(shape, lambda *_: (0,) * len(shape))


def fold_kernel(gain_ref, query_ref, keyval_ref, *out_refs):
    depth = query_ref.shape[0]
    row = lax.broadcasted_iota(jnp.int32, (depth, depth), 0)
    column = lax.broadcasted_iota(jnp.int32, (depth, depth), 1)
    gain = jnp.where(row == column, gain_ref[...].astype(f32), 0.0).astype(bf16)
    query = jnp.dot(gain, query_ref[...], preferred_element_type=f32).astype(bf16)
    keyval = jnp.dot(gain, keyval_ref[...], preferred_element_type=f32).astype(bf16)
    rows = out_refs[0].shape[0]
    for i, out_ref in enumerate(out_refs):
        out_ref[:, : QH * HD] = query[i * rows : (i + 1) * rows]
        out_ref[:, QH * HD :] = keyval[i * rows : (i + 1) * rows]


def fold(gain, query_weight, keyval_weight):
    depth = gain.shape[0]
    half = jax.ShapeDtypeStruct((depth // 2, WIDE), bf16)
    return pl.pallas_call(fold_kernel, out_shape=(half, half), name="fold_gain")(
        gain.reshape(1, depth), query_weight, keyval_weight
    )


def prepare_kernel(where_ref, keep_ref, give_ref, out_ref, inverse_ref, squares):
    step = pl.program_id(0)
    out_ref[...] = give_ref[...]
    both = jnp.square(keep_ref[...].astype(f32)) + jnp.square(give_ref[...].astype(f32))
    part = sum(both[:, i * 128 : (i + 1) * 128] for i in range(both.shape[1] // 128))

    @pl.when(step == 0)
    def _():
        squares[...] = part

    @pl.when(step > 0)
    def _():
        squares[...] += part

    @pl.when(step == pl.num_programs(0) - 1)
    def _():
        depth = 2 * pl.num_programs(0) * keep_ref.shape[1]
        mean = jnp.sum(squares[...], axis=1, keepdims=True) / depth
        inverse_ref[...] = jnp.broadcast_to(lax.rsqrt(mean + norm_eps), inverse_ref.shape)


def prepare(rows, where, block):
    tokens, depth = rows.shape
    steps = depth // (2 * block)
    return pl.pallas_call(
        prepare_kernel,
        out_shape=(
            jax.ShapeDtypeStruct((tokens, depth // 2), bf16),
            jax.ShapeDtypeStruct((tokens, HD), f32),
        ),
        grid_spec=pltpu.PrefetchScalarGridSpec(
            num_scalar_prefetch=1,
            grid=(steps,),
            in_specs=[
                pl.BlockSpec((tokens, block), lambda i, where: (0, 2 * i + where[1])),
                pl.BlockSpec((tokens, block), lambda i, where: (0, 2 * i + 1 - where[1])),
            ],
            out_specs=[
                pl.BlockSpec((tokens, block), lambda i, where: (0, i)),
                pl.BlockSpec((tokens, HD), lambda i, where: (0, 0)),
            ],
            scratch_shapes=[pltpu.VMEM((tokens, 128), f32)],
        ),
        cost_estimate=pl.CostEstimate(
            flops=3 * tokens * depth, bytes_accessed=3 * tokens * depth, transcendentals=0
        ),
        name="prepare",
    )(where, rows, rows)


def partial_kernel(count, carried, place_ref, *refs):
    weights, columns = refs[:count], refs[count : 2 * count]
    out_ref = refs[-1]
    total = jnp.dot(columns[0][...], weights[0][...], preferred_element_type=f32)
    for c, w in zip(columns[1:], weights[1:]):
        total += jnp.dot(c[...], w[...], preferred_element_type=f32)
    out_ref[...] = refs[2 * count][...] + total if carried else total


def partial(rows, where, blocks, before, ring, shared):
    count, tokens = len(blocks), rows.shape[0]
    weights = [w for _, _, w in blocks]
    depth = weights[0].shape[0]
    carried = before is not None

    def columns(distance, half):
        def index(_, where):
            place = lax.rem(where[0] + (distance + ring), ring)
            return 0, (4 * place + 2 * where[1] + half if shared else 2 * place + half)

        return pl.BlockSpec((tokens, depth), index)

    total = whole((tokens, WIDE))
    return pl.pallas_call(
        lambda *refs: partial_kernel(count, carried, *refs),
        out_shape=jax.ShapeDtypeStruct((tokens, WIDE), f32),
        grid_spec=pltpu.PrefetchScalarGridSpec(
            num_scalar_prefetch=1,
            grid=(1,),
            in_specs=[whole((depth, WIDE))] * count
            + [columns(d, h) for d, h, _ in blocks]
            + [total] * carried,
            out_specs=total,
        ),
        compiler_params=pltpu.CompilerParams(vmem_limit_bytes=24 << 20),
        cost_estimate=pl.CostEstimate(
            flops=2 * tokens * depth * WIDE * count,
            bytes_accessed=2 * depth * (tokens + WIDE) * count + 4 * tokens * WIDE * (1 + carried),
            transcendentals=0,
        ),
        name="partial_sums",
    )(where, *weights, *[rows] * count, *([before] if carried else []))


def attend_kernel(lengths_ref, mine_ref, other_ref, inverse_ref, cosine_ref, sine_ref, out_ref, mixed):
    tokens = out_ref.shape[0]
    inverse = inverse_ref[...]
    cosine, sine = cosine_ref[...] * inverse, sine_ref[...] * inverse

    def product(head):
        own = slice(head * HD, (head + 1) * HD)
        return mine_ref[:, own] + other_ref[:, own]

    def rotated(head):
        values = product(head)
        return (values * cosine + pltpu.roll(values, HD // 2, 1) * sine).astype(bf16)

    heads = [rotated(h) for h in range(QH)]
    key_part = rotated(QH)
    value_part = (product(QH + 1) * inverse).astype(bf16)
    asks = lax.broadcasted_iota(jnp.int32, (PAIR, PAIR), 0)
    keys = lax.broadcasted_iota(jnp.int32, (PAIR, PAIR), 1)
    for pair in range(tokens // PAIR):
        own = slice(pair * PAIR, (pair + 1) * PAIR)
        lead = lengths_ref[2 * pair]
        allowed = (keys <= asks) & ((asks < lead) | (keys >= lead))
        allowed = jnp.concatenate([allowed.astype(jnp.int32)] * QH, axis=0) > 0
        query = jnp.concatenate([h[own] for h in heads], axis=0)
        scores = lax.dot_general(
            query, key_part[own], (((1,), (1,)), ((), ())), preferred_element_type=f32
        ) * (HD**-0.5)
        scores = jnp.where(allowed, scores, -1e30)
        weights = jnp.exp(scores - jnp.max(scores, axis=1, keepdims=True))
        probability = (weights / jnp.sum(weights, axis=1, keepdims=True)).astype(bf16)
        result = jnp.dot(probability, value_part[own], preferred_element_type=f32).astype(bf16)
        for h in range(QH):
            mixed[own, h * HD : (h + 1) * HD] = result[h * PAIR : (h + 1) * PAIR]
    row = lax.broadcasted_iota(jnp.int32, (tokens, tokens), 0)
    token = lax.broadcasted_iota(jnp.int32, (tokens, tokens), 1)
    source = ((row >> 2) & 1) * PAIR + (row >> 3) * 4 + (row & 3)
    order = jnp.where(token == source, 1.0, 0.0).astype(bf16)
    out_ref[...] = jnp.dot(order, mixed[...], preferred_element_type=f32).astype(out_ref.dtype)


def attend(lengths, mine, other, inverse, cosine, sine):
    tokens = mine.shape[0]
    vmem = pl.BlockSpec(memory_space=pltpu.VMEM)
    return pl.pallas_call(
        attend_kernel,
        out_shape=jax.ShapeDtypeStruct((tokens, QH * HD), bf16),
        in_specs=[pl.BlockSpec(memory_space=pltpu.SMEM)] + [vmem] * 5,
        out_specs=vmem,
        scratch_shapes=[pltpu.VMEM((tokens, QH * HD), bf16)],
        name="attend",
    )(lengths, mine, other, inverse, cosine, sine)


def rotary(lengths, tokens):
    slot = jnp.arange(tokens, dtype=jnp.int32)
    place = slot % PAIR
    lead = sum(jnp.where(slot // PAIR == k, lengths[2 * k], 0) for k in range(tokens // PAIR))
    position = jnp.where(place < lead, place, place - lead)
    lane = jnp.arange(HD, dtype=jnp.int32)
    frequency = rope_base ** (-(lane % (HD // 2)).astype(f32) * 2.0 / HD)
    angles = position.astype(f32)[:, None] * frequency[None, :]
    sign = jnp.where(lane < HD // 2, -1.0, 1.0)
    return jnp.cos(angles), jnp.sin(angles) * sign


def orders_kernel(me_ref, table_ref, first_ref, last_ref):
    rows = first_ref.shape[0]
    peers = table_ref.shape[0]
    down = lax.broadcasted_iota(jnp.int32, (rows, rows), 0)
    along = lax.broadcasted_iota(jnp.int32, (rows, rows), 1)
    table = table_ref[:, 0, :].astype(f32).astype(bf16)
    spread = jnp.where(
        lax.broadcasted_iota(jnp.int32, (rows, peers), 1)
        == lax.broadcasted_iota(jnp.int32, (rows, peers), 0) // 8,
        1.0,
        0.0,
    ).astype(bf16)
    table = jnp.dot(spread, table, preferred_element_type=f32)
    place = lax.broadcasted_iota(jnp.int32, (rows, 1), 0)
    second = (place // 4) % 2 == 1

    def pick(even, odd):
        return jnp.where(second, table[:, odd : odd + 1], table[:, even : even + 1])

    lead, target = pick(0, 2), pick(4, 6)
    offset_a, offset_b = pick(8, 10), pick(9, 11)
    key = target * rows + (place // 4).astype(f32)
    key_along = jnp.sum(jnp.where(down == along, key, 0.0), axis=0, keepdims=True)
    ahead_along = jnp.sum(jnp.where(key < key_along, 1.0, 0.0), axis=0, keepdims=True)
    ahead = jnp.sum(jnp.where(key_along < key, 1.0, 0.0), axis=1, keepdims=True)
    row = lax.broadcasted_iota(jnp.int32, (1, rows), 1)
    goes = ahead_along.astype(jnp.int32) + row % 4
    first_ref[...] = jnp.where(down == goes, 1.0, 0.0).astype(bf16)
    token = (row // 8) * 4 + row % 4

    def slots(k):
        mine = (ahead.astype(jnp.int32) == 4 * (2 * me_ref[0] + k)) & (place % 4 == 0)

        def own(values):
            return jnp.sum(jnp.where(mine, values, 0.0), axis=0, keepdims=True).astype(jnp.int32)

        return jnp.where(
            token < own(lead), own(offset_a) + token, own(offset_b) + token - own(lead)
        )

    slot = jnp.where((row // 4) % 2 == 0, slots(0), slots(1))
    last_ref[...] = jnp.where(down == slot, 1.0, 0.0).astype(bf16)


def orders(table, rows):
    order = jax.ShapeDtypeStruct((rows, rows), bf16)
    vmem = pl.BlockSpec(memory_space=pltpu.VMEM)
    return pl.pallas_call(
        orders_kernel,
        out_shape=(order, order),
        in_specs=[pl.BlockSpec(memory_space=pltpu.SMEM), vmem],
        out_specs=(vmem, vmem),
        name="row_orders",
    )(lax.axis_index("dp").reshape(1), table)


def to_peers(blocks):
    return lax.all_to_all(blocks, "dp", split_axis=0, concat_axis=0, tiled=True)


def exchange(rows):
    return to_peers(rows.reshape(lax.axis_size("dp"), -1, rows.shape[1])).reshape(rows.shape)


def shards(hidden, lengths, learner, slot_offset, norm_gain, query_weight, keyval_weight):
    tokens = hidden.shape[0]
    block = norm_gain.shape[0]
    size = lax.axis_size("fsdp")
    ring = size // 2
    index = lax.axis_index("fsdp")
    where = jnp.stack([index // 2, index % 2])
    up = [(i, (i + 2) % size) for i in range(size)]
    down = [(i, (i - 2) % size) for i in range(size)]
    swap = [(i, i ^ 1) for i in range(size)]

    def send(values, pairs):
        return lax.ppermute(values, "fsdp", pairs)

    def after(value, *others):
        return lax.optimization_barrier((value, *others))[0]

    held = fold(norm_gain, query_weight, keyval_weight)
    give, inverse = prepare(hidden, after(where, held[0]), block)
    got = send(give, swap)

    def add(blocks, before, side):
        return partial((hidden, got)[side], where, blocks, before, ring, side == 0)

    above, below = list(held), list(held)
    sums = [None, None]
    blocks = [(0, h, held[h]) for h in (0, 1)]
    for step in range(1, ring // 2):
        above = [send(w, up) for w in above]
        below = [send(w, down) for w in below]
        sums = [add(blocks, before, side) for side, before in enumerate(sums)]
        wanted = list(sums)
        if step == 1:
            table = jnp.pad(jnp.concatenate([lengths, learner, slot_offset]), (0, 116))
            table = jnp.broadcast_to(after(table, above[0]), (lax.axis_size("dp"), 8, 128))
            first, last = orders(to_peers(table), tokens)
            cosine, sine = rotary(after(lengths, above[0]), tokens)
        if step == 2:
            wanted += [first, last, cosine, sine]
        above[0] = after(above[0], *wanted)
        blocks = [(-step, h, above[h]) for h in (0, 1)] + [(step, h, below[h]) for h in (0, 1)]
    far = [(ring // 2, 0, send(above[0], up)), (ring // 2, 1, send(below[1], down))]
    sums = [add(blocks, before, side) for side, before in enumerate(sums)]
    far[1] = (*far[1][:2], after(far[1][2], *sums))
    other = send(add(far, sums[1], 1), swap)
    mine = add(far, sums[0], 0)
    mixed = attend(lengths, mine, other, inverse, cosine, sine)
    spread = exchange(mixed)
    arranged = jnp.dot(first, spread, preferred_element_type=f32).astype(bf16)
    landed = exchange(arranged)
    return jnp.dot(last, landed, preferred_element_type=f32).astype(bf16)


def solution(mesh):
    placed = (
        P(("dp", "fsdp"), None),
        P(("dp", "fsdp")),
        P(("dp", "fsdp")),
        P(("dp", "fsdp")),
        P("fsdp"),
        P("fsdp", None),
        P("fsdp", None),
    )
    return jax.shard_map(
        shards, mesh=mesh, in_specs=placed, out_specs=P(("dp", "fsdp"), None), check_vma=False
    )
```

time: 185 us -> 162 us (0.88)
  the two profiles are of different devices: /device:TPU:2 before, /device:TPU:8 now
where the time goes in v2:
time: 162 us; the launch traced here: 161 us
  starting transfers between devices  68 us (42%)
  blocking collectives  38.2 us (24%)
  Pallas kernels  33.6 us (21%)
  local copies, waits for them, and re-layouts  9.2 us (6%)
  waiting for transfers between devices  7.13 us (4%)
  other arithmetic  3.22 us (2%)
    ppermute x16, starting transfers between devices, send(): return lax.ppermute(values, 'fsdp', pairs)  57.8 us
    all_to_all x2, blocking collectives, to_peers(): return lax.all_to_all(blocks, 'dp', split_axis=0, concat_axis=0, tiled=True)  38.2 us
    pallas_call x10, Pallas kernels, partial(): pl.pallas_call(lambda *refs: partial_kernel(count, carried, *refs), out_s...  17.8 us
    all_to_all x1, starting transfers between devices, to_peers(): return lax.all_to_all(blocks, 'dp', split_axis=0, concat_axis=0, tiled=True)  10.2 us
    pallas_call x1, Pallas kernels, prepare(): pl.pallas_call(prepare_kernel, out_shape=(jax.ShapeDtypeStruct((tokens, d...  7.67 us
    ppermute x16, waiting for transfers between devices, send(): return lax.ppermute(values, 'fsdp', pairs)  7.13 us
    unnamed x28, local copies, waits for them, and re-layouts  6.66 us
    pallas_call x1, Pallas kernels, attend(): pl.pallas_call(attend_kernel, out_shape=jax.ShapeDtypeStruct((tokens, QH...  3.37 us
  transfers between devices with their start and end apart: 17, of which 2 were waited for; matrix products, arithmetic and copies ran while one was open for 2% of the time, Pallas kernels for 12%

profile of v2, /device:TPU:8, one launch (start us, length us, event | category | flops | bytes accessed | tf_op | source)
XLA Modules:
  0.0 160.8 jit_solution(8713911451238710749)
XLA Ops:
  1.9 2.5 %fold_gain.1 = (bf16[256,768]{1,0:T(8,128)(2,1)}, bf16[256,768]{1,0:T(8,128)(2,1)}) custom-call(bf16[1,512]{1,0:T(2,128)(2,1)} %reshape.66.gain_ref, bf16[512,512]{1,0:T(8,128)(2,1)} %query_ref.1, bf16[512,256]{1,0:T(8,128)(2,1)} %keyval_ref.1), custom_call_target="tpu_custom_call" | custom-call | tf_op jit(solution)/shard_map/fold_gain/pallas_call | solution.py:40
  4.4 7.7 %prepare.1 = (bf16[256,4096]{1,0:T(8,128)(2,1)}, f32[256,128]{1,0:T(8,128)}) custom-call(s32[2]{0:T(128)} %pad_add_fusion.1.refs_0_.where_ref, bf16[256,8192]{1,0:T(8,128)(2,1)} %refs_4_.3, bf16[256,8192]{1,0:T(8,128)(2,1)} %refs_4_.3), custom_call_target="tpu_custom_call" | custom-call | flops 6291456 | bytes 6291456 | tf_op jit(solution)/shard_map/prepare/pallas_call | solution.py:69
  14.0 4.3 %collective-permute-start = (bf16[256,768]{1,0:T(8,128)(2,1)}, bf16[256,768]{1,0:T(8,128)(2,1)}, u32[]{:S(2)}, u32[]{:S(2)}) collective-permute-start(bf16[256,768]{1,0:T(8,128)(2,1)} %get-tuple-element.18.refs_1_), channel_id=1, source_target_pairs={{0,2},{1,3},{2,4},{3,5},{4,6},{5,7},{6,8},{7,9},{8,10},{9,11},{10,... | collective-permute-start | bytes 1179656 | tf_op jit(solution)/shard_map/ppermute | solution.py:280
  18.3 8.6 %collective-permute-start.5 = (bf16[256,768]{1,0:T(8,128)(2,1)S(1)}, bf16[256,768]{1,0:T(8,128)(2,1)}, u32[]{:S(2)}, u32[]{:S(2)}) collective-permute-start(bf16[256,768]{1,0:T(8,128)(2,1)S(1)} %copy-done.5), channel_id=1, source_target_pairs={{0,14},{1,15},{2,0},{3,1},{4,2},{5,3},{6,4},{7,5},{8,6},{9,7},{10,... | collective-permute-start | bytes 1179656 | tf_op jit(solution)/shard_map/ppermute | solution.py:280
  26.9 3.9 %collective-permute-start.4 = (bf16[256,768]{1,0:T(8,128)(2,1)}, bf16[256,768]{1,0:T(8,128)(2,1)}, u32[]{:S(2)}, u32[]{:S(2)}) collective-permute-start(bf16[256,768]{1,0:T(8,128)(2,1)} %get-tuple-element.18.refs_1_), channel_id=1, source_target_pairs={{0,14},{1,15},{2,0},{3,1},{4,2},{5,3},{6,4},{7,5},{8,6},{9,7},{10,... | collective-permute-start | bytes 1179656 | tf_op jit(solution)/shard_map/ppermute | solution.py:280
  30.8 1.9 %collective-permute-start.3 = (bf16[256,768]{1,0:T(8,128)(2,1)S(1)}, bf16[256,768]{1,0:T(8,128)(2,1)}, u32[]{:S(2)}, u32[]{:S(2)}) collective-permute-start(bf16[256,768]{1,0:T(8,128)(2,1)S(1)} %copy-done.5), channel_id=1, source_target_pairs={{0,2},{1,3},{2,4},{3,5},{4,6},{5,7},{6,8},{7,9},{8,10},{9,11},{10,... | collective-permute-start | bytes 1179656 | tf_op jit(solution)/shard_map/ppermute | solution.py:280
  32.9 2.2 %copy-done = bf16[256,8192]{1,0:T(8,128)(2,1)S(1)} copy-done((bf16[256,8192]{1,0:T(8,128)(2,1)S(1)}, bf16[256,8192]{1,0:T(8,128)(2,1)}, u32[]{:S(2)}) %copy-start) | copy-done | bytes 4194328
  37.0 5.1 %collective-permute-start.9 = (bf16[256,768]{1,0:T(8,128)(2,1)}, bf16[256,768]{1,0:T(8,128)(2,1)}, u32[]{:S(2)}, u32[]{:S(2)}) collective-permute-start(bf16[256,768]{1,0:T(8,128)(2,1)} %collective-permute-done.5.refs_4_), channel_id=1, source_target_pairs={{0,14},{1,15},{2,0},{3,1},{4,2},{5,3},{6,4},{7,5},{8,6},{9,7},{10,... | collective-permute-start | bytes 1179656 | tf_op jit(solution)/shard_map/ppermute | solution.py:280
  43.4 10.2 %all-to-all-start = ((s32[32,8,128]{2,1,0:T(8,128)}), s32[32,8,128]{2,1,0:T(8,128)S(1)}, u32[]{:S(2)}, u32[]{:S(2)}) async-start(s32[32,8,128]{2,1,0:T(8,128)} %broadcast_in_dim.24), calls=%async_computation | async-start | bytes 262144 | tf_op jit(solution)/shard_map/all_to_all | solution.py:261
  59.6 5.1 %collective-permute-start.8 = (bf16[256,768]{1,0:T(8,128)(2,1)}, bf16[256,768]{1,0:T(8,128)(2,1)}, u32[]{:S(2)}, u32[]{:S(2)}) collective-permute-start(bf16[256,768]{1,0:T(8,128)(2,1)} %collective-permute-done.4.refs_3_), channel_id=1, source_target_pairs={{0,14},{1,15},{2,0},{3,1},{4,2},{5,3},{6,4},{7,5},{8,6},{9,7},{10,... | collective-permute-start | bytes 1179656 | tf_op jit(solution)/shard_map/ppermute | solution.py:280
  68.6 2.2 %row_orders.1 = (bf16[256,256]{1,0:T(8,128)(2,1)}, bf16[256,256]{1,0:T(8,128)(2,1)}) custom-call(s32[1]{0:T(128)} %bitcast.me_ref, s32[32,8,128]{2,1,0:T(8,128)} %copy-done.8), custom_call_target="tpu_custom_call" | custom-call | tf_op jit(solution)/shard_map/row_orders/pallas_call | solution.py:251
  70.8 5.1 %collective-permute-start.11 = (bf16[256,768]{1,0:T(8,128)(2,1)}, bf16[256,768]{1,0:T(8,128)(2,1)S(1)}, u32[]{:S(2)}, u32[]{:S(2)}) collective-permute-start(bf16[256,768]{1,0:T(8,128)(2,1)} %collective-permute-done.9.refs_4_), channel_id=1, source_target_pairs={{0,14},{1,15},{2,0},{3,1},{4,2},{5,3},{6,4},{7,5},{8,6},{9,7},{10,... | collective-permute-start | bytes 1179656 | tf_op jit(solution)/shard_map/ppermute | solution.py:280
  77.1 2.7 %partial_sums.13.refs_9_ = f32[256,768]{1,0:T(8,128)S(1)} custom-call(s32[2]{0:T(128)S(1)} %copy-done.6, bf16[256,768]{1,0:T(8,128)(2,1)} %collective-permute-done.refs_1_, bf16[256,768]{1,0:T(8,128)(2,1)} %collective-permute-done.3.refs_2_, bf16[256,768]{1,0:T(8,128)(2,1)} %collective-permute-done.4.refs_3_, ...), custom_call_target="tpu_custom_call" | custom-call | flops 402653184 | bytes 3670016 | tf_op jit(solution)/shard_map/partial_sums/pallas_call | solution.py:118
  79.8 2.5 %partial_sums.12.refs_9_ = f32[256,768]{1,0:T(8,128)S(1)} custom-call(s32[2]{0:T(128)S(1)} %copy-done.6, bf16[256,768]{1,0:T(8,128)(2,1)} %collective-permute-done.refs_1_, bf16[256,768]{1,0:T(8,128)(2,1)} %collective-permute-done.3.refs_2_, bf16[256,768]{1,0:T(8,128)(2,1)} %collective-permute-done.4.refs_3_, ...), custom_call_target="tpu_custom_call" | custom-call | flops 402653184 | bytes 3670016 | tf_op jit(solution)/shard_map/partial_sums/pallas_call | solution.py:118
  84.3 5.1 %collective-permute-start.14 = (bf16[256,768]{1,0:T(8,128)(2,1)}, bf16[256,768]{1,0:T(8,128)(2,1)S(1)}, u32[]{:S(2)}, u32[]{:S(2)}) collective-permute-start(bf16[256,768]{1,0:T(8,128)(2,1)} %collective-permute-done.8.refs_3_), channel_id=1, source_target_pairs={{0,14},{1,15},{2,0},{3,1},{4,2},{5,3},{6,4},{7,5},{8,6},{9,7},{10,... | collective-permute-start | bytes 1179656 | tf_op jit(solution)/shard_map/ppermute | solution.py:280
  89.4 1.9 %collective-permute-start.13 = (bf16[256,768]{1,0:T(8,128)(2,1)S(1)}, bf16[256,768]{1,0:T(8,128)(2,1)S(1)}, u32[]{:S(2)}, u32[]{:S(2)}) collective-permute-start(bf16[256,768]{1,0:T(8,128)(2,1)S(1)} %collective-permute-done.7.refs_2_), channel_id=1, source_target_pairs={{0,2},{1,3},{2,4},{3,5},{4,6},{5,7},{6,8},{7,9},{8,10},{9,11},{10,... | collective-permute-start | bytes 1179656 | tf_op jit(solution)/shard_map/ppermute | solution.py:280
  91.4 5.1 %collective-permute-start.12 = (bf16[256,768]{1,0:T(8,128)(2,1)S(1)}, bf16[256,768]{1,0:T(8,128)(2,1)S(1)}, u32[]{:S(2)}, u32[]{:S(2)}) collective-permute-start(bf16[256,768]{1,0:T(8,128)(2,1)S(1)} %collective-permute-done.11.refs_4_), channel_id=1, source_target_pairs={{0,14},{1,15},{2,0},{3,1},{4,2},{5,3},{6,4},{7,5},{8,6},{9,7},{10,... | collective-permute-start | bytes 1179656 | tf_op jit(solution)/shard_map/ppermute | solution.py:280
  96.5 2.4 %partial_sums.15.refs_9_ = f32[256,768]{1,0:T(8,128)S(1)} custom-call(s32[2]{0:T(128)S(1)} %copy-done.6, bf16[256,768]{1,0:T(8,128)(2,1)} %collective-permute-done.2.refs_1_, bf16[256,768]{1,0:T(8,128)(2,1)S(1)} %collective-permute-done.7.refs_2_, bf16[256,768]{1,0:T(8,128)(2,1)} %collective-permute-done.8.refs_3_, ...), custom_call_target="tpu_custom_call" | custom-call | flops 402653184 | bytes 3670016 | tf_op jit(solution)/shard_map/partial_sums/pallas_call | solution.py:118
  98.9 2.4 %partial_sums.14.refs_9_ = f32[256,768]{1,0:T(8,128)S(1)} custom-call(s32[2]{0:T(128)S(1)} %copy-done.6, bf16[256,768]{1,0:T(8,128)(2,1)} %collective-permute-done.2.refs_1_, bf16[256,768]{1,0:T(8,128)(2,1)S(1)} %collective-permute-done.7.refs_2_, bf16[256,768]{1,0:T(8,128)(2,1)} %collective-permute-done.8.refs_3_, ...), custom_call_target="tpu_custom_call" | custom-call | flops 402653184 | bytes 3670016 | tf_op jit(solution)/shard_map/partial_sums/pallas_call | solution.py:118
  101.3 1.9 %collective-permute-start.10 = (bf16[256,768]{1,0:T(8,128)(2,1)S(1)}, bf16[256,768]{1,0:T(8,128)(2,1)S(1)}, u32[]{:S(2)}, u32[]{:S(2)}) collective-permute-start(bf16[256,768]{1,0:T(8,128)(2,1)S(1)} %collective-permute-done.6.refs_1_), channel_id=1, source_target_pairs={{0,2},{1,3},{2,4},{3,5},{4,6},{5,7},{6,8},{7,9},{8,10},{9,11},{10,... | collective-permute-start | bytes 1179656 | tf_op jit(solution)/shard_map/ppermute | solution.py:280
  105.5 6.6 %collective-permute-done.10.refs_1_ = bf16[256,768]{1,0:T(8,128)(2,1)S(1)} collective-permute-done((bf16[256,768]{1,0:T(8,128)(2,1)S(1)}, bf16[256,768]{1,0:T(8,128)(2,1)S(1)}, u32[]{:S(2)}, u32[]{:S(2)}) %collective-permute-start.10) | collective-permute-done | bytes 393248 | tf_op jit(solution)/shard_map/ppermute | solution.py:280
  118.1 3.4 %attend.1 = bf16[256,512]{1,0:T(8,128)(2,1)} custom-call(s32[4]{0:T(128)} %lengths_ref.1, f32[256,768]{1,0:T(8,128)} %copy-done.4, f32[256,768]{1,0:T(8,128)} %copy-done.7, f32[256,128]{1,0:T(8,128)} %get-tuple-element.30.inverse_ref, f32[256,128]{1,0:T(8,128)} %get-tuple-element.32.cosine_ref, f32[256,128]{1,0:T(8,128)} %get-tuple-element.31.sine_ref), custom_call_target="tpu_custom_call" | custom-call | tf_op jit(solution)/shard_map/attend/pallas_call | solution.py:182
  121.5 22.2 %all_to_all.15 = bf16[32,8,512]{2,1,0:T(8,128)(2,1)S(1)} all-to-all(bf16[32,8,512]{2,1,0:T(8,128)(2,1)} %bitcast.16), channel_id=1, replica_groups=mesh['dp'=32,'fsdp'=16] {'dp'}, dimensions={0} | all-to-all | bytes 524288 | tf_op jit(solution)/shard_map/all_to_all | solution.py:261
  144.0 15.9 %all_to_all.16 = bf16[32,8,512]{2,1,0:T(8,128)(2,1)S(1)} all-to-all(bf16[32,8,512]{2,1,0:T(8,128)(2,1)S(1)} %fusion), channel_id=1, replica_groups=mesh['dp'=32,'fsdp'=16] {'dp'}, dimensions={0} | all-to-all | bytes 524288 | tf_op jit(solution)/shard_map/all_to_all | solution.py:261
  (65 shorter events, 29.3 us)
Async XLA Ops:
  4.4 13.9 %copy-start.5 = (bf16[256,768]{1,0:T(8,128)(2,1)S(1)}, bf16[256,768]{1,0:T(8,128)(2,1)}, u32[]{:S(2)}) copy-start(bf16[256,768]{1,0:T(8,128)(2,1)} %get-tuple-element.22.refs_2_) | copy-start | bytes 1179652
  4.4 28.4 %copy-start.11 = (s32[4]{0:T(128)S(1)}, s32[4]{0:T(128)}, u32[]{:S(2)}) copy-start(s32[4]{0:T(128)} %lengths_ref.1) | copy-start | bytes 52
  4.4 28.4 %copy-start.12 = (s32[4]{0:T(128)S(1)}, s32[4]{0:T(128)}, u32[]{:S(2)}) copy-start(s32[4]{0:T(128)} %param.10) | copy-start | bytes 52
  4.4 28.4 %copy-start.13 = (s32[4]{0:T(128)S(1)}, s32[4]{0:T(128)}, u32[]{:S(2)}) copy-start(s32[4]{0:T(128)} %param.9) | copy-start | bytes 52
  4.4 28.5 %copy-start.6 = (s32[2]{0:T(128)S(1)}, s32[2]{0:T(128)}, u32[]{:S(2)}) copy-start(s32[2]{0:T(128)} %pad_add_fusion.1.refs_0_.where_ref) | copy-start | bytes 28
  12.1 41.5 %collective-permute-start.1 = (bf16[256,4096]{1,0:T(8,128)(2,1)}, bf16[256,4096]{1,0:T(8,128)(2,1)S(1)}, u32[]{:S(2)}, u32[]{:S(2)}) collective-permute-start(bf16[256,4096]{1,0:T(8,128)(2,1)} %get-tuple-element.24), channel_id=1, source_target_pairs={{0,1},{1,0},{2,3},{3,2},{4,5},{5,4},{6,7},{7,6},{8,9},{9,8},{10,11... | collective-permute-start | bytes 6291464 | tf_op jit(solution)/shard_map/ppermute | solution.py:280
  14.0 23.0 %collective-permute-start = (bf16[256,768]{1,0:T(8,128)(2,1)}, bf16[256,768]{1,0:T(8,128)(2,1)}, u32[]{:S(2)}, u32[]{:S(2)}) collective-permute-start(bf16[256,768]{1,0:T(8,128)(2,1)} %get-tuple-element.18.refs_1_), channel_id=1, source_target_pairs={{0,2},{1,3},{2,4},{3,5},{4,6},{5,7},{6,8},{7,9},{8,10},{9,11},{10,... | collective-permute-start | bytes 1179656 | tf_op jit(solution)/shard_map/ppermute | solution.py:280
  18.3 18.7 %collective-permute-start.5 = (bf16[256,768]{1,0:T(8,128)(2,1)S(1)}, bf16[256,768]{1,0:T(8,128)(2,1)}, u32[]{:S(2)}, u32[]{:S(2)}) collective-permute-start(bf16[256,768]{1,0:T(8,128)(2,1)S(1)} %copy-done.5), channel_id=1, source_target_pairs={{0,14},{1,15},{2,0},{3,1},{4,2},{5,3},{6,4},{7,5},{8,6},{9,7},{10,... | collective-permute-start | bytes 1179656 | tf_op jit(solution)/shard_map/ppermute | solution.py:280
  26.9 32.7 %collective-permute-start.4 = (bf16[256,768]{1,0:T(8,128)(2,1)}, bf16[256,768]{1,0:T(8,128)(2,1)}, u32[]{:S(2)}, u32[]{:S(2)}) collective-permute-start(bf16[256,768]{1,0:T(8,128)(2,1)} %get-tuple-element.18.refs_1_), channel_id=1, source_target_pairs={{0,14},{1,15},{2,0},{3,1},{4,2},{5,3},{6,4},{7,5},{8,6},{9,7},{10,... | collective-permute-start | bytes 1179656 | tf_op jit(solution)/shard_map/ppermute | solution.py:280
  30.8 33.9 %collective-permute-start.3 = (bf16[256,768]{1,0:T(8,128)(2,1)S(1)}, bf16[256,768]{1,0:T(8,128)(2,1)}, u32[]{:S(2)}, u32[]{:S(2)}) collective-permute-start(bf16[256,768]{1,0:T(8,128)(2,1)S(1)} %copy-done.5), channel_id=1, source_target_pairs={{0,2},{1,3},{2,4},{3,5},{4,6},{5,7},{6,8},{7,9},{8,10},{9,11},{10,... | collective-permute-start | bytes 1179656 | tf_op jit(solution)/shard_map/ppermute | solution.py:280
  37.0 33.8 %collective-permute-start.9 = (bf16[256,768]{1,0:T(8,128)(2,1)}, bf16[256,768]{1,0:T(8,128)(2,1)}, u32[]{:S(2)}, u32[]{:S(2)}) collective-permute-start(bf16[256,768]{1,0:T(8,128)(2,1)} %collective-permute-done.5.refs_4_), channel_id=1, source_target_pairs={{0,14},{1,15},{2,0},{3,1},{4,2},{5,3},{6,4},{7,5},{8,6},{9,7},{10,... | collective-permute-start | bytes 1179656 | tf_op jit(solution)/shard_map/ppermute | solution.py:280
  43.4 24.5 %all-to-all-start = ((s32[32,8,128]{2,1,0:T(8,128)}), s32[32,8,128]{2,1,0:T(8,128)S(1)}, u32[]{:S(2)}, u32[]{:S(2)}) async-start(s32[32,8,128]{2,1,0:T(8,128)} %broadcast_in_dim.24), calls=%async_computation | async-start | bytes 262144 | tf_op jit(solution)/shard_map/all_to_all | solution.py:261
  56.4 25.9 %collective-permute-start.2 = (bf16[256,768]{1,0:T(8,128)(2,1)}, bf16[256,768]{1,0:T(8,128)(2,1)}, u32[]{:S(2)}, u32[]{:S(2)}) collective-permute-start(bf16[256,768]{1,0:T(8,128)(2,1)} %collective-permute-done.refs_1_), channel_id=1, source_target_pairs={{0,2},{1,3},{2,4},{3,5},{4,6},{5,7},{6,8},{7,9},{8,10},{9,11},{10,... | collective-permute-start | bytes 1179656 | tf_op jit(solution)/shard_map/ppermute | solution.py:280
  59.6 24.6 %collective-permute-start.8 = (bf16[256,768]{1,0:T(8,128)(2,1)}, bf16[256,768]{1,0:T(8,128)(2,1)}, u32[]{:S(2)}, u32[]{:S(2)}) collective-permute-start(bf16[256,768]{1,0:T(8,128)(2,1)} %collective-permute-done.4.refs_3_), channel_id=1, source_target_pairs={{0,14},{1,15},{2,0},{3,1},{4,2},{5,3},{6,4},{7,5},{8,6},{9,7},{10,... | collective-permute-start | bytes 1179656 | tf_op jit(solution)/shard_map/ppermute | solution.py:280
  64.8 24.6 %collective-permute-start.7 = (bf16[256,768]{1,0:T(8,128)(2,1)}, bf16[256,768]{1,0:T(8,128)(2,1)S(1)}, u32[]{:S(2)}, u32[]{:S(2)}) collective-permute-start(bf16[256,768]{1,0:T(8,128)(2,1)} %collective-permute-done.3.refs_2_), channel_id=1, source_target_pairs={{0,2},{1,3},{2,4},{3,5},{4,6},{5,7},{6,8},{7,9},{8,10},{9,11},{10,... | collective-permute-start | bytes 1179656 | tf_op jit(solution)/shard_map/ppermute | solution.py:280
  70.8 20.5 %collective-permute-start.11 = (bf16[256,768]{1,0:T(8,128)(2,1)}, bf16[256,768]{1,0:T(8,128)(2,1)S(1)}, u32[]{:S(2)}, u32[]{:S(2)}) collective-permute-start(bf16[256,768]{1,0:T(8,128)(2,1)} %collective-permute-done.9.refs_4_), channel_id=1, source_target_pairs={{0,14},{1,15},{2,0},{3,1},{4,2},{5,3},{6,4},{7,5},{8,6},{9,7},{10,... | collective-permute-start | bytes 1179656 | tf_op jit(solution)/shard_map/ppermute | solution.py:280
  82.3 18.9 %collective-permute-start.6 = (bf16[256,768]{1,0:T(8,128)(2,1)}, bf16[256,768]{1,0:T(8,128)(2,1)S(1)}, u32[]{:S(2)}, u32[]{:S(2)}) collective-permute-start(bf16[256,768]{1,0:T(8,128)(2,1)} %collective-permute-done.2.refs_1_), channel_id=1, source_target_pairs={{0,2},{1,3},{2,4},{3,5},{4,6},{5,7},{6,8},{7,9},{8,10},{9,11},{10,... | collective-permute-start | bytes 1179656 | tf_op jit(solution)/shard_map/ppermute | solution.py:280
  84.3 18.9 %collective-permute-start.14 = (bf16[256,768]{1,0:T(8,128)(2,1)}, bf16[256,768]{1,0:T(8,128)(2,1)S(1)}, u32[]{:S(2)}, u32[]{:S(2)}) collective-permute-start(bf16[256,768]{1,0:T(8,128)(2,1)} %collective-permute-done.8.refs_3_), channel_id=1, source_target_pairs={{0,14},{1,15},{2,0},{3,1},{4,2},{5,3},{6,4},{7,5},{8,6},{9,7},{10,... | collective-permute-start | bytes 1179656 | tf_op jit(solution)/shard_map/ppermute | solution.py:280
  89.4 13.8 %collective-permute-start.13 = (bf16[256,768]{1,0:T(8,128)(2,1)S(1)}, bf16[256,768]{1,0:T(8,128)(2,1)S(1)}, u32[]{:S(2)}, u32[]{:S(2)}) collective-permute-start(bf16[256,768]{1,0:T(8,128)(2,1)S(1)} %collective-permute-done.7.refs_2_), channel_id=1, source_target_pairs={{0,2},{1,3},{2,4},{3,5},{4,6},{5,7},{6,8},{7,9},{8,10},{9,11},{10,... | collective-permute-start | bytes 1179656 | tf_op jit(solution)/shard_map/ppermute | solution.py:280
  91.4 14.1 %collective-permute-start.12 = (bf16[256,768]{1,0:T(8,128)(2,1)S(1)}, bf16[256,768]{1,0:T(8,128)(2,1)S(1)}, u32[]{:S(2)}, u32[]{:S(2)}) collective-permute-start(bf16[256,768]{1,0:T(8,128)(2,1)S(1)} %collective-permute-done.11.refs_4_), channel_id=1, source_target_pairs={{0,14},{1,15},{2,0},{3,1},{4,2},{5,3},{6,4},{7,5},{8,6},{9,7},{10,... | collective-permute-start | bytes 1179656 | tf_op jit(solution)/shard_map/ppermute | solution.py:280
  101.3 10.9 %collective-permute-start.10 = (bf16[256,768]{1,0:T(8,128)(2,1)S(1)}, bf16[256,768]{1,0:T(8,128)(2,1)S(1)}, u32[]{:S(2)}, u32[]{:S(2)}) collective-permute-start(bf16[256,768]{1,0:T(8,128)(2,1)S(1)} %collective-permute-done.6.refs_1_), channel_id=1, source_target_pairs={{0,2},{1,3},{2,4},{3,5},{4,6},{5,7},{6,8},{7,9},{8,10},{9,11},{10,... | collective-permute-start | bytes 1179656 | tf_op jit(solution)/shard_map/ppermute | solution.py:280
  113.0 4.2 %collective-permute-start.15 = (f32[256,768]{1,0:T(8,128)S(1)}, f32[256,768]{1,0:T(8,128)S(1)}, u32[]{:S(2)}, u32[]{:S(2)}) collective-permute-start(f32[256,768]{1,0:T(8,128)S(1)} %partial_sums.19), channel_id=1, source_target_pairs={{0,1},{1,0},{2,3},{3,2},{4,5},{5,4},{6,7},{7,6},{8,9},{9,8},{10,11... | collective-permute-start | bytes 2359304 | tf_op jit(solution)/shard_map/ppermute | solution.py:280
  116.8 27.0 %copy-start.10 = (bf16[256,256]{1,0:T(8,128)(2,1)S(1)}, bf16[256,256]{1,0:T(8,128)(2,1)}, u32[]{:S(2)}) copy-start(bf16[256,256]{1,0:T(8,128)(2,1)} %get-tuple-element.21) | copy-start | bytes 393220
  116.8 43.1 %copy-start.9 = (bf16[256,256]{1,0:T(8,128)(2,1)S(1)}, bf16[256,256]{1,0:T(8,128)(2,1)}, u32[]{:S(2)}) copy-start(bf16[256,256]{1,0:T(8,128)(2,1)} %get-tuple-element.20) | copy-start | bytes 393220
  (7 other events, 9.4 us)

commit v3 on v2

v3 whole, which is shorter than its diff:
```python
import functools

import jax
import jax.numpy as jnp
from jax import lax
from jax.experimental import pallas as pl
from jax.experimental.pallas import tpu as pltpu
from jax.sharding import PartitionSpec as P

HD = 128
QH = 4
WIDE = (QH + 2) * HD
PAIR = 128
TABLE = 128

rope_base = 500000.0
norm_eps = 1e-05

f32 = jnp.float32
bf16 = jnp.bfloat16


VMEM = pl.BlockSpec(memory_space=pltpu.VMEM)
SMEM = pl.BlockSpec(memory_space=pltpu.SMEM)


def fold_kernel(gain_ref, query_ref, keyval_ref, *out_refs):
    rows = out_refs[0].shape[0]
    row = lax.broadcasted_iota(jnp.int32, (rows, rows), 0)
    column = lax.broadcasted_iota(jnp.int32, (rows, rows), 1)
    for i, out_ref in enumerate(out_refs):
        own = slice(i * rows, (i + 1) * rows)
        gain = gain_ref[own].astype(f32).reshape(1, rows)
        gain = jnp.where(row == column, gain, 0.0).astype(bf16)
        out_ref[:, : QH * HD] = jnp.dot(gain, query_ref[own, :], preferred_element_type=f32).astype(bf16)
        out_ref[:, QH * HD :] = jnp.dot(gain, keyval_ref[own, :], preferred_element_type=f32).astype(bf16)


def fold(gain, query_weight, keyval_weight):
    half = jax.ShapeDtypeStruct((gain.shape[0] // 2, WIDE), bf16)
    return pl.pallas_call(
        fold_kernel,
        out_shape=(half, half),
        in_specs=[VMEM] * 3,
        out_specs=(VMEM, VMEM),
        name="fold_gain",
    )(gain, query_weight, keyval_weight)


def prepare_kernel(where_ref, keep_ref, give_ref, out_ref, inverse_ref, squares):
    step = pl.program_id(0)
    out_ref[...] = give_ref[...]
    part = jnp.zeros(squares.shape, f32)
    for i in range(keep_ref.shape[1] // 128):
        for ref in (keep_ref, give_ref):
            part += jnp.square(ref[:, i * 128 : (i + 1) * 128].astype(f32))

    @pl.when(step == 0)
    def _():
        squares[...] = part

    @pl.when(step > 0)
    def _():
        squares[...] += part

    @pl.when(step == pl.num_programs(0) - 1)
    def _():
        depth = 2 * pl.num_programs(0) * keep_ref.shape[1]
        mean = jnp.sum(squares[...], axis=1, keepdims=True) / depth
        inverse_ref[...] = jnp.broadcast_to(lax.rsqrt(mean + norm_eps), inverse_ref.shape)


def prepare(rows, where, block):
    tokens, depth = rows.shape
    steps = depth // (2 * block)
    return pl.pallas_call(
        prepare_kernel,
        out_shape=(
            jax.ShapeDtypeStruct((tokens, depth // 2), bf16),
            jax.ShapeDtypeStruct((tokens, HD), f32),
        ),
        grid_spec=pltpu.PrefetchScalarGridSpec(
            num_scalar_prefetch=1,
            grid=(steps,),
            in_specs=[
                pl.BlockSpec((tokens, block), lambda i, where: (0, 2 * i + where[1])),
                pl.BlockSpec((tokens, block), lambda i, where: (0, 2 * i + 1 - where[1])),
            ],
            out_specs=[
                pl.BlockSpec((tokens, block), lambda i, where: (0, i)),
                pl.BlockSpec((tokens, HD), lambda i, where: (0, 0)),
            ],
            scratch_shapes=[pltpu.VMEM((tokens, 128), f32)],
        ),
        cost_estimate=pl.CostEstimate(
            flops=3 * tokens * depth, bytes_accessed=3 * tokens * depth, transcendentals=0
        ),
        name="prepare",
    )(where, rows, rows)


def partial_kernel(count, sides, carried, where_ref, *refs):
    weights, refs = refs[:count], refs[count:]
    columns, refs = refs[: count * sides], refs[count * sides :]
    for side in range(sides):
        total = refs[side][...] if carried else None
        for c, w in zip(columns[side * count :], weights):
            part = jnp.dot(c[...], w[...], preferred_element_type=f32)
            total = part if total is None else total + part
        refs[-sides + side][...] = total


def partial(where, blocks, rows, before):
    count, sides = len(blocks), len(rows)
    weights = [w for _, _, w in blocks]
    tokens, depth = rows[0].shape[0], weights[0].shape[0]
    ring = lax.axis_size("fsdp") // 2
    carried = before is not None

    def columns(distance, half, shared):
        def index(_, where):
            origin = lax.rem(where[0] + ring + (2 * where[1] - 1) * distance, ring)
            return 0, (4 * origin + 2 * where[1] + half if shared else 2 * origin + half)

        return pl.BlockSpec((tokens, depth), index)

    total = pl.BlockSpec((tokens, WIDE), lambda *_: (0, 0))
    shape = jax.ShapeDtypeStruct((tokens, WIDE), f32)
    return pl.pallas_call(
        functools.partial(partial_kernel, count, sides, carried),
        out_shape=[shape] * sides,
        grid_spec=pltpu.PrefetchScalarGridSpec(
            num_scalar_prefetch=1,
            grid=(1,),
            in_specs=[pl.BlockSpec((depth, WIDE), lambda *_: (0, 0))] * count
            + [columns(d, h, r.shape[1] == 4 * ring * depth) for r in rows for d, h, _ in blocks]
            + [total] * (sides * carried),
            out_specs=[total] * sides,
        ),
        compiler_params=pltpu.CompilerParams(vmem_limit_bytes=28 << 20),
        cost_estimate=pl.CostEstimate(
            flops=2 * tokens * depth * WIDE * count * sides,
            bytes_accessed=2 * depth * (sides * tokens + WIDE) * count + 8 * tokens * WIDE * sides,
            transcendentals=0,
        ),
        name="partial_sums",
    )(where, *weights, *[r for r in rows for _ in blocks], *(before or []))


def attend_kernel(
    lengths_ref, learner_ref, offset_ref, mine_ref, other_ref, inverse_ref, cosine_ref, sine_ref, out_ref, mixed
):
    tokens = out_ref.shape[0]
    inverse = inverse_ref[...]
    cosine, sine = cosine_ref[...] * inverse, sine_ref[...] * inverse

    def product(head):
        own = slice(head * HD, (head + 1) * HD)
        return mine_ref[:, own] + other_ref[:, own]

    def rotated(head):
        values = product(head)
        return (values * cosine + pltpu.roll(values, HD // 2, 1) * sine).astype(bf16)

    heads = [rotated(h) for h in range(QH)]
    key_part = rotated(QH)
    value_part = (product(QH + 1) * inverse).astype(bf16)
    asks = lax.broadcasted_iota(jnp.int32, (PAIR, PAIR), 0)
    keys = lax.broadcasted_iota(jnp.int32, (PAIR, PAIR), 1)
    for pair in range(tokens // PAIR):
        own = slice(pair * PAIR, (pair + 1) * PAIR)
        lead = lengths_ref[2 * pair]
        allowed = (keys <= asks) & ((asks < lead) | (keys >= lead))
        allowed = jnp.concatenate([allowed.astype(jnp.int32)] * QH, axis=0) > 0
        query = jnp.concatenate([h[own] for h in heads], axis=0)
        scores = lax.dot_general(
            query, key_part[own], (((1,), (1,)), ((), ())), preferred_element_type=f32
        ) * (HD**-0.5)
        scores = jnp.where(allowed, scores, -1e30)
        weights = jnp.exp(scores - jnp.max(scores, axis=1, keepdims=True))
        probability = (weights / jnp.sum(weights, axis=1, keepdims=True)).astype(bf16)
        result = jnp.dot(probability, value_part[own], preferred_element_type=f32).astype(bf16)
        for h in range(QH):
            mixed[own, h * HD : (h + 1) * HD] = result[h * PAIR : (h + 1) * PAIR]
    row = lax.broadcasted_iota(jnp.int32, (tokens, tokens), 0)
    token = lax.broadcasted_iota(jnp.int32, (tokens, tokens), 1)
    source = ((row >> 2) & 1) * PAIR + (row >> 3) * 4 + (row & 3)
    order = jnp.where(token == source, 1.0, 0.0).astype(bf16)
    out_ref[:, : QH * HD] = jnp.dot(order, mixed[...], preferred_element_type=f32).astype(bf16)
    lane = lax.broadcasted_iota(jnp.int32, (tokens, TABLE), 1)
    table = jnp.zeros((tokens, TABLE), jnp.int32)
    for i, ref in enumerate((lengths_ref, learner_ref, offset_ref)):
        for j in range(4):
            table = jnp.where(lane == 4 * i + j, ref[j], table)
    out_ref[:, QH * HD :] = table.astype(f32).astype(bf16)


def attend(lengths, learner, slot_offset, mine, other, inverse, cosine, sine):
    tokens = mine.shape[0]
    return pl.pallas_call(
        attend_kernel,
        out_shape=jax.ShapeDtypeStruct((tokens, QH * HD + TABLE), bf16),
        in_specs=[SMEM] * 3 + [VMEM] * 5,
        out_specs=VMEM,
        scratch_shapes=[pltpu.VMEM((tokens, QH * HD), bf16)],
        name="attend",
    )(lengths, learner, slot_offset, mine, other, inverse, cosine, sine)


def rotary(lengths, tokens):
    slot = jnp.arange(tokens, dtype=jnp.int32)
    place = slot % PAIR
    lead = sum(jnp.where(slot // PAIR == k, lengths[2 * k], 0) for k in range(tokens // PAIR))
    position = jnp.where(place < lead, place, place - lead)
    lane = jnp.arange(HD, dtype=jnp.int32)
    frequency = rope_base ** (-(lane % (HD // 2)).astype(f32) * 2.0 / HD)
    angles = position.astype(f32)[:, None] * frequency[None, :]
    sign = jnp.where(lane < HD // 2, -1.0, 1.0)
    return jnp.cos(angles), jnp.sin(angles) * sign


def ranks(spread_ref):
    rows = spread_ref.shape[0]
    place = lax.broadcasted_iota(jnp.int32, (rows, 1), 0)
    table = spread_ref[:, QH * HD :].astype(f32)
    target = jnp.where((place // 4) % 2 == 1, table[:, 6:7], table[:, 4:5])
    key = target * rows + (place // 4).astype(f32)
    down = lax.broadcasted_iota(jnp.int32, (rows, rows), 0)
    along = lax.broadcasted_iota(jnp.int32, (rows, rows), 1)
    key_along = jnp.sum(jnp.where(down == along, key, 0.0), axis=0, keepdims=True)
    ahead_along = jnp.sum(jnp.where(key < key_along, 1.0, 0.0), axis=0, keepdims=True)
    return table, place, key, key_along, ahead_along.astype(jnp.int32), down


def arrange_kernel(spread_ref, out_ref):
    *_, ahead_along, down = ranks(spread_ref)
    row = lax.broadcasted_iota(jnp.int32, ahead_along.shape, 1)
    order = jnp.where(down == ahead_along + row % 4, 1.0, 0.0).astype(bf16)
    out_ref[...] = jnp.dot(order, spread_ref[:, : QH * HD], preferred_element_type=f32).astype(bf16)


def slots_kernel(me_ref, spread_ref, out_ref):
    table, place, key, key_along, _, down = ranks(spread_ref)
    ahead = jnp.sum(jnp.where(key_along < key, 1.0, 0.0), axis=1, keepdims=True).astype(jnp.int32)
    second = (place // 4) % 2 == 1
    row = lax.broadcasted_iota(jnp.int32, key_along.shape, 1)
    token = (row // 8) * 4 + row % 4

    def slots(k):
        mine = (ahead == 4 * (2 * me_ref[0] + k)) & (place % 4 == 0)

        def own(even, odd):
            values = jnp.where(second, table[:, odd : odd + 1], table[:, even : even + 1])
            return jnp.sum(jnp.where(mine, values, 0.0), axis=0, keepdims=True).astype(jnp.int32)

        lead = own(0, 2)
        return jnp.where(token < lead, own(8, 10) + token, own(9, 11) + token - lead)

    slot = jnp.where((row // 4) % 2 == 0, slots(0), slots(1))
    out_ref[...] = jnp.where(down == slot, 1.0, 0.0).astype(bf16)


def arrange(spread):
    return pl.pallas_call(
        arrange_kernel,
        out_shape=jax.ShapeDtypeStruct((spread.shape[0], QH * HD), bf16),
        in_specs=[VMEM],
        out_specs=VMEM,
        name="arrange",
    )(spread)


def slots(spread):
    return pl.pallas_call(
        slots_kernel,
        out_shape=jax.ShapeDtypeStruct((spread.shape[0],) * 2, bf16),
        in_specs=[SMEM, VMEM],
        out_specs=VMEM,
        name="slots",
    )(lax.axis_index("dp").reshape(1), spread)


def exchange(rows):
    blocks = rows.reshape(lax.axis_size("dp"), -1, rows.shape[1])
    return lax.all_to_all(blocks, "dp", split_axis=0, concat_axis=0, tiled=True).reshape(rows.shape)


def shards(hidden, lengths, learner, slot_offset, norm_gain, query_weight, keyval_weight):
    tokens = hidden.shape[0]
    block = norm_gain.shape[0]
    size = lax.axis_size("fsdp")
    ring = size // 2
    index = lax.axis_index("fsdp")
    onward = [(i, (i + 2 - 4 * (i % 2)) % size) for i in range(size)]
    swap = [(i, i ^ 1) for i in range(size)]

    def send(values, pairs):
        return lax.ppermute(values, "fsdp", pairs)

    def after(value, *others):
        return lax.optimization_barrier((value, *others))[0]

    where = jnp.stack([index // 2, index % 2])
    moving = list(fold(norm_gain, query_weight, keyval_weight))
    blocks = [(0, h, moving[h]) for h in (0, 1)]
    sums = None
    for step in range(1, ring):
        moving = [send(w, onward) for w in moving]
        if step == 1:
            give, inverse = prepare(hidden, after(where, *moving), block)
            got = send(give, swap)
            cosine, sine = rotary(after(lengths, *moving), tokens)
        if step in (3, 5, ring - 1):
            sums = partial(where, blocks, (hidden, got), sums)
            blocks = []
            moving[0] = after(moving[0], *sums)
        if step == 4:
            moving[0] = after(moving[0], inverse, cosine, sine)
        blocks += [(step, h, moving[h]) for h in (0, 1)]
    [other] = partial(where, blocks, (got,), sums[1:])
    other = send(other, swap)
    [mine] = partial(where, blocks, (hidden,), sums[:1])
    mixed = attend(lengths, learner, slot_offset, mine, other, inverse, cosine, sine)
    spread = exchange(mixed)
    landed = exchange(arrange(spread))
    return jnp.dot(slots(spread), landed, preferred_element_type=f32).astype(bf16)


def solution(mesh):
    placed = (
        P(("dp", "fsdp"), None),
        P(("dp", "fsdp")),
        P(("dp", "fsdp")),
        P(("dp", "fsdp")),
        P("fsdp"),
        P("fsdp", None),
        P("fsdp", None),
    )
    return jax.shard_map(
        shards, mesh=mesh, in_specs=placed, out_specs=P(("dp", "fsdp"), None), check_vma=False
    )
```

time: 162 us -> 163 us (level)
  waiting for transfers between devices: 7.13 us -> 62.6 us
  starting transfers between devices: 68 us -> 41.3 us
  blocking collectives: 38.2 us -> 24 us
  Pallas kernels: 33.6 us -> 24.1 us
  local copies, waits for them, and re-layouts: 9.2 us -> 4.64 us
    ppermute x16, waiting for transfers between devices: 7.13 us -> 53.2 us  [send(): return lax.ppermute(values, 'fsdp', pairs)]
    ppermute x16, starting transfers between devices: 57.8 us -> 36.5 us  [send(): return lax.ppermute(values, 'fsdp', pairs)]
    all_to_all x2 -> x1, blocking collectives: 38.2 us -> 24 us  [exchange(): lax.all_to_all(blocks, 'dp', split_axis=0, concat_axis=0, tiled=True)]
    all_to_all x1, waiting for transfers between devices: 0.01 us -> 9.33 us  [exchange(): lax.all_to_all(blocks, 'dp', split_axis=0, concat_axis=0, tiled=True)]
    pallas_call x12 -> x8, Pallas kernels: 22.6 us -> 13.3 us  [the longest x5 6.8 us: partial(): pl.pallas_call(functools.partial(partial_kernel, count, sides, carried),...]
    all_to_all x1, starting transfers between devices: 10.2 us -> 4.77 us  [exchange(): lax.all_to_all(blocks, 'dp', split_axis=0, concat_axis=0, tiled=True)]
    unnamed x28 -> x16, local copies, waits for them, and re-layouts: 6.66 us -> 4.03 us
  transfers between devices with their start and end apart: 17 -> 17, of which waited for: 2 -> 14; matrix products, arithmetic and copies ran while one was open for 2% -> 2% of each run, Pallas kernels for 12% -> 5%
where the time goes in v3:
time: 163 us; the launch traced here: 162 us
  waiting for transfers between devices  62.6 us (38%)
  starting transfers between devices  41.3 us (25%)
  Pallas kernels  24.1 us (15%)
  blocking collectives  24 us (15%)
  local copies, waits for them, and re-layouts  4.64 us (3%)
  other arithmetic  3.17 us (2%)
  matrix products  1.83 us (1%)
    ppermute x16, waiting for transfers between devices, send(): return lax.ppermute(values, 'fsdp', pairs)  53.2 us
    ppermute x16, starting transfers between devices, send(): return lax.ppermute(values, 'fsdp', pairs)  36.5 us
    all_to_all x1, blocking collectives, exchange(): lax.all_to_all(blocks, 'dp', split_axis=0, concat_axis=0, tiled=True)  24 us
    all_to_all x1, waiting for transfers between devices, exchange(): lax.all_to_all(blocks, 'dp', split_axis=0, concat_axis=0, tiled=True)  9.33 us
    pallas_call x1, Pallas kernels, prepare(): pl.pallas_call(prepare_kernel, out_shape=(jax.ShapeDtypeStruct((tokens, d...  7.39 us
    pallas_call x5, Pallas kernels, partial(): pl.pallas_call(functools.partial(partial_kernel, count, sides, carried),...  6.8 us
    all_to_all x1, starting transfers between devices, exchange(): lax.all_to_all(blocks, 'dp', split_axis=0, concat_axis=0, tiled=True)  4.77 us
    unnamed x16, local copies, waits for them, and re-layouts  4.03 us
  transfers between devices with their start and end apart: 17, of which 14 were waited for; matrix products, arithmetic and copies ran while one was open for 2% of the time, Pallas kernels for 5%

profile of v3, /device:TPU:8, one launch (start us, length us, event | category | flops | bytes accessed | tf_op | source)
XLA Modules:
  0.0 161.9 jit_solution(15738408066312008431)
XLA Ops:
  0.0 2.3 %fold_gain.1 = (bf16[256,768]{1,0:T(8,128)(2,1)}, bf16[256,768]{1,0:T(8,128)(2,1)}) custom-call(bf16[512]{0:T(512)(128)(2,1)} %gain_ref.1, bf16[512,512]{1,0:T(8,128)(2,1)} %query_ref.1, bf16[512,256]{1,0:T(8,128)(2,1)} %keyval_ref.1), custom_call_target="tpu_custom_call" | custom-call | tf_op jit(solution)/shard_map/fold_gain/pallas_call | solution.py:41
  2.3 4.3 %collective-permute-start = (bf16[256,768]{1,0:T(8,128)(2,1)}, bf16[256,768]{1,0:T(8,128)(2,1)S(1)}, u32[]{:S(2)}, u32[]{:S(2)}) collective-permute-start(bf16[256,768]{1,0:T(8,128)(2,1)} %get-tuple-element.21.refs_0_), channel_id=1, source_target_pairs={{0,2},{1,15},{2,4},{3,1},{4,6},{5,3},{6,8},{7,5},{8,10},{9,7},{10,... | collective-permute-start | bytes 1179656 | tf_op jit(solution)/shard_map/ppermute | solution.py:298
  6.6 4.3 %collective-permute-start.3 = (bf16[256,768]{1,0:T(8,128)(2,1)}, bf16[256,768]{1,0:T(8,128)(2,1)S(1)}, u32[]{:S(2)}, u32[]{:S(2)}) collective-permute-start(bf16[256,768]{1,0:T(8,128)(2,1)} %get-tuple-element.22.refs_1_), channel_id=1, source_target_pairs={{0,2},{1,15},{2,4},{3,1},{4,6},{5,3},{6,8},{7,5},{8,10},{9,7},{10,... | collective-permute-start | bytes 1179656 | tf_op jit(solution)/shard_map/ppermute | solution.py:298
  11.6 7.6 %collective-permute-done.refs_2_ = bf16[256,768]{1,0:T(8,128)(2,1)S(1)} collective-permute-done((bf16[256,768]{1,0:T(8,128)(2,1)}, bf16[256,768]{1,0:T(8,128)(2,1)S(1)}, u32[]{:S(2)}, u32[]{:S(2)}) %collective-permute-start) | collective-permute-done | bytes 393248 | tf_op jit(solution)/shard_map/ppermute | solution.py:298
  19.2 4.2 %collective-permute-done.3.refs_3_ = bf16[256,768]{1,0:T(8,128)(2,1)S(1)} collective-permute-done((bf16[256,768]{1,0:T(8,128)(2,1)}, bf16[256,768]{1,0:T(8,128)(2,1)S(1)}, u32[]{:S(2)}, u32[]{:S(2)}) %collective-permute-start.3) | collective-permute-done | bytes 393248 | tf_op jit(solution)/shard_map/ppermute | solution.py:298
  23.4 7.4 %prepare.1 = (bf16[256,4096]{1,0:T(8,128)(2,1)}, f32[256,128]{1,0:T(8,128)}) custom-call(s32[2]{0:T(128)} %pad_add_fusion.where_ref, bf16[256,8192]{1,0:T(8,128)(2,1)} %refs_3_.1, bf16[256,8192]{1,0:T(8,128)(2,1)} %refs_3_.1), custom_call_target="tpu_custom_call" | custom-call | flops 6291456 | bytes 6291456 | tf_op jit(solution)/shard_map/prepare/pallas_call | solution.py:76
  36.6 7.0 %collective-permute-done.4.refs_5_ = bf16[256,768]{1,0:T(8,128)(2,1)S(1)} collective-permute-done((bf16[256,768]{1,0:T(8,128)(2,1)S(1)}, bf16[256,768]{1,0:T(8,128)(2,1)S(1)}, u32[]{:S(2)}, u32[]{:S(2)}) %collective-permute-start.4) | collective-permute-done | bytes 393248 | tf_op jit(solution)/shard_map/ppermute | solution.py:298
  45.5 2.3 %collective-permute-done.1.refs_4_ = bf16[256,768]{1,0:T(8,128)(2,1)S(1)} collective-permute-done((bf16[256,768]{1,0:T(8,128)(2,1)S(1)}, bf16[256,768]{1,0:T(8,128)(2,1)S(1)}, u32[]{:S(2)}, u32[]{:S(2)}) %collective-permute-start.1) | collective-permute-done | bytes 393248 | tf_op jit(solution)/shard_map/ppermute | solution.py:298
  49.8 4.7 %collective-permute-done.8.refs_1_ = bf16[256,768]{1,0:T(8,128)(2,1)S(1)} collective-permute-done((bf16[256,768]{1,0:T(8,128)(2,1)S(1)}, bf16[256,768]{1,0:T(8,128)(2,1)S(1)}, u32[]{:S(2)}, u32[]{:S(2)}) %collective-permute-start.8) | collective-permute-done | bytes 393248 | tf_op jit(solution)/shard_map/ppermute | solution.py:298
  56.5 2.2 %copy-done = bf16[256,8192]{1,0:T(8,128)(2,1)S(1)} copy-done((bf16[256,8192]{1,0:T(8,128)(2,1)S(1)}, bf16[256,8192]{1,0:T(8,128)(2,1)}, u32[]{:S(2)}) %copy-start) | copy-done | bytes 4194328
  65.6 5.8 %collective-permute-done.6.refs_2_ = bf16[256,768]{1,0:T(8,128)(2,1)S(1)} collective-permute-done((bf16[256,768]{1,0:T(8,128)(2,1)S(1)}, bf16[256,768]{1,0:T(8,128)(2,1)S(1)}, u32[]{:S(2)}, u32[]{:S(2)}) %collective-permute-start.6) | collective-permute-done | bytes 393248 | tf_op jit(solution)/shard_map/ppermute | solution.py:298
  73.4 3.1 %collective-permute-start.12 = (bf16[256,768]{1,0:T(8,128)(2,1)S(1)}, bf16[256,768]{1,0:T(8,128)(2,1)S(1)}, u32[]{:S(2)}, u32[]{:S(2)}) collective-permute-start(bf16[256,768]{1,0:T(8,128)(2,1)S(1)} %collective-permute-done.9.refs_3_), channel_id=1, source_target_pairs={{0,2},{1,15},{2,4},{3,1},{4,6},{5,3},{6,8},{7,5},{8,10},{9,7},{10,... | collective-permute-start | bytes 1179656 | tf_op jit(solution)/shard_map/ppermute | solution.py:298
  78.0 4.3 %collective-permute-done.7.refs_0_ = bf16[256,768]{1,0:T(8,128)(2,1)S(1)} collective-permute-done((bf16[256,768]{1,0:T(8,128)(2,1)S(1)}, bf16[256,768]{1,0:T(8,128)(2,1)S(1)}, u32[]{:S(2)}, u32[]{:S(2)}) %collective-permute-start.7) | collective-permute-done | bytes 393248 | tf_op jit(solution)/shard_map/ppermute | solution.py:298
  84.2 2.3 %collective-permute-done.12.refs_1_ = bf16[256,768]{1,0:T(8,128)(2,1)S(1)} collective-permute-done((bf16[256,768]{1,0:T(8,128)(2,1)S(1)}, bf16[256,768]{1,0:T(8,128)(2,1)S(1)}, u32[]{:S(2)}, u32[]{:S(2)}) %collective-permute-start.12) | collective-permute-done | bytes 393248 | tf_op jit(solution)/shard_map/ppermute | solution.py:298
  88.4 4.7 %collective-permute-done.10.refs_2_ = bf16[256,768]{1,0:T(8,128)(2,1)S(1)} collective-permute-done((bf16[256,768]{1,0:T(8,128)(2,1)S(1)}, bf16[256,768]{1,0:T(8,128)(2,1)S(1)}, u32[]{:S(2)}, u32[]{:S(2)}) %collective-permute-start.10) | collective-permute-done | bytes 393248 | tf_op jit(solution)/shard_map/ppermute | solution.py:298
  95.1 2.3 %collective-permute-done.13.refs_3_ = bf16[256,768]{1,0:T(8,128)(2,1)S(1)} collective-permute-done((bf16[256,768]{1,0:T(8,128)(2,1)S(1)}, bf16[256,768]{1,0:T(8,128)(2,1)S(1)}, u32[]{:S(2)}, u32[]{:S(2)}) %collective-permute-start.13) | collective-permute-done | bytes 393248 | tf_op jit(solution)/shard_map/ppermute | solution.py:298
  100.8 3.2 %collective-permute-done.11.refs_0_ = bf16[256,768]{1,0:T(8,128)(2,1)S(1)} collective-permute-done((bf16[256,768]{1,0:T(8,128)(2,1)S(1)}, bf16[256,768]{1,0:T(8,128)(2,1)S(1)}, u32[]{:S(2)}, u32[]{:S(2)}) %collective-permute-start.11) | collective-permute-done | bytes 393248 | tf_op jit(solution)/shard_map/ppermute | solution.py:298
  104.1 4.2 %collective-permute-done.14.refs_1_ = bf16[256,768]{1,0:T(8,128)(2,1)S(1)} collective-permute-done((bf16[256,768]{1,0:T(8,128)(2,1)S(1)}, bf16[256,768]{1,0:T(8,128)(2,1)S(1)}, u32[]{:S(2)}, u32[]{:S(2)}) %collective-permute-start.14) | collective-permute-done | bytes 393248 | tf_op jit(solution)/shard_map/ppermute | solution.py:298
  114.3 3.4 %attend.1 = bf16[256,640]{1,0:T(8,128)(2,1)} custom-call(s32[4]{0:T(128)} %lengths_ref.1, s32[4]{0:T(128)} %learner_ref.1, s32[4]{0:T(128)} %offset_ref.1, f32[256,768]{1,0:T(8,128)} %copy-done.2, f32[256,768]{1,0:T(8,128)} %copy-done.6, f32[256,128]{1,0:T(8,128)} %get-tuple-element.28.inverse_ref, f32[256,128]{1,0:T(8,128)} %get-tuple-element.38.cosine_ref, ...), custom_call_target="tpu_custom_call" | custom-call | tf_op jit(solution)/shard_map/attend/pallas_call | solution.py:200
  117.7 24.0 %all_to_all.10 = bf16[32,8,640]{2,1,0:T(8,128)(2,1)} all-to-all(bf16[32,8,640]{2,1,0:T(8,128)(2,1)} %bitcast.14), channel_id=1, replica_groups=mesh['dp'=32,'fsdp'=16] {'dp'}, dimensions={0} | all-to-all | bytes 655360 | tf_op jit(solution)/shard_map/all_to_all | solution.py:285
  141.7 2.1 %arrange.1 = bf16[256,512]{1,0:T(8,128)(2,1)} custom-call(bf16[256,640]{1,0:T(8,128)(2,1)} %bitcast.12), custom_call_target="tpu_custom_call" | custom-call | tf_op jit(solution)/shard_map/arrange/pallas_call | solution.py:264
  143.8 4.8 %all-to-all-start.1 = ((bf16[32,8,512]{2,1,0:T(8,128)(2,1)}), bf16[32,8,512]{2,1,0:T(8,128)(2,1)S(1)}, u32[]{:S(2)}, u32[]{:S(2)}) async-start(bf16[32,8,512]{2,1,0:T(8,128)(2,1)} %bitcast.15), calls=%async_computation.1 | async-start | bytes 524288 | tf_op jit(solution)/shard_map/all_to_all | solution.py:285
  148.6 2.1 %slots.1 = bf16[256,256]{1,0:T(8,128)(2,1)} custom-call(s32[1]{0:T(128)} %bitcast.me_ref, bf16[256,640]{1,0:T(8,128)(2,1)} %bitcast.13), custom_call_target="tpu_custom_call" | custom-call | tf_op jit(solution)/shard_map/slots/pallas_call | solution.py:274
  150.7 9.3 %all-to-all-done.1 = bf16[32,8,512]{2,1,0:T(8,128)(2,1)S(1)} async-done(((bf16[32,8,512]{2,1,0:T(8,128)(2,1)}), bf16[32,8,512]{2,1,0:T(8,128)(2,1)S(1)}, u32[]{:S(2)}, u32[]{:S(2)}) %all-to-all-start.1) | async-done | bytes 262176 | tf_op jit(solution)/shard_map/all_to_all | solution.py:285
  (43 shorter events, 39.6 us)
Async XLA Ops:
  2.3 16.9 %collective-permute-start = (bf16[256,768]{1,0:T(8,128)(2,1)}, bf16[256,768]{1,0:T(8,128)(2,1)S(1)}, u32[]{:S(2)}, u32[]{:S(2)}) collective-permute-start(bf16[256,768]{1,0:T(8,128)(2,1)} %get-tuple-element.21.refs_0_), channel_id=1, source_target_pairs={{0,2},{1,15},{2,4},{3,1},{4,6},{5,3},{6,8},{7,5},{8,10},{9,7},{10,... | collective-permute-start | bytes 1179656 | tf_op jit(solution)/shard_map/ppermute | solution.py:298
  6.6 16.8 %collective-permute-start.3 = (bf16[256,768]{1,0:T(8,128)(2,1)}, bf16[256,768]{1,0:T(8,128)(2,1)S(1)}, u32[]{:S(2)}, u32[]{:S(2)}) collective-permute-start(bf16[256,768]{1,0:T(8,128)(2,1)} %get-tuple-element.22.refs_1_), channel_id=1, source_target_pairs={{0,2},{1,15},{2,4},{3,1},{4,6},{5,3},{6,8},{7,5},{8,10},{9,7},{10,... | collective-permute-start | bytes 1179656 | tf_op jit(solution)/shard_map/ppermute | solution.py:298
  11.6 44.8 %copy-start.3 = (bf16[256,768]{1,0:T(8,128)(2,1)S(1)}, bf16[256,768]{1,0:T(8,128)(2,1)}, u32[]{:S(2)}) copy-start(bf16[256,768]{1,0:T(8,128)(2,1)} %get-tuple-element.21.refs_0_) | copy-start | bytes 1179652
  11.6 44.9 %copy-start.4 = (bf16[256,768]{1,0:T(8,128)(2,1)S(1)}, bf16[256,768]{1,0:T(8,128)(2,1)}, u32[]{:S(2)}) copy-start(bf16[256,768]{1,0:T(8,128)(2,1)} %get-tuple-element.22.refs_1_) | copy-start | bytes 1179652
  11.6 44.9 %copy-start.5 = (s32[2]{0:T(128)S(1)}, s32[2]{0:T(128)}, u32[]{:S(2)}) copy-start(s32[2]{0:T(128)} %pad_add_fusion.where_ref) | copy-start | bytes 28
  30.8 25.6 %collective-permute-start.5 = (bf16[256,4096]{1,0:T(8,128)(2,1)}, bf16[256,4096]{1,0:T(8,128)(2,1)S(1)}, u32[]{:S(2)}, u32[]{:S(2)}) collective-permute-start(bf16[256,4096]{1,0:T(8,128)(2,1)} %get-tuple-element.24), channel_id=1, source_target_pairs={{0,1},{1,0},{2,3},{3,2},{4,5},{5,4},{6,7},{7,6},{8,9},{9,8},{10,11... | collective-permute-start | bytes 6291464 | tf_op jit(solution)/shard_map/ppermute | solution.py:298
  32.7 10.9 %collective-permute-start.4 = (bf16[256,768]{1,0:T(8,128)(2,1)S(1)}, bf16[256,768]{1,0:T(8,128)(2,1)S(1)}, u32[]{:S(2)}, u32[]{:S(2)}) collective-permute-start(bf16[256,768]{1,0:T(8,128)(2,1)S(1)} %collective-permute-done.3.refs_3_), channel_id=1, source_target_pairs={{0,2},{1,15},{2,4},{3,1},{4,6},{5,3},{6,8},{7,5},{8,10},{9,7},{10,... | collective-permute-start | bytes 1179656 | tf_op jit(solution)/shard_map/ppermute | solution.py:298
  34.7 13.2 %collective-permute-start.1 = (bf16[256,768]{1,0:T(8,128)(2,1)S(1)}, bf16[256,768]{1,0:T(8,128)(2,1)S(1)}, u32[]{:S(2)}, u32[]{:S(2)}) collective-permute-start(bf16[256,768]{1,0:T(8,128)(2,1)S(1)} %collective-permute-done.refs_2_), channel_id=1, source_target_pairs={{0,2},{1,15},{2,4},{3,1},{4,6},{5,3},{6,8},{7,5},{8,10},{9,7},{10,... | collective-permute-start | bytes 1179656 | tf_op jit(solution)/shard_map/ppermute | solution.py:298
  43.6 10.9 %collective-permute-start.8 = (bf16[256,768]{1,0:T(8,128)(2,1)S(1)}, bf16[256,768]{1,0:T(8,128)(2,1)S(1)}, u32[]{:S(2)}, u32[]{:S(2)}) collective-permute-start(bf16[256,768]{1,0:T(8,128)(2,1)S(1)} %collective-permute-done.4.refs_5_), channel_id=1, source_target_pairs={{0,2},{1,15},{2,4},{3,1},{4,6},{5,3},{6,8},{7,5},{8,10},{9,7},{10,... | collective-permute-start | bytes 1179656 | tf_op jit(solution)/shard_map/ppermute | solution.py:298
  47.8 12.7 %collective-permute-start.2 = (bf16[256,768]{1,0:T(8,128)(2,1)S(1)}, bf16[256,768]{1,0:T(8,128)(2,1)S(1)}, u32[]{:S(2)}, u32[]{:S(2)}) collective-permute-start(bf16[256,768]{1,0:T(8,128)(2,1)S(1)} %collective-permute-done.1.refs_4_), channel_id=1, source_target_pairs={{0,2},{1,15},{2,4},{3,1},{4,6},{5,3},{6,8},{7,5},{8,10},{9,7},{10,... | collective-permute-start | bytes 1179656 | tf_op jit(solution)/shard_map/ppermute | solution.py:298
  49.7 12.8 %copy-start.7 = (s32[4]{0:T(128)S(1)}, s32[4]{0:T(128)}, u32[]{:S(2)}) copy-start(s32[4]{0:T(128)} %lengths_ref.1) | copy-start | bytes 52
  54.5 18.9 %collective-permute-start.9 = (bf16[256,768]{1,0:T(8,128)(2,1)S(1)}, bf16[256,768]{1,0:T(8,128)(2,1)S(1)}, u32[]{:S(2)}, u32[]{:S(2)}) collective-permute-start(bf16[256,768]{1,0:T(8,128)(2,1)S(1)} %collective-permute-done.8.refs_1_), channel_id=1, source_target_pairs={{0,2},{1,15},{2,4},{3,1},{4,6},{5,3},{6,8},{7,5},{8,10},{9,7},{10,... | collective-permute-start | bytes 1179656 | tf_op jit(solution)/shard_map/ppermute | solution.py:298
  56.4 2.2 %copy-start = (bf16[256,8192]{1,0:T(8,128)(2,1)S(1)}, bf16[256,8192]{1,0:T(8,128)(2,1)}, u32[]{:S(2)}) copy-start(bf16[256,8192]{1,0:T(8,128)(2,1)} %refs_3_.1) | copy-start | bytes 12582916
  58.6 17.8 %copy-start.1 = (bf16[256,8192]{1,0:T(8,128)(2,1)S(1)}, bf16[256,8192]{1,0:T(8,128)(2,1)}, u32[]{:S(2)}) copy-start(bf16[256,8192]{1,0:T(8,128)(2,1)} %refs_3_.1) | copy-start | bytes 12582916
  60.6 10.9 %collective-permute-start.6 = (bf16[256,768]{1,0:T(8,128)(2,1)S(1)}, bf16[256,768]{1,0:T(8,128)(2,1)S(1)}, u32[]{:S(2)}, u32[]{:S(2)}) collective-permute-start(bf16[256,768]{1,0:T(8,128)(2,1)S(1)} %collective-permute-done.2.refs_0_), channel_id=1, source_target_pairs={{0,2},{1,15},{2,4},{3,1},{4,6},{5,3},{6,8},{7,5},{8,10},{9,7},{10,... | collective-permute-start | bytes 1179656 | tf_op jit(solution)/shard_map/ppermute | solution.py:298
  71.4 10.9 %collective-permute-start.7 = (bf16[256,768]{1,0:T(8,128)(2,1)S(1)}, bf16[256,768]{1,0:T(8,128)(2,1)S(1)}, u32[]{:S(2)}, u32[]{:S(2)}) collective-permute-start(bf16[256,768]{1,0:T(8,128)(2,1)S(1)} %collective-permute-done.6.refs_2_), channel_id=1, source_target_pairs={{0,2},{1,15},{2,4},{3,1},{4,6},{5,3},{6,8},{7,5},{8,10},{9,7},{10,... | collective-permute-start | bytes 1179656 | tf_op jit(solution)/shard_map/ppermute | solution.py:298
  73.4 13.2 %collective-permute-start.12 = (bf16[256,768]{1,0:T(8,128)(2,1)S(1)}, bf16[256,768]{1,0:T(8,128)(2,1)S(1)}, u32[]{:S(2)}, u32[]{:S(2)}) collective-permute-start(bf16[256,768]{1,0:T(8,128)(2,1)S(1)} %collective-permute-done.9.refs_3_), channel_id=1, source_target_pairs={{0,2},{1,15},{2,4},{3,1},{4,6},{5,3},{6,8},{7,5},{8,10},{9,7},{10,... | collective-permute-start | bytes 1179656 | tf_op jit(solution)/shard_map/ppermute | solution.py:298
  82.3 10.9 %collective-permute-start.10 = (bf16[256,768]{1,0:T(8,128)(2,1)S(1)}, bf16[256,768]{1,0:T(8,128)(2,1)S(1)}, u32[]{:S(2)}, u32[]{:S(2)}) collective-permute-start(bf16[256,768]{1,0:T(8,128)(2,1)S(1)} %collective-permute-done.7.refs_0_), channel_id=1, source_target_pairs={{0,2},{1,15},{2,4},{3,1},{4,6},{5,3},{6,8},{7,5},{8,10},{9,7},{10,... | collective-permute-start | bytes 1179656 | tf_op jit(solution)/shard_map/ppermute | solution.py:298
  86.5 10.9 %collective-permute-start.13 = (bf16[256,768]{1,0:T(8,128)(2,1)S(1)}, bf16[256,768]{1,0:T(8,128)(2,1)S(1)}, u32[]{:S(2)}, u32[]{:S(2)}) collective-permute-start(bf16[256,768]{1,0:T(8,128)(2,1)S(1)} %collective-permute-done.12.refs_1_), channel_id=1, source_target_pairs={{0,2},{1,15},{2,4},{3,1},{4,6},{5,3},{6,8},{7,5},{8,10},{9,7},{10,... | collective-permute-start | bytes 1179656 | tf_op jit(solution)/shard_map/ppermute | solution.py:298
  93.2 10.9 %collective-permute-start.11 = (bf16[256,768]{1,0:T(8,128)(2,1)S(1)}, bf16[256,768]{1,0:T(8,128)(2,1)S(1)}, u32[]{:S(2)}, u32[]{:S(2)}) collective-permute-start(bf16[256,768]{1,0:T(8,128)(2,1)S(1)} %collective-permute-done.10.refs_2_), channel_id=1, source_target_pairs={{0,2},{1,15},{2,4},{3,1},{4,6},{5,3},{6,8},{7,5},{8,10},{9,7},{10,... | collective-permute-start | bytes 1179656 | tf_op jit(solution)/shard_map/ppermute | solution.py:298
  97.4 10.9 %collective-permute-start.14 = (bf16[256,768]{1,0:T(8,128)(2,1)S(1)}, bf16[256,768]{1,0:T(8,128)(2,1)S(1)}, u32[]{:S(2)}, u32[]{:S(2)}) collective-permute-start(bf16[256,768]{1,0:T(8,128)(2,1)S(1)} %collective-permute-done.13.refs_3_), channel_id=1, source_target_pairs={{0,2},{1,15},{2,4},{3,1},{4,6},{5,3},{6,8},{7,5},{8,10},{9,7},{10,... | collective-permute-start | bytes 1179656 | tf_op jit(solution)/shard_map/ppermute | solution.py:298
  109.2 4.2 %collective-permute-start.15 = (f32[256,768]{1,0:T(8,128)S(1)}, f32[256,768]{1,0:T(8,128)S(1)}, u32[]{:S(2)}, u32[]{:S(2)}) collective-permute-start(f32[256,768]{1,0:T(8,128)S(1)} %partial_sums.9), channel_id=1, source_target_pairs={{0,1},{1,0},{2,3},{3,2},{4,5},{5,4},{6,7},{7,6},{8,9},{9,8},{10,11... | collective-permute-start | bytes 2359304 | tf_op jit(solution)/shard_map/ppermute | solution.py:298
  113.4 0.9 copy-start.6
  143.8 16.2 %all-to-all-start.1 = ((bf16[32,8,512]{2,1,0:T(8,128)(2,1)}), bf16[32,8,512]{2,1,0:T(8,128)(2,1)S(1)}, u32[]{:S(2)}, u32[]{:S(2)}) async-start(bf16[32,8,512]{2,1,0:T(8,128)(2,1)} %bitcast.15), calls=%async_computation.1 | async-start | bytes 524288 | tf_op jit(solution)/shard_map/all_to_all | solution.py:285
  (1 other events, 0.9 us)

commit v4 on v3

v4 whole, which is shorter than its diff:
```python
import functools

import jax
import jax.numpy as jnp
from jax import lax
from jax.experimental import pallas as pl
from jax.experimental.pallas import tpu as pltpu
from jax.sharding import PartitionSpec as P

HD = 128
QH = 4
WIDE = (QH + 2) * HD
PAIR = 128
TABLE = 128
PIECE = 256

rope_base = 500000.0
norm_eps = 1e-05

f32 = jnp.float32
bf16 = jnp.bfloat16


VMEM = pl.BlockSpec(memory_space=pltpu.VMEM)
SMEM = pl.BlockSpec(memory_space=pltpu.SMEM)


def fold_kernel(gain_ref, query_ref, keyval_ref, *out_refs):
    rows = 256
    row = lax.broadcasted_iota(jnp.int32, (rows, rows), 0)
    column = lax.broadcasted_iota(jnp.int32, (rows, rows), 1)
    for start in range(0, query_ref.shape[0], rows):
        own = slice(start, start + rows)
        gain = gain_ref[own].astype(f32).reshape(1, rows)
        gain = jnp.where(row == column, gain, 0.0).astype(bf16)
        pieces = [query_ref[own, :PIECE], query_ref[own, PIECE:], keyval_ref[own, :]]
        for piece, out_ref in zip(pieces, out_refs):
            out_ref[own, :] = jnp.dot(gain, piece, preferred_element_type=f32).astype(bf16)


def fold(gain, query_weight, keyval_weight):
    pieces = WIDE // PIECE
    return pl.pallas_call(
        fold_kernel,
        out_shape=[jax.ShapeDtypeStruct((gain.shape[0], PIECE), bf16)] * pieces,
        in_specs=[VMEM] * 3,
        out_specs=[VMEM] * pieces,
        name="fold_gain",
    )(gain, query_weight, keyval_weight)


def inverse_kernel(rows_ref, inverse_ref, products):
    step = pl.program_id(0)
    rows = rows_ref[...]
    part = lax.dot_general(rows, rows, (((1,), (1,)), ((), ())), preferred_element_type=f32)

    @pl.when(step == 0)
    def _():
        products[...] = part

    @pl.when(step > 0)
    def _():
        products[...] += part

    @pl.when(step == pl.num_programs(0) - 1)
    def _():
        depth = pl.num_programs(0) * rows_ref.shape[1]
        row = lax.broadcasted_iota(jnp.int32, products.shape, 0)
        column = lax.broadcasted_iota(jnp.int32, products.shape, 1)
        squares = jnp.sum(jnp.where(row == column, products[...], 0.0), axis=1, keepdims=True)
        inverse_ref[...] = jnp.broadcast_to(lax.rsqrt(squares / depth + norm_eps), inverse_ref.shape)


def inverses(rows):
    tokens, depth = rows.shape
    steps = 4
    return pl.pallas_call(
        inverse_kernel,
        out_shape=jax.ShapeDtypeStruct((tokens, HD), f32),
        grid=(steps,),
        in_specs=[pl.BlockSpec((tokens, depth // steps), lambda i: (0, i))],
        out_specs=pl.BlockSpec((tokens, HD), lambda i: (0, 0)),
        scratch_shapes=[pltpu.VMEM((tokens, tokens), f32)],
        compiler_params=pltpu.CompilerParams(vmem_limit_bytes=60 << 20),
        cost_estimate=pl.CostEstimate(
            flops=2 * tokens * tokens * depth, bytes_accessed=2 * tokens * depth, transcendentals=0
        ),
        name="inverse",
    )(rows)


def partial_kernel(distances, sides, carried, *refs):
    pieces = WIDE // PIECE
    count = len(distances)
    weights, refs = refs[: count * pieces], refs[count * pieces :]
    rows, refs = refs[:sides], refs[sides:]
    before, refs = refs[: sides * carried], refs[sides * carried :]
    out_refs, (columns, arrived) = refs[:sides], refs[sides:]
    depth = columns.shape[2]
    index = lax.axis_index("fsdp")
    place, core = lax.div(index, 2), lax.rem(index, 2)
    ring = lax.axis_size("fsdp") // 2
    copies = []
    for side in range(sides):
        for i, distance in enumerate(distances):
            origin = lax.rem(place + ring + (2 * core - 1) * distance, ring)
            start = pl.multiple_of((2 * origin + core) * depth, depth)
            at = side * count + i
            copies.append(
                pltpu.make_async_copy(
                    rows[side].at[:, pl.ds(start, depth)], columns.at[at], arrived.at[at]
                )
            )
            copies[-1].start()
    for side in range(sides):
        for copy in copies[side * count : (side + 1) * count]:
            copy.wait()
        for piece in range(pieces):
            own = slice(piece * PIECE, (piece + 1) * PIECE)
            total = before[side][:, own] if carried else None
            for i in range(count):
                part = jnp.dot(
                    columns[side * count + i],
                    weights[i * pieces + piece][...],
                    preferred_element_type=f32,
                )
                total = part if total is None else total + part
            out_refs[side][:, own] = total


def partial(blocks, rows, before, vmem):
    count, sides = len(blocks), len(rows)
    weights = [w for _, pieces in blocks for w in pieces]
    tokens, depth = rows[0].shape[0], weights[0].shape[0]
    carried = before is not None
    shape = jax.ShapeDtypeStruct((tokens, WIDE), f32)
    return pl.pallas_call(
        functools.partial(partial_kernel, [d for d, _ in blocks], sides, carried),
        out_shape=[shape] * sides,
        in_specs=[VMEM] * len(weights)
        + [pl.BlockSpec(memory_space=pltpu.HBM)] * sides
        + [VMEM] * (sides * carried),
        out_specs=[VMEM] * sides,
        scratch_shapes=[
            pltpu.VMEM((sides * count, tokens, depth), bf16),
            pltpu.SemaphoreType.DMA((sides * count,)),
        ],
        compiler_params=pltpu.CompilerParams(vmem_limit_bytes=vmem << 20),
        cost_estimate=pl.CostEstimate(
            flops=2 * tokens * depth * WIDE * count * sides,
            bytes_accessed=2 * depth * (sides * tokens + WIDE) * count + 8 * tokens * WIDE * sides,
            transcendentals=0,
        ),
        name="partial_sums",
    )(*weights, *rows, *(before or []))


def attend_kernel(
    lengths_ref, learner_ref, offset_ref, mine_ref, other_ref, inverse_ref, cosine_ref, sine_ref, out_ref, mixed
):
    tokens = out_ref.shape[0]
    inverse = inverse_ref[...]
    cosine, sine = cosine_ref[...] * inverse, sine_ref[...] * inverse

    def product(head):
        own = slice(head * HD, (head + 1) * HD)
        return mine_ref[:, own] + other_ref[:, own]

    def rotated(head):
        values = product(head)
        return (values * cosine + pltpu.roll(values, HD // 2, 1) * sine).astype(bf16)

    heads = [rotated(h) for h in range(QH)]
    key_part = rotated(QH)
    value_part = (product(QH + 1) * inverse).astype(bf16)
    asks = lax.broadcasted_iota(jnp.int32, (PAIR, PAIR), 0)
    keys = lax.broadcasted_iota(jnp.int32, (PAIR, PAIR), 1)
    for pair in range(tokens // PAIR):
        own = slice(pair * PAIR, (pair + 1) * PAIR)
        lead = lengths_ref[2 * pair]
        allowed = (keys <= asks) & ((asks < lead) | (keys >= lead))
        barred = jnp.concatenate([jnp.where(allowed, 0.0, -1e30)] * QH, axis=0)
        query = jnp.concatenate([h[own] for h in heads], axis=0)
        scores = lax.dot_general(
            query, key_part[own], (((1,), (1,)), ((), ())), preferred_element_type=f32
        ) * (HD**-0.5)
        scores += barred
        weights = jnp.exp(scores - jnp.max(scores, axis=1, keepdims=True))
        share = 1.0 / jnp.sum(weights, axis=1, keepdims=True)
        probability = (weights * share).astype(bf16)
        result = jnp.dot(probability, value_part[own], preferred_element_type=f32).astype(bf16)
        for h in range(QH):
            mixed[own, h * HD : (h + 1) * HD] = result[h * PAIR : (h + 1) * PAIR]
    row = lax.broadcasted_iota(jnp.int32, (tokens, tokens), 0)
    token = lax.broadcasted_iota(jnp.int32, (tokens, tokens), 1)
    source = ((row >> 2) & 1) * PAIR + (row >> 3) * 4 + (row & 3)
    order = jnp.where(token == source, 1.0, 0.0).astype(bf16)
    out_ref[:, : QH * HD] = jnp.dot(order, mixed[...], preferred_element_type=f32).astype(bf16)
    lane = lax.broadcasted_iota(jnp.int32, (tokens, TABLE), 1)
    table = jnp.zeros((tokens, TABLE), jnp.int32)
    for i, ref in enumerate((lengths_ref, learner_ref, offset_ref)):
        for j in range(4):
            table = jnp.where(lane == 4 * i + j, ref[j], table)
    out_ref[:, QH * HD :] = table.astype(f32).astype(bf16)


def attend(lengths, learner, slot_offset, mine, other, inverse, cosine, sine):
    tokens = mine.shape[0]
    return pl.pallas_call(
        attend_kernel,
        out_shape=jax.ShapeDtypeStruct((tokens, QH * HD + TABLE), bf16),
        in_specs=[SMEM] * 3 + [VMEM] * 5,
        out_specs=VMEM,
        scratch_shapes=[pltpu.VMEM((tokens, QH * HD), bf16)],
        compiler_params=pltpu.CompilerParams(vmem_limit_bytes=16 << 20),
        name="attend",
    )(lengths, learner, slot_offset, mine, other, inverse, cosine, sine)


def rotary(lengths, tokens):
    slot = jnp.arange(tokens, dtype=jnp.int32)
    place = slot % PAIR
    lead = sum(jnp.where(slot // PAIR == k, lengths[2 * k], 0) for k in range(tokens // PAIR))
    position = jnp.where(place < lead, place, place - lead)
    lane = jnp.arange(HD, dtype=jnp.int32)
    frequency = rope_base ** (-(lane % (HD // 2)).astype(f32) * 2.0 / HD)
    angles = position.astype(f32)[:, None] * frequency[None, :]
    sign = jnp.where(lane < HD // 2, -1.0, 1.0)
    return jnp.cos(angles), jnp.sin(angles) * sign


def ranks(spread_ref):
    rows = spread_ref.shape[0]
    place = lax.broadcasted_iota(jnp.int32, (rows, 1), 0)
    table = spread_ref[:, QH * HD :].astype(f32)
    target = jnp.where((place >> 2) & 1 == 1, table[:, 6:7], table[:, 4:5])
    key = target * rows + (place >> 2).astype(f32)
    down = lax.broadcasted_iota(jnp.int32, (rows, rows), 0)
    along = lax.broadcasted_iota(jnp.int32, (rows, rows), 1)
    key_along = jnp.sum(jnp.where(down == along, key, 0.0), axis=0, keepdims=True)
    ahead_along = jnp.sum(jnp.where(key < key_along, 1.0, 0.0), axis=0, keepdims=True)
    return table, place, key, key_along, ahead_along.astype(jnp.int32), down


def arrange_kernel(spread_ref, out_ref):
    *_, ahead_along, down = ranks(spread_ref)
    row = lax.broadcasted_iota(jnp.int32, ahead_along.shape, 1)
    order = jnp.where(down == ahead_along + (row & 3), 1.0, 0.0).astype(bf16)
    out_ref[...] = jnp.dot(order, spread_ref[:, : QH * HD], preferred_element_type=f32).astype(bf16)


def slots_kernel(me_ref, spread_ref, out_ref):
    table, place, key, key_along, _, down = ranks(spread_ref)
    ahead = jnp.sum(jnp.where(key_along < key, 1.0, 0.0), axis=1, keepdims=True).astype(jnp.int32)
    second = (place >> 2) & 1 == 1
    row = lax.broadcasted_iota(jnp.int32, key_along.shape, 1)
    token = (row >> 3) * 4 + (row & 3)

    def slots(k):
        mine = (ahead == 4 * (2 * me_ref[0] + k)) & (place & 3 == 0)

        def own(even, odd):
            values = jnp.where(second, table[:, odd : odd + 1], table[:, even : even + 1])
            return jnp.sum(jnp.where(mine, values, 0.0), axis=0, keepdims=True).astype(jnp.int32)

        lead = own(0, 2)
        return jnp.where(token < lead, own(8, 10) + token, own(9, 11) + token - lead)

    slot = jnp.where((row >> 2) & 1 == 0, slots(0), slots(1))
    out_ref[...] = jnp.where(down == slot, 1.0, 0.0).astype(bf16)


def arrange(spread):
    return pl.pallas_call(
        arrange_kernel,
        out_shape=jax.ShapeDtypeStruct((spread.shape[0], QH * HD), bf16),
        in_specs=[VMEM],
        out_specs=VMEM,
        name="arrange",
    )(spread)


def slots(spread):
    return pl.pallas_call(
        slots_kernel,
        out_shape=jax.ShapeDtypeStruct((spread.shape[0],) * 2, bf16),
        in_specs=[SMEM, VMEM],
        out_specs=VMEM,
        name="slots",
    )(lax.axis_index("dp").reshape(1), spread)


def exchange(rows):
    blocks = rows.reshape(lax.axis_size("dp"), -1, rows.shape[1])
    return lax.all_to_all(blocks, "dp", split_axis=0, concat_axis=0, tiled=True).reshape(rows.shape)


def shards(hidden, lengths, learner, slot_offset, norm_gain, query_weight, keyval_weight):
    tokens = hidden.shape[0]
    size = lax.axis_size("fsdp")
    ring = size // 2
    onward = [(i, (i + 2 - 4 * (i % 2)) % size) for i in range(size)]
    swap = [(i, i ^ 1) for i in range(size)]

    def send(values, pairs):
        return lax.ppermute(values, "fsdp", pairs)

    def after(value, *others):
        return lax.optimization_barrier((value, *others))[0]

    moving = fold(norm_gain, query_weight, keyval_weight)
    blocks = [(0, list(moving))]
    sums = None
    got = send(hidden, swap)
    for step in range(1, ring):
        moving = [send(w, onward) for w in moving]
        if step == 3:
            inverse = inverses(after(hidden, moving[2]))
            cosine, sine = rotary(after(lengths, moving[2]), tokens)
        if step in (3, 5, ring - 1):
            sums = partial(blocks, (hidden, got), sums, 60)
            blocks = []
            moving[0] = after(moving[0], *sums)
        if step == 4:
            moving[0] = after(moving[0], inverse, cosine, sine)
        blocks += [(step, list(moving))]
    [other] = partial(blocks, (got,), sums[1:], 28)
    other = send(other, swap)
    [mine] = partial(blocks, (hidden,), sums[:1], 28)
    mixed = attend(lengths, learner, slot_offset, mine, other, inverse, cosine, sine)
    spread = exchange(mixed)
    landed = exchange(arrange(spread))
    return jnp.dot(slots(spread), landed, preferred_element_type=f32).astype(bf16)


def solution(mesh):
    placed = (
        P(("dp", "fsdp"), None),
        P(("dp", "fsdp")),
        P(("dp", "fsdp")),
        P(("dp", "fsdp")),
        P("fsdp"),
        P("fsdp", None),
        P("fsdp", None),
    )
    return jax.shard_map(
        shards, mesh=mesh, in_specs=placed, out_specs=P(("dp", "fsdp"), None), check_vma=False
    )
```

time: 163 us -> 156 us (0.957)
  waiting for transfers between devices: 62.6 us -> 17.6 us
  starting transfers between devices: 41.3 us -> 75.9 us
  Pallas kernels: 24.1 us -> 30.9 us
  local copies, waits for them, and re-layouts: 4.64 us -> 2.63 us
    ppermute x16 -> x23, waiting for transfers between devices: 53.2 us -> 8.23 us  [send(): return lax.ppermute(values, 'fsdp', pairs)]
    ppermute x16 -> x23, starting transfers between devices: 36.5 us -> 71.1 us  [send(): return lax.ppermute(values, 'fsdp', pairs)]
    pallas_call x7, Pallas kernels: 16.5 us -> 24.9 us  [the longest x5 17.8 us: partial(): pl.pallas_call(functools.partial(partial_kernel, [d for d, _ in blocks],...]
    unnamed x16 -> x50, local copies, waits for them, and re-layouts: 4.03 us -> 1.24 us
    pallas_call x1, Pallas kernels: 3.43 us -> 1.77 us  [attend(): pl.pallas_call(attend_kernel, out_shape=jax.ShapeDtypeStruct((tokens, QH...]
  transfers between devices with their start and end apart: 17 -> 24, of which waited for: 14 -> 6; matrix products, arithmetic and copies ran while one was open for 2% -> 2% of each run, Pallas kernels for 5% -> 17%
where the time goes in v4:
time: 156 us; the launch traced here: 155 us
  starting transfers between devices  75.9 us (49%)
  Pallas kernels  30.9 us (20%)
  blocking collectives  23.8 us (15%)
  waiting for transfers between devices  17.6 us (11%)
  local copies, waits for them, and re-layouts  2.63 us (2%)
  other arithmetic  1.85 us (1%)
  matrix products  1.83 us (1%)
    ppermute x23, starting transfers between devices, send(): return lax.ppermute(values, 'fsdp', pairs)  71.1 us
    all_to_all x1, blocking collectives, exchange(): lax.all_to_all(blocks, 'dp', split_axis=0, concat_axis=0, tiled=True)  23.8 us
    pallas_call x5, Pallas kernels, partial(): pl.pallas_call(functools.partial(partial_kernel, [d for d, _ in blocks],...  17.8 us
    all_to_all x1, waiting for transfers between devices, exchange(): lax.all_to_all(blocks, 'dp', split_axis=0, concat_axis=0, tiled=True)  9.35 us
    ppermute x23, waiting for transfers between devices, send(): return lax.ppermute(values, 'fsdp', pairs)  8.23 us
    pallas_call x1, Pallas kernels, inverses(): pl.pallas_call(inverse_kernel, out_shape=jax.ShapeDtypeStruct((tokens, HD...  4.81 us
    all_to_all x1, starting transfers between devices, exchange(): lax.all_to_all(blocks, 'dp', split_axis=0, concat_axis=0, tiled=True)  4.75 us
  transfers between devices with their start and end apart: 24, of which 6 were waited for; matrix products, arithmetic and copies ran while one was open for 2% of the time, Pallas kernels for 17%

profile of v4, /device:TPU:8, one launch (start us, length us, event | category | flops | bytes accessed | tf_op | source)
XLA Modules:
  0.0 155.2 jit_solution(1306408596626966007)
XLA Ops:
  4.2 4.3 %collective-permute-start.4 = (bf16[512,256]{1,0:T(8,128)(2,1)}, bf16[512,256]{1,0:T(8,128)(2,1)S(1)}, u32[]{:S(2)}, u32[]{:S(2)}) collective-permute-start(bf16[512,256]{1,0:T(8,128)(2,1)} %get-tuple-element.22.refs_2_), channel_id=1, source_target_pairs={{0,2},{1,15},{2,4},{3,1},{4,6},{5,3},{6,8},{7,5},{8,10},{9,7},{10,... | collective-permute-start | bytes 786440 | tf_op jit(solution)/shard_map/ppermute | solution.py:306
  8.5 4.3 %collective-permute-start.3 = (bf16[512,256]{1,0:T(8,128)(2,1)}, bf16[512,256]{1,0:T(8,128)(2,1)S(1)}, u32[]{:S(2)}, u32[]{:S(2)}) collective-permute-start(bf16[512,256]{1,0:T(8,128)(2,1)} %get-tuple-element.21.refs_1_), channel_id=1, source_target_pairs={{0,2},{1,15},{2,4},{3,1},{4,6},{5,3},{6,8},{7,5},{8,10},{9,7},{10,... | collective-permute-start | bytes 786440 | tf_op jit(solution)/shard_map/ppermute | solution.py:306
  12.8 4.3 %collective-permute-start = (bf16[512,256]{1,0:T(8,128)(2,1)}, bf16[512,256]{1,0:T(8,128)(2,1)S(1)}, u32[]{:S(2)}, u32[]{:S(2)}) collective-permute-start(bf16[512,256]{1,0:T(8,128)(2,1)} %get-tuple-element.20.refs_0_), channel_id=1, source_target_pairs={{0,2},{1,15},{2,4},{3,1},{4,6},{5,3},{6,8},{7,5},{8,10},{9,7},{10,... | collective-permute-start | bytes 786440 | tf_op jit(solution)/shard_map/ppermute | solution.py:306
  19.7 2.9 %collective-permute-start.6 = (bf16[512,256]{1,0:T(8,128)(2,1)S(1)}, bf16[512,256]{1,0:T(8,128)(2,1)S(1)}, u32[]{:S(2)}, u32[]{:S(2)}) collective-permute-start(bf16[512,256]{1,0:T(8,128)(2,1)S(1)} %collective-permute-done.4.refs_5_), channel_id=1, source_target_pairs={{0,2},{1,15},{2,4},{3,1},{4,6},{5,3},{6,8},{7,5},{8,10},{9,7},{10,... | collective-permute-start | bytes 786440 | tf_op jit(solution)/shard_map/ppermute | solution.py:306
  22.6 3.4 %collective-permute-start.5 = (bf16[512,256]{1,0:T(8,128)(2,1)S(1)}, bf16[512,256]{1,0:T(8,128)(2,1)S(1)}, u32[]{:S(2)}, u32[]{:S(2)}) collective-permute-start(bf16[512,256]{1,0:T(8,128)(2,1)S(1)} %collective-permute-done.3.refs_4_), channel_id=1, source_target_pairs={{0,2},{1,15},{2,4},{3,1},{4,6},{5,3},{6,8},{7,5},{8,10},{9,7},{10,... | collective-permute-start | bytes 786440 | tf_op jit(solution)/shard_map/ppermute | solution.py:306
  26.0 3.4 %collective-permute-start.1 = (bf16[512,256]{1,0:T(8,128)(2,1)S(1)}, bf16[512,256]{1,0:T(8,128)(2,1)S(1)}, u32[]{:S(2)}, u32[]{:S(2)}) collective-permute-start(bf16[512,256]{1,0:T(8,128)(2,1)S(1)} %collective-permute-done.refs_3_), channel_id=1, source_target_pairs={{0,2},{1,15},{2,4},{3,1},{4,6},{5,3},{6,8},{7,5},{8,10},{9,7},{10,... | collective-permute-start | bytes 786440 | tf_op jit(solution)/shard_map/ppermute | solution.py:306
  29.4 3.4 %collective-permute-start.9 = (bf16[512,256]{1,0:T(8,128)(2,1)S(1)}, bf16[512,256]{1,0:T(8,128)(2,1)S(1)}, u32[]{:S(2)}, u32[]{:S(2)}) collective-permute-start(bf16[512,256]{1,0:T(8,128)(2,1)S(1)} %collective-permute-done.6.refs_8_), channel_id=1, source_target_pairs={{0,2},{1,15},{2,4},{3,1},{4,6},{5,3},{6,8},{7,5},{8,10},{9,7},{10,... | collective-permute-start | bytes 786440 | tf_op jit(solution)/shard_map/ppermute | solution.py:306
  32.8 2.9 %collective-permute-start.11 = (bf16[512,256]{1,0:T(8,128)(2,1)S(1)}, bf16[512,256]{1,0:T(8,128)(2,1)S(1)}, u32[]{:S(2)}, u32[]{:S(2)}) collective-permute-start(bf16[512,256]{1,0:T(8,128)(2,1)S(1)} %collective-permute-done.5.refs_7_), channel_id=1, source_target_pairs={{0,2},{1,15},{2,4},{3,1},{4,6},{5,3},{6,8},{7,5},{8,10},{9,7},{10,... | collective-permute-start | bytes 786440 | tf_op jit(solution)/shard_map/ppermute | solution.py:306
  35.7 3.4 %collective-permute-start.2 = (bf16[512,256]{1,0:T(8,128)(2,1)S(1)}, bf16[512,256]{1,0:T(8,128)(2,1)S(1)}, u32[]{:S(2)}, u32[]{:S(2)}) collective-permute-start(bf16[512,256]{1,0:T(8,128)(2,1)S(1)} %collective-permute-done.1.refs_6_), channel_id=1, source_target_pairs={{0,2},{1,15},{2,4},{3,1},{4,6},{5,3},{6,8},{7,5},{8,10},{9,7},{10,... | collective-permute-start | bytes 786440 | tf_op jit(solution)/shard_map/ppermute | solution.py:306
  40.5 3.2 %collective-permute-start.13 = (bf16[512,256]{1,0:T(8,128)(2,1)S(1)}, bf16[512,256]{1,0:T(8,128)(2,1)S(1)}, u32[]{:S(2)}, u32[]{:S(2)}) collective-permute-start(bf16[512,256]{1,0:T(8,128)(2,1)S(1)} %collective-permute-done.9.refs_2_), channel_id=1, source_target_pairs={{0,2},{1,15},{2,4},{3,1},{4,6},{5,3},{6,8},{7,5},{8,10},{9,7},{10,... | collective-permute-start | bytes 786440 | tf_op jit(solution)/shard_map/ppermute | solution.py:306
  43.7 2.9 %collective-permute-start.12 = (bf16[512,256]{1,0:T(8,128)(2,1)S(1)}, bf16[512,256]{1,0:T(8,128)(2,1)S(1)}, u32[]{:S(2)}, u32[]{:S(2)}) collective-permute-start(bf16[512,256]{1,0:T(8,128)(2,1)S(1)} %collective-permute-done.11.refs_1_), channel_id=1, source_target_pairs={{0,2},{1,15},{2,4},{3,1},{4,6},{5,3},{6,8},{7,5},{8,10},{9,7},{10,... | collective-permute-start | bytes 786440 | tf_op jit(solution)/shard_map/ppermute | solution.py:306
  48.0 5.6 %partial_sums.5 = (f32[256,768]{1,0:T(8,128)}, f32[256,768]{1,0:T(8,128)}) custom-call(bf16[512,256]{1,0:T(8,128)(2,1)} %get-tuple-element.20.refs_0_, bf16[512,256]{1,0:T(8,128)(2,1)} %get-tuple-element.21.refs_1_, bf16[512,256]{1,0:T(8,128)(2,1)} %get-tuple-element.22.refs_2_, bf16[512,256]{1,0:T(8,128)(2,1)} %copy-done.21, bf16[512,256]{1,0:T(8,128)(2,1)} %copy-done.20, ...), custom_call_target="tpu_custom_call" | custom-call | flops 1207959552 | bytes 7077888 | tf_op jit(solution)/shard_map/partial_sums/pallas_call | solution.py:137
  53.6 3.3 %collective-permute-start.8 = (bf16[512,256]{1,0:T(8,128)(2,1)S(1)}, bf16[512,256]{1,0:T(8,128)(2,1)S(1)}, u32[]{:S(2)}, u32[]{:S(2)}) collective-permute-start(bf16[512,256]{1,0:T(8,128)(2,1)S(1)} %collective-permute-done.2.refs_0_), channel_id=1, source_target_pairs={{0,2},{1,15},{2,4},{3,1},{4,6},{5,3},{6,8},{7,5},{8,10},{9,7},{10,... | collective-permute-start | bytes 786440 | tf_op jit(solution)/shard_map/ppermute | solution.py:306
  57.0 4.8 %inverse.1.inverse_ref = f32[256,128]{1,0:T(8,128)} custom-call(bf16[256,8192]{1,0:T(8,128)(2,1)} %refs_3_.1), custom_call_target="tpu_custom_call" | custom-call | flops 1073741824 | bytes 4194304 | tf_op jit(solution)/shard_map/inverse/pallas_call | solution.py:77
  65.5 2.9 %collective-permute-start.17 = (bf16[512,256]{1,0:T(8,128)(2,1)S(1)}, bf16[512,256]{1,0:T(8,128)(2,1)S(1)}, u32[]{:S(2)}, u32[]{:S(2)}) collective-permute-start(bf16[512,256]{1,0:T(8,128)(2,1)S(1)} %collective-permute-done.13.refs_5_), channel_id=1, source_target_pairs={{0,2},{1,15},{2,4},{3,1},{4,6},{5,3},{6,8},{7,5},{8,10},{9,7},{10,... | collective-permute-start | bytes 786440 | tf_op jit(solution)/shard_map/ppermute | solution.py:306
  68.4 3.0 %collective-permute-start.16 = (bf16[512,256]{1,0:T(8,128)(2,1)S(1)}, bf16[512,256]{1,0:T(8,128)(2,1)S(1)}, u32[]{:S(2)}, u32[]{:S(2)}) collective-permute-start(bf16[512,256]{1,0:T(8,128)(2,1)S(1)} %collective-permute-done.12.refs_4_), channel_id=1, source_target_pairs={{0,2},{1,15},{2,4},{3,1},{4,6},{5,3},{6,8},{7,5},{8,10},{9,7},{10,... | collective-permute-start | bytes 786440 | tf_op jit(solution)/shard_map/ppermute | solution.py:306
  71.4 5.2 %partial_sums.6 = (f32[256,768]{1,0:T(8,128)}, f32[256,768]{1,0:T(8,128)}) custom-call(bf16[512,256]{1,0:T(8,128)(2,1)} %copy-done.11, bf16[512,256]{1,0:T(8,128)(2,1)} %copy-done.8, bf16[512,256]{1,0:T(8,128)(2,1)} %copy-done.7, bf16[512,256]{1,0:T(8,128)(2,1)} %copy-done.17, bf16[512,256]{1,0:T(8,128)(2,1)} %copy-done.9, bf16[512,256]{1,0:T(8,128)(2,1)} %copy-done.10, ...), custom_call_target="tpu_custom_call" | custom-call | flops 805306368 | bytes 5767168 | tf_op jit(solution)/shard_map/partial_sums/pallas_call | solution.py:137
  76.7 4.1 %collective-permute-start.14 = (bf16[512,256]{1,0:T(8,128)(2,1)S(1)}, bf16[512,256]{1,0:T(8,128)(2,1)S(1)}, u32[]{:S(2)}, u32[]{:S(2)}) collective-permute-start(bf16[512,256]{1,0:T(8,128)(2,1)S(1)} %collective-permute-done.10.refs_0_), channel_id=1, source_target_pairs={{0,2},{1,15},{2,4},{3,1},{4,6},{5,3},{6,8},{7,5},{8,10},{9,7},{10,... | collective-permute-start | bytes 786440 | tf_op jit(solution)/shard_map/ppermute | solution.py:306
  83.0 3.2 %collective-permute-start.18 = (bf16[512,256]{1,0:T(8,128)(2,1)S(1)}, bf16[512,256]{1,0:T(8,128)(2,1)S(1)}, u32[]{:S(2)}, u32[]{:S(2)}) collective-permute-start(bf16[512,256]{1,0:T(8,128)(2,1)S(1)} %collective-permute-done.16.refs_1_), channel_id=1, source_target_pairs={{0,2},{1,15},{2,4},{3,1},{4,6},{5,3},{6,8},{7,5},{8,10},{9,7},{10,... | collective-permute-start | bytes 786440 | tf_op jit(solution)/shard_map/ppermute | solution.py:306
  86.2 2.9 %collective-permute-start.15 = (bf16[512,256]{1,0:T(8,128)(2,1)S(1)}, bf16[512,256]{1,0:T(8,128)(2,1)S(1)}, u32[]{:S(2)}, u32[]{:S(2)}) collective-permute-start(bf16[512,256]{1,0:T(8,128)(2,1)S(1)} %collective-permute-done.14.refs_3_), channel_id=1, source_target_pairs={{0,2},{1,15},{2,4},{3,1},{4,6},{5,3},{6,8},{7,5},{8,10},{9,7},{10,... | collective-permute-start | bytes 786440 | tf_op jit(solution)/shard_map/ppermute | solution.py:306
  95.6 5.2 %partial_sums.7 = (f32[256,768]{1,0:T(8,128)}, f32[256,768]{1,0:T(8,128)}) custom-call(bf16[512,256]{1,0:T(8,128)(2,1)} %copy-done.12, bf16[512,256]{1,0:T(8,128)(2,1)} %copy-done.14, bf16[512,256]{1,0:T(8,128)(2,1)} %copy-done.13, bf16[512,256]{1,0:T(8,128)(2,1)} %copy-done.15, bf16[512,256]{1,0:T(8,128)(2,1)} %copy-done.18, bf16[512,256]{1,0:T(8,128)(2,1)} %copy-done.16, ...), custom_call_target="tpu_custom_call" | custom-call | flops 805306368 | bytes 5767168 | tf_op jit(solution)/shard_map/partial_sums/pallas_call | solution.py:137
  111.3 23.8 %all_to_all.10 = bf16[32,8,640]{2,1,0:T(8,128)(2,1)} all-to-all(bf16[32,8,640]{2,1,0:T(8,128)(2,1)S(1)} %bitcast.10), channel_id=1, replica_groups=mesh['dp'=32,'fsdp'=16] {'dp'}, dimensions={0} | all-to-all | bytes 655360 | tf_op jit(solution)/shard_map/all_to_all | solution.py:295
  137.2 4.8 %all-to-all-start.1 = ((bf16[32,8,512]{2,1,0:T(8,128)(2,1)}), bf16[32,8,512]{2,1,0:T(8,128)(2,1)S(1)}, u32[]{:S(2)}, u32[]{:S(2)}) async-start(bf16[32,8,512]{2,1,0:T(8,128)(2,1)} %bitcast.13), calls=%async_computation.1 | async-start | bytes 524288 | tf_op jit(solution)/shard_map/all_to_all | solution.py:295
  144.0 9.3 %all-to-all-done.1 = bf16[32,8,512]{2,1,0:T(8,128)(2,1)S(1)} async-done(((bf16[32,8,512]{2,1,0:T(8,128)(2,1)}), bf16[32,8,512]{2,1,0:T(8,128)(2,1)S(1)}, u32[]{:S(2)}, u32[]{:S(2)}) %all-to-all-start.1) | async-done | bytes 262176 | tf_op jit(solution)/shard_map/all_to_all | solution.py:295
  (90 shorter events, 38.3 us)
Async XLA Ops:
  0.0 47.9 %collective-permute-start.7 = (bf16[256,8192]{1,0:T(8,128)(2,1)}, bf16[256,8192]{1,0:T(8,128)(2,1)}, u32[]{:S(2)}, u32[]{:S(2)}) collective-permute-start(bf16[256,8192]{1,0:T(8,128)(2,1)} %refs_3_.1), channel_id=1, source_target_pairs={{0,1},{1,0},{2,3},{3,2},{4,5},{5,4},{6,7},{7,6},{8,9},{9,8},{10,11... | collective-permute-start | bytes 12582920 | tf_op jit(solution)/shard_map/ppermute | solution.py:306
  4.2 15.5 %collective-permute-start.4 = (bf16[512,256]{1,0:T(8,128)(2,1)}, bf16[512,256]{1,0:T(8,128)(2,1)S(1)}, u32[]{:S(2)}, u32[]{:S(2)}) collective-permute-start(bf16[512,256]{1,0:T(8,128)(2,1)} %get-tuple-element.22.refs_2_), channel_id=1, source_target_pairs={{0,2},{1,15},{2,4},{3,1},{4,6},{5,3},{6,8},{7,5},{8,10},{9,7},{10,... | collective-permute-start | bytes 786440 | tf_op jit(solution)/shard_map/ppermute | solution.py:306
  8.5 14.1 %collective-permute-start.3 = (bf16[512,256]{1,0:T(8,128)(2,1)}, bf16[512,256]{1,0:T(8,128)(2,1)S(1)}, u32[]{:S(2)}, u32[]{:S(2)}) collective-permute-start(bf16[512,256]{1,0:T(8,128)(2,1)} %get-tuple-element.21.refs_1_), channel_id=1, source_target_pairs={{0,2},{1,15},{2,4},{3,1},{4,6},{5,3},{6,8},{7,5},{8,10},{9,7},{10,... | collective-permute-start | bytes 786440 | tf_op jit(solution)/shard_map/ppermute | solution.py:306
  12.8 13.2 %collective-permute-start = (bf16[512,256]{1,0:T(8,128)(2,1)}, bf16[512,256]{1,0:T(8,128)(2,1)S(1)}, u32[]{:S(2)}, u32[]{:S(2)}) collective-permute-start(bf16[512,256]{1,0:T(8,128)(2,1)} %get-tuple-element.20.refs_0_), channel_id=1, source_target_pairs={{0,2},{1,15},{2,4},{3,1},{4,6},{5,3},{6,8},{7,5},{8,10},{9,7},{10,... | collective-permute-start | bytes 786440 | tf_op jit(solution)/shard_map/ppermute | solution.py:306
  19.7 9.7 %collective-permute-start.6 = (bf16[512,256]{1,0:T(8,128)(2,1)S(1)}, bf16[512,256]{1,0:T(8,128)(2,1)S(1)}, u32[]{:S(2)}, u32[]{:S(2)}) collective-permute-start(bf16[512,256]{1,0:T(8,128)(2,1)S(1)} %collective-permute-done.4.refs_5_), channel_id=1, source_target_pairs={{0,2},{1,15},{2,4},{3,1},{4,6},{5,3},{6,8},{7,5},{8,10},{9,7},{10,... | collective-permute-start | bytes 786440 | tf_op jit(solution)/shard_map/ppermute | solution.py:306
  22.6 10.2 %collective-permute-start.5 = (bf16[512,256]{1,0:T(8,128)(2,1)S(1)}, bf16[512,256]{1,0:T(8,128)(2,1)S(1)}, u32[]{:S(2)}, u32[]{:S(2)}) collective-permute-start(bf16[512,256]{1,0:T(8,128)(2,1)S(1)} %collective-permute-done.3.refs_4_), channel_id=1, source_target_pairs={{0,2},{1,15},{2,4},{3,1},{4,6},{5,3},{6,8},{7,5},{8,10},{9,7},{10,... | collective-permute-start | bytes 786440 | tf_op jit(solution)/shard_map/ppermute | solution.py:306
  26.0 9.7 %collective-permute-start.1 = (bf16[512,256]{1,0:T(8,128)(2,1)S(1)}, bf16[512,256]{1,0:T(8,128)(2,1)S(1)}, u32[]{:S(2)}, u32[]{:S(2)}) collective-permute-start(bf16[512,256]{1,0:T(8,128)(2,1)S(1)} %collective-permute-done.refs_3_), channel_id=1, source_target_pairs={{0,2},{1,15},{2,4},{3,1},{4,6},{5,3},{6,8},{7,5},{8,10},{9,7},{10,... | collective-permute-start | bytes 786440 | tf_op jit(solution)/shard_map/ppermute | solution.py:306
  29.4 9.7 %collective-permute-start.9 = (bf16[512,256]{1,0:T(8,128)(2,1)S(1)}, bf16[512,256]{1,0:T(8,128)(2,1)S(1)}, u32[]{:S(2)}, u32[]{:S(2)}) collective-permute-start(bf16[512,256]{1,0:T(8,128)(2,1)S(1)} %collective-permute-done.6.refs_8_), channel_id=1, source_target_pairs={{0,2},{1,15},{2,4},{3,1},{4,6},{5,3},{6,8},{7,5},{8,10},{9,7},{10,... | collective-permute-start | bytes 786440 | tf_op jit(solution)/shard_map/ppermute | solution.py:306
  32.8 10.8 %collective-permute-start.11 = (bf16[512,256]{1,0:T(8,128)(2,1)S(1)}, bf16[512,256]{1,0:T(8,128)(2,1)S(1)}, u32[]{:S(2)}, u32[]{:S(2)}) collective-permute-start(bf16[512,256]{1,0:T(8,128)(2,1)S(1)} %collective-permute-done.5.refs_7_), channel_id=1, source_target_pairs={{0,2},{1,15},{2,4},{3,1},{4,6},{5,3},{6,8},{7,5},{8,10},{9,7},{10,... | collective-permute-start | bytes 786440 | tf_op jit(solution)/shard_map/ppermute | solution.py:306
  35.7 17.8 %collective-permute-start.2 = (bf16[512,256]{1,0:T(8,128)(2,1)S(1)}, bf16[512,256]{1,0:T(8,128)(2,1)S(1)}, u32[]{:S(2)}, u32[]{:S(2)}) collective-permute-start(bf16[512,256]{1,0:T(8,128)(2,1)S(1)} %collective-permute-done.1.refs_6_), channel_id=1, source_target_pairs={{0,2},{1,15},{2,4},{3,1},{4,6},{5,3},{6,8},{7,5},{8,10},{9,7},{10,... | collective-permute-start | bytes 786440 | tf_op jit(solution)/shard_map/ppermute | solution.py:306
  40.5 25.0 %collective-permute-start.13 = (bf16[512,256]{1,0:T(8,128)(2,1)S(1)}, bf16[512,256]{1,0:T(8,128)(2,1)S(1)}, u32[]{:S(2)}, u32[]{:S(2)}) collective-permute-start(bf16[512,256]{1,0:T(8,128)(2,1)S(1)} %collective-permute-done.9.refs_2_), channel_id=1, source_target_pairs={{0,2},{1,15},{2,4},{3,1},{4,6},{5,3},{6,8},{7,5},{8,10},{9,7},{10,... | collective-permute-start | bytes 786440 | tf_op jit(solution)/shard_map/ppermute | solution.py:306
  43.7 24.7 %collective-permute-start.12 = (bf16[512,256]{1,0:T(8,128)(2,1)S(1)}, bf16[512,256]{1,0:T(8,128)(2,1)S(1)}, u32[]{:S(2)}, u32[]{:S(2)}) collective-permute-start(bf16[512,256]{1,0:T(8,128)(2,1)S(1)} %collective-permute-done.11.refs_1_), channel_id=1, source_target_pairs={{0,2},{1,15},{2,4},{3,1},{4,6},{5,3},{6,8},{7,5},{8,10},{9,7},{10,... | collective-permute-start | bytes 786440 | tf_op jit(solution)/shard_map/ppermute | solution.py:306
  53.6 9.5 %collective-permute-start.8 = (bf16[512,256]{1,0:T(8,128)(2,1)S(1)}, bf16[512,256]{1,0:T(8,128)(2,1)S(1)}, u32[]{:S(2)}, u32[]{:S(2)}) collective-permute-start(bf16[512,256]{1,0:T(8,128)(2,1)S(1)} %collective-permute-done.2.refs_0_), channel_id=1, source_target_pairs={{0,2},{1,15},{2,4},{3,1},{4,6},{5,3},{6,8},{7,5},{8,10},{9,7},{10,... | collective-permute-start | bytes 786440 | tf_op jit(solution)/shard_map/ppermute | solution.py:306
  63.1 13.6 %collective-permute-start.10 = (bf16[512,256]{1,0:T(8,128)(2,1)S(1)}, bf16[512,256]{1,0:T(8,128)(2,1)S(1)}, u32[]{:S(2)}, u32[]{:S(2)}) collective-permute-start(bf16[512,256]{1,0:T(8,128)(2,1)S(1)} %collective-permute-done.8.refs_3_), channel_id=1, source_target_pairs={{0,2},{1,15},{2,4},{3,1},{4,6},{5,3},{6,8},{7,5},{8,10},{9,7},{10,... | collective-permute-start | bytes 786440 | tf_op jit(solution)/shard_map/ppermute | solution.py:306
  65.5 15.3 %collective-permute-start.17 = (bf16[512,256]{1,0:T(8,128)(2,1)S(1)}, bf16[512,256]{1,0:T(8,128)(2,1)S(1)}, u32[]{:S(2)}, u32[]{:S(2)}) collective-permute-start(bf16[512,256]{1,0:T(8,128)(2,1)S(1)} %collective-permute-done.13.refs_5_), channel_id=1, source_target_pairs={{0,2},{1,15},{2,4},{3,1},{4,6},{5,3},{6,8},{7,5},{8,10},{9,7},{10,... | collective-permute-start | bytes 786440 | tf_op jit(solution)/shard_map/ppermute | solution.py:306
  68.4 14.5 %collective-permute-start.16 = (bf16[512,256]{1,0:T(8,128)(2,1)S(1)}, bf16[512,256]{1,0:T(8,128)(2,1)S(1)}, u32[]{:S(2)}, u32[]{:S(2)}) collective-permute-start(bf16[512,256]{1,0:T(8,128)(2,1)S(1)} %collective-permute-done.12.refs_4_), channel_id=1, source_target_pairs={{0,2},{1,15},{2,4},{3,1},{4,6},{5,3},{6,8},{7,5},{8,10},{9,7},{10,... | collective-permute-start | bytes 786440 | tf_op jit(solution)/shard_map/ppermute | solution.py:306
  76.7 9.5 %collective-permute-start.14 = (bf16[512,256]{1,0:T(8,128)(2,1)S(1)}, bf16[512,256]{1,0:T(8,128)(2,1)S(1)}, u32[]{:S(2)}, u32[]{:S(2)}) collective-permute-start(bf16[512,256]{1,0:T(8,128)(2,1)S(1)} %collective-permute-done.10.refs_0_), channel_id=1, source_target_pairs={{0,2},{1,15},{2,4},{3,1},{4,6},{5,3},{6,8},{7,5},{8,10},{9,7},{10,... | collective-permute-start | bytes 786440 | tf_op jit(solution)/shard_map/ppermute | solution.py:306
  80.8 9.5 %collective-permute-start.19 = (bf16[512,256]{1,0:T(8,128)(2,1)S(1)}, bf16[512,256]{1,0:T(8,128)(2,1)S(1)}, u32[]{:S(2)}, u32[]{:S(2)}) collective-permute-start(bf16[512,256]{1,0:T(8,128)(2,1)S(1)} %collective-permute-done.17.refs_2_), channel_id=1, source_target_pairs={{0,2},{1,15},{2,4},{3,1},{4,6},{5,3},{6,8},{7,5},{8,10},{9,7},{10,... | collective-permute-start | bytes 786440 | tf_op jit(solution)/shard_map/ppermute | solution.py:306
  83.0 10.2 %collective-permute-start.18 = (bf16[512,256]{1,0:T(8,128)(2,1)S(1)}, bf16[512,256]{1,0:T(8,128)(2,1)S(1)}, u32[]{:S(2)}, u32[]{:S(2)}) collective-permute-start(bf16[512,256]{1,0:T(8,128)(2,1)S(1)} %collective-permute-done.16.refs_1_), channel_id=1, source_target_pairs={{0,2},{1,15},{2,4},{3,1},{4,6},{5,3},{6,8},{7,5},{8,10},{9,7},{10,... | collective-permute-start | bytes 786440 | tf_op jit(solution)/shard_map/ppermute | solution.py:306
  86.2 14.7 %collective-permute-start.15 = (bf16[512,256]{1,0:T(8,128)(2,1)S(1)}, bf16[512,256]{1,0:T(8,128)(2,1)S(1)}, u32[]{:S(2)}, u32[]{:S(2)}) collective-permute-start(bf16[512,256]{1,0:T(8,128)(2,1)S(1)} %collective-permute-done.14.refs_3_), channel_id=1, source_target_pairs={{0,2},{1,15},{2,4},{3,1},{4,6},{5,3},{6,8},{7,5},{8,10},{9,7},{10,... | collective-permute-start | bytes 786440 | tf_op jit(solution)/shard_map/ppermute | solution.py:306
  90.3 10.6 %collective-permute-start.21 = (bf16[512,256]{1,0:T(8,128)(2,1)S(1)}, bf16[512,256]{1,0:T(8,128)(2,1)S(1)}, u32[]{:S(2)}, u32[]{:S(2)}) collective-permute-start(bf16[512,256]{1,0:T(8,128)(2,1)S(1)} %collective-permute-done.19.refs_5_), channel_id=1, source_target_pairs={{0,2},{1,15},{2,4},{3,1},{4,6},{5,3},{6,8},{7,5},{8,10},{9,7},{10,... | collective-permute-start | bytes 786440 | tf_op jit(solution)/shard_map/ppermute | solution.py:306
  93.1 9.5 %collective-permute-start.20 = (bf16[512,256]{1,0:T(8,128)(2,1)S(1)}, bf16[512,256]{1,0:T(8,128)(2,1)S(1)}, u32[]{:S(2)}, u32[]{:S(2)}) collective-permute-start(bf16[512,256]{1,0:T(8,128)(2,1)S(1)} %collective-permute-done.18.refs_4_), channel_id=1, source_target_pairs={{0,2},{1,15},{2,4},{3,1},{4,6},{5,3},{6,8},{7,5},{8,10},{9,7},{10,... | collective-permute-start | bytes 786440 | tf_op jit(solution)/shard_map/ppermute | solution.py:306
  105.1 4.3 %collective-permute-start.22 = (f32[256,768]{1,0:T(8,128)S(1)}, f32[256,768]{1,0:T(8,128)S(1)}, u32[]{:S(2)}, u32[]{:S(2)}) collective-permute-start(f32[256,768]{1,0:T(8,128)S(1)} %partial_sums.9), channel_id=1, source_target_pairs={{0,1},{1,0},{2,3},{3,2},{4,5},{5,4},{6,7},{7,6},{8,9},{9,8},{10,11... | collective-permute-start | bytes 2359304 | tf_op jit(solution)/shard_map/ppermute | solution.py:306
  137.2 16.2 %all-to-all-start.1 = ((bf16[32,8,512]{2,1,0:T(8,128)(2,1)}), bf16[32,8,512]{2,1,0:T(8,128)(2,1)S(1)}, u32[]{:S(2)}, u32[]{:S(2)}) async-start(bf16[32,8,512]{2,1,0:T(8,128)(2,1)} %bitcast.13), calls=%async_computation.1 | async-start | bytes 524288 | tf_op jit(solution)/shard_map/all_to_all | solution.py:295
  (25 other events, 275.4 us)

commit v5 on v4

--- a/solution.py
+++ b/solution.py
@@ -12,7 +12,6 @@
 WIDE = (QH + 2) * HD
 PAIR = 128
 TABLE = 128
-PIECE = 256
 
 rope_base = 500000.0
 norm_eps = 1e-05
@@ -26,33 +25,37 @@
 
 
 def fold_kernel(gain_ref, query_ref, keyval_ref, *out_refs):
-    rows = 256
+    rows = out_refs[0].shape[0]
     row = lax.broadcasted_iota(jnp.int32, (rows, rows), 0)
     column = lax.broadcasted_iota(jnp.int32, (rows, rows), 1)
-    for start in range(0, query_ref.shape[0], rows):
-        own = slice(start, start + rows)
+    for i, out_ref in enumerate(out_refs):
+        own = slice(i * rows, (i + 1) * rows)
         gain = gain_ref[own].astype(f32).reshape(1, rows)
         gain = jnp.where(row == column, gain, 0.0).astype(bf16)
-        pieces = [query_ref[own, :PIECE], query_ref[own, PIECE:], keyval_ref[own, :]]
-        for piece, out_ref in zip(pieces, out_refs):
-            out_ref[own, :] = jnp.dot(gain, piece, preferred_element_type=f32).astype(bf16)
+        query = jnp.dot(gain, query_ref[own, :], preferred_element_type=f32)
+        keyval = jnp.dot(gain, keyval_ref[own, :], preferred_element_type=f32)
+        out_ref[:, : QH * HD] = query.astype(bf16)
+        out_ref[:, QH * HD :] = keyval.astype(bf16)
 
 
 def fold(gain, query_weight, keyval_weight):
-    pieces = WIDE // PIECE
+    half = jax.ShapeDtypeStruct((gain.shape[0] // 2, WIDE), bf16)
     return pl.pallas_call(
         fold_kernel,
-        out_shape=[jax.ShapeDtypeStruct((gain.shape[0], PIECE), bf16)] * pieces,
+        out_shape=[half] * 2,
         in_specs=[VMEM] * 3,
-        out_specs=[VMEM] * pieces,
+        out_specs=[VMEM] * 2,
         name="fold_gain",
     )(gain, query_weight, keyval_weight)
 
 
-def inverse_kernel(rows_ref, inverse_ref, products):
+def inverse_kernel(*refs):
+    *rows_refs, inverse_ref, products = refs
     step = pl.program_id(0)
-    rows = rows_ref[...]
-    part = lax.dot_general(rows, rows, (((1,), (1,)), ((), ())), preferred_element_type=f32)
+    part = sum(
+        lax.dot_general(r[...], r[...], (((1,), (1,)), ((), ())), preferred_element_type=f32)
+        for r in rows_refs
+    )
 
     @pl.when(step == 0)
     def _():
@@ -64,7 +67,7 @@
 
     @pl.when(step == pl.num_programs(0) - 1)
     def _():
-        depth = pl.num_programs(0) * rows_ref.shape[1]
+        depth = pl.num_programs(0) * sum(r.shape[1] for r in rows_refs)
         row = lax.broadcasted_iota(jnp.int32, products.shape, 0)
         column = lax.broadcasted_iota(jnp.int32, products.shape, 1)
         squares = jnp.sum(jnp.where(row == column, products[...], 0.0), axis=1, keepdims=True)
@@ -73,12 +76,17 @@
 
 def inverses(rows):
     tokens, depth = rows.shape
-    steps = 4
+    steps, streams = 4, 4
+    block = depth // (steps * streams)
+
+    def part(stream):
+        return pl.BlockSpec((tokens, block), lambda i: (0, stream * steps + i))
+
     return pl.pallas_call(
         inverse_kernel,
         out_shape=jax.ShapeDtypeStruct((tokens, HD), f32),
         grid=(steps,),
-        in_specs=[pl.BlockSpec((tokens, depth // steps), lambda i: (0, i))],
+        in_specs=[part(s) for s in range(streams)],
         out_specs=pl.BlockSpec((tokens, HD), lambda i: (0, 0)),
         scratch_shapes=[pltpu.VMEM((tokens, tokens), f32)],
         compiler_params=pltpu.CompilerParams(vmem_limit_bytes=60 << 20),
@@ -86,64 +94,60 @@
             flops=2 * tokens * tokens * depth, bytes_accessed=2 * tokens * depth, transcendentals=0
         ),
         name="inverse",
-    )(rows)
+    )(*[rows] * streams)
 
 
 def partial_kernel(distances, sides, carried, *refs):
-    pieces = WIDE // PIECE
     count = len(distances)
-    weights, refs = refs[: count * pieces], refs[count * pieces :]
+    halves, refs = refs[: 2 * count], refs[2 * count :]
     rows, refs = refs[:sides], refs[sides:]
     before, refs = refs[: sides * carried], refs[sides * carried :]
-    out_refs, (columns, arrived) = refs[:sides], refs[sides:]
+    out_refs, (columns, weights, arrived) = refs[:sides], refs[sides:]
     depth = columns.shape[2]
     index = lax.axis_index("fsdp")
     place, core = lax.div(index, 2), lax.rem(index, 2)
     ring = lax.axis_size("fsdp") // 2
     copies = []
-    for side in range(sides):
-        for i, distance in enumerate(distances):
-            origin = lax.rem(place + ring + (2 * core - 1) * distance, ring)
-            start = pl.multiple_of((2 * origin + core) * depth, depth)
-            at = side * count + i
-            copies.append(
-                pltpu.make_async_copy(
-                    rows[side].at[:, pl.ds(start, depth)], columns.at[at], arrived.at[at]
-                )
-            )
-            copies[-1].start()
-    for side in range(sides):
-        for copy in copies[side * count : (side + 1) * count]:
-            copy.wait()
-        for piece in range(pieces):
-            own = slice(piece * PIECE, (piece + 1) * PIECE)
-            total = before[side][:, own] if carried else None
-            for i in range(count):
-                part = jnp.dot(
-                    columns[side * count + i],
-                    weights[i * pieces + piece][...],
-                    preferred_element_type=f32,
-                )
-                total = part if total is None else total + part
-            out_refs[side][:, own] = total
+
+    def copy(source, target):
+        copies.append(pltpu.make_async_copy(source, target, arrived.at[len(copies)]))
+        copies[-1].start()
+
+    for i, distance in enumerate(distances):
+        origin = lax.rem(place + (ring + distance), ring)
+        start = pl.multiple_of((2 * origin + core) * depth, depth)
+        for side in range(sides):
+            copy(rows[side].at[:, pl.ds(start, depth)], columns.at[side * count + i])
+        for h in range(2):
+            rest = pl.ds(h * (depth // 2), depth // 2)
+            copy(halves[2 * i + h], weights.at[i, rest, :])
+    for i in range(count):
+        for c in copies[i * (sides + 2) : (i + 1) * (sides + 2)]:
+            c.wait()
+        for side in range(sides):
+            part = jnp.dot(columns[side * count + i], weights[i], preferred_element_type=f32)
+            if i:
+                out_refs[side][...] += part
+            else:
+                out_refs[side][...] = before[side][...] + part if carried else part
 
 
 def partial(blocks, rows, before, vmem):
     count, sides = len(blocks), len(rows)
-    weights = [w for _, pieces in blocks for w in pieces]
-    tokens, depth = rows[0].shape[0], weights[0].shape[0]
+    halves = [w for _, pair in blocks for w in pair]
+    tokens, depth = rows[0].shape[0], 2 * halves[0].shape[0]
     carried = before is not None
     shape = jax.ShapeDtypeStruct((tokens, WIDE), f32)
     return pl.pallas_call(
         functools.partial(partial_kernel, [d for d, _ in blocks], sides, carried),
         out_shape=[shape] * sides,
-        in_specs=[VMEM] * len(weights)
-        + [pl.BlockSpec(memory_space=pltpu.HBM)] * sides
+        in_specs=[pl.BlockSpec(memory_space=pl.ANY)] * (len(halves) + sides)
         + [VMEM] * (sides * carried),
         out_specs=[VMEM] * sides,
         scratch_shapes=[
             pltpu.VMEM((sides * count, tokens, depth), bf16),
-            pltpu.SemaphoreType.DMA((sides * count,)),
+            pltpu.VMEM((count, depth, WIDE), bf16),
+            pltpu.SemaphoreType.DMA((count * (sides + 2),)),
         ],
         compiler_params=pltpu.CompilerParams(vmem_limit_bytes=vmem << 20),
         cost_estimate=pl.CostEstimate(
@@ -152,7 +156,7 @@
             transcendentals=0,
         ),
         name="partial_sums",
-    )(*weights, *rows, *(before or []))
+    )(*halves, *rows, *(before or []))
 
 
 def attend_kernel(
@@ -276,6 +280,7 @@
         out_shape=jax.ShapeDtypeStruct((spread.shape[0], QH * HD), bf16),
         in_specs=[VMEM],
         out_specs=VMEM,
+        compiler_params=pltpu.CompilerParams(vmem_limit_bytes=16 << 20),
         name="arrange",
     )(spread)
 
@@ -286,6 +291,7 @@
         out_shape=jax.ShapeDtypeStruct((spread.shape[0],) * 2, bf16),
         in_specs=[SMEM, VMEM],
         out_specs=VMEM,
+        compiler_params=pltpu.CompilerParams(vmem_limit_bytes=16 << 20),
         name="slots",
     )(lax.axis_index("dp").reshape(1), spread)
 
@@ -299,7 +305,8 @@
     tokens = hidden.shape[0]
     size = lax.axis_size("fsdp")
     ring = size // 2
-    onward = [(i, (i + 2 - 4 * (i % 2)) % size) for i in range(size)]
+    up = [(i, (i + 2) % size) for i in range(size)]
+    down = [(i, (i - 2) % size) for i in range(size)]
     swap = [(i, i ^ 1) for i in range(size)]
 
     def send(values, pairs):
@@ -308,25 +315,25 @@
     def after(value, *others):
         return lax.optimization_barrier((value, *others))[0]
 
-    moving = fold(norm_gain, query_weight, keyval_weight)
-    blocks = [(0, list(moving))]
-    sums = None
+    held = fold(norm_gain, query_weight, keyval_weight)
     got = send(hidden, swap)
-    for step in range(1, ring):
-        moving = [send(w, onward) for w in moving]
-        if step == 3:
-            inverse = inverses(after(hidden, moving[2]))
-            cosine, sine = rotary(after(lengths, moving[2]), tokens)
-        if step in (3, 5, ring - 1):
-            sums = partial(blocks, (hidden, got), sums, 60)
-            blocks = []
-            moving[0] = after(moving[0], *sums)
-        if step == 4:
-            moving[0] = after(moving[0], inverse, cosine, sine)
-        blocks += [(step, list(moving))]
-    [other] = partial(blocks, (got,), sums[1:], 28)
+    above, below = list(held), list(held)
+    blocks = [(0, held)]
+    for step in range(1, ring // 2):
+        above = [send(w, up) for w in above]
+        below = [send(w, down) for w in below]
+        if step == 1:
+            inverse = inverses(after(hidden, above[1]))
+            cosine, sine = rotary(after(lengths, above[1]), tokens)
+        if step == 2:
+            above[0] = after(above[0], inverse, cosine, sine)
+        blocks += [(-step, list(above)), (step, list(below))]
+    far = [send(above[0], up), send(below[1], down)]
+    sums = partial(blocks, (hidden, got), None, 60)
+    far[1] = after(far[1], *sums)
+    [other] = partial([(ring // 2, far)], (got,), sums[1:], 28)
     other = send(other, swap)
-    [mine] = partial(blocks, (hidden,), sums[:1], 28)
+    [mine] = partial([(ring // 2, far)], (hidden,), sums[:1], 28)
     mixed = attend(lengths, learner, slot_offset, mine, other, inverse, cosine, sine)
     spread = exchange(mixed)
     landed = exchange(arrange(spread))

time: 156 us -> 135 us (0.87)
  starting transfers between devices: 75.9 us -> 59.8 us
  Pallas kernels: 30.9 us -> 18.6 us
  waiting for transfers between devices: 17.6 us -> 25.7 us
    ppermute x23 -> x16, starting transfers between devices: 71.1 us -> 55.1 us  [send(): return lax.ppermute(values, 'fsdp', pairs)]
    pallas_call x5 -> x3, Pallas kernels: 17.8 us -> 8.07 us  [partial(): pl.pallas_call(functools.partial(partial_kernel, [d for d, _ in blocks],...]
    ppermute x23 -> x16, waiting for transfers between devices: 8.23 us -> 14.8 us  [send(): return lax.ppermute(values, 'fsdp', pairs)]
    pallas_call x1, Pallas kernels: 2.09 us -> 0.47 us  [slots(): pl.pallas_call(slots_kernel, out_shape=jax.ShapeDtypeStruct((spread.shape...]
    all_to_all x1, waiting for transfers between devices: 9.35 us -> 11 us  [exchange(): lax.all_to_all(blocks, 'dp', split_axis=0, concat_axis=0, tiled=True)]
  transfers between devices with their start and end apart: 24 -> 17, of which waited for: 6 -> 8; matrix products, arithmetic and copies ran while one was open for 2% -> 2% of each run, Pallas kernels for 17% -> 11%
where the time goes in v5:
time: 135 us
  starting transfers between devices  59.8 us (44%)
  waiting for transfers between devices  25.7 us (19%)
  blocking collectives  23.7 us (18%)
  Pallas kernels  18.6 us (14%)
  local copies, waits for them, and re-layouts  3.52 us (3%)
  other arithmetic  1.89 us (1%)
    ppermute x16, starting transfers between devices, send(): return lax.ppermute(values, 'fsdp', pairs)  55.1 us
    all_to_all x1, blocking collectives, exchange(): lax.all_to_all(blocks, 'dp', split_axis=0, concat_axis=0, tiled=True)  23.7 us
    ppermute x16, waiting for transfers between devices, send(): return lax.ppermute(values, 'fsdp', pairs)  14.8 us
    all_to_all x1, waiting for transfers between devices, exchange(): lax.all_to_all(blocks, 'dp', split_axis=0, concat_axis=0, tiled=True)  11 us
    pallas_call x3, Pallas kernels, partial(): pl.pallas_call(functools.partial(partial_kernel, [d for d, _ in blocks],...  8.07 us
    pallas_call x1, Pallas kernels, inverses(): pl.pallas_call(inverse_kernel, out_shape=jax.ShapeDtypeStruct((tokens, HD...  4.79 us
    all_to_all x1, starting transfers between devices, exchange(): lax.all_to_all(blocks, 'dp', split_axis=0, concat_axis=0, tiled=True)  4.75 us
  transfers between devices with their start and end apart: 17, of which 8 were waited for; matrix products, arithmetic and copies ran while one was open for 2% of the time, Pallas kernels for 11%

profile of v5, /device:TPU:8, one launch (start us, length us, event | category | flops | bytes accessed | tf_op | source)
XLA Modules:
  0.0 134.6 jit_solution(6698682213721794717)
XLA Ops:
  0.0 1.9 %collective-permute-start.14 = (bf16[256,8192]{1,0:T(8,128)(2,1)}, bf16[256,8192]{1,0:T(8,128)(2,1)}, u32[]{:S(2)}, u32[]{:S(2)}) collective-permute-start(bf16[256,8192]{1,0:T(8,128)(2,1)} %refs_2_.2), channel_id=1, source_target_pairs={{0,1},{1,0},{2,3},{3,2},{4,5},{5,4},{6,7},{7,6},{8,9},{9,8},{10,11... | collective-permute-start | bytes 12582920 | tf_op jit(solution)/shard_map/ppermute | solution.py:313
  1.9 2.3 %fold_gain.1 = (bf16[256,768]{1,0:T(8,128)(2,1)}, bf16[256,768]{1,0:T(8,128)(2,1)}) custom-call(bf16[512]{0:T(512)(128)(2,1)} %gain_ref.1, bf16[512,512]{1,0:T(8,128)(2,1)} %query_ref.1, bf16[512,256]{1,0:T(8,128)(2,1)} %keyval_ref.1), custom_call_target="tpu_custom_call" | custom-call | tf_op jit(solution)/shard_map/fold_gain/pallas_call | solution.py:43
  4.2 4.3 %collective-permute-start.2 = (bf16[256,768]{1,0:T(8,128)(2,1)}, bf16[256,768]{1,0:T(8,128)(2,1)S(1)}, u32[]{:S(2)}, u32[]{:S(2)}) collective-permute-start(bf16[256,768]{1,0:T(8,128)(2,1)} %get-tuple-element.14.refs_1_), channel_id=1, source_target_pairs={{0,2},{1,3},{2,4},{3,5},{4,6},{5,7},{6,8},{7,9},{8,10},{9,11},{10,... | collective-permute-start | bytes 1179656 | tf_op jit(solution)/shard_map/ppermute | solution.py:313
  8.5 4.3 %collective-permute-start = (bf16[256,768]{1,0:T(8,128)(2,1)}, bf16[256,768]{1,0:T(8,128)(2,1)S(1)}, u32[]{:S(2)}, u32[]{:S(2)}) collective-permute-start(bf16[256,768]{1,0:T(8,128)(2,1)} %get-tuple-element.13.refs_0_), channel_id=1, source_target_pairs={{0,2},{1,3},{2,4},{3,5},{4,6},{5,7},{6,8},{7,9},{8,10},{9,11},{10,... | collective-permute-start | bytes 1179656 | tf_op jit(solution)/shard_map/ppermute | solution.py:313
  12.8 6.2 %collective-permute-start.5 = (bf16[256,768]{1,0:T(8,128)(2,1)}, bf16[256,768]{1,0:T(8,128)(2,1)S(1)}, u32[]{:S(2)}, u32[]{:S(2)}) collective-permute-start(bf16[256,768]{1,0:T(8,128)(2,1)} %get-tuple-element.14.refs_1_), channel_id=1, source_target_pairs={{0,14},{1,15},{2,0},{3,1},{4,2},{5,3},{6,4},{7,5},{8,6},{9,7},{10,... | collective-permute-start | bytes 1179656 | tf_op jit(solution)/shard_map/ppermute | solution.py:313
  19.0 3.9 %collective-permute-start.9 = (bf16[256,768]{1,0:T(8,128)(2,1)}, bf16[256,768]{1,0:T(8,128)(2,1)S(1)}, u32[]{:S(2)}, u32[]{:S(2)}) collective-permute-start(bf16[256,768]{1,0:T(8,128)(2,1)} %get-tuple-element.13.refs_0_), channel_id=1, source_target_pairs={{0,14},{1,15},{2,0},{3,1},{4,2},{5,3},{6,4},{7,5},{8,6},{9,7},{10,... | collective-permute-start | bytes 1179656 | tf_op jit(solution)/shard_map/ppermute | solution.py:313
  23.0 2.4 %collective-permute-done.2.refs_3_ = bf16[256,768]{1,0:T(8,128)(2,1)S(1)} collective-permute-done((bf16[256,768]{1,0:T(8,128)(2,1)}, bf16[256,768]{1,0:T(8,128)(2,1)S(1)}, u32[]{:S(2)}, u32[]{:S(2)}) %collective-permute-start.2) | collective-permute-done | bytes 393248 | tf_op jit(solution)/shard_map/ppermute | solution.py:313
  25.4 1.9 %collective-permute-start.10 = (bf16[256,768]{1,0:T(8,128)(2,1)S(1)}, bf16[256,768]{1,0:T(8,128)(2,1)S(1)}, u32[]{:S(2)}, u32[]{:S(2)}) collective-permute-start(bf16[256,768]{1,0:T(8,128)(2,1)S(1)} %collective-permute-done.2.refs_3_), channel_id=1, source_target_pairs={{0,2},{1,3},{2,4},{3,5},{4,6},{5,7},{6,8},{7,9},{8,10},{9,11},{10,... | collective-permute-start | bytes 1179656 | tf_op jit(solution)/shard_map/ppermute | solution.py:313
  27.3 6.5 %collective-permute-done.refs_2_ = bf16[256,768]{1,0:T(8,128)(2,1)S(1)} collective-permute-done((bf16[256,768]{1,0:T(8,128)(2,1)}, bf16[256,768]{1,0:T(8,128)(2,1)S(1)}, u32[]{:S(2)}, u32[]{:S(2)}) %collective-permute-start) | collective-permute-done | bytes 393248 | tf_op jit(solution)/shard_map/ppermute | solution.py:313
  35.7 5.1 %collective-permute-start.6 = (bf16[256,768]{1,0:T(8,128)(2,1)S(1)}, bf16[256,768]{1,0:T(8,128)(2,1)S(1)}, u32[]{:S(2)}, u32[]{:S(2)}) collective-permute-start(bf16[256,768]{1,0:T(8,128)(2,1)S(1)} %collective-permute-done.5.refs_5_), channel_id=1, source_target_pairs={{0,14},{1,15},{2,0},{3,1},{4,2},{5,3},{6,4},{7,5},{8,6},{9,7},{10,... | collective-permute-start | bytes 1179656 | tf_op jit(solution)/shard_map/ppermute | solution.py:313
  40.9 2.6 %collective-permute-start.11 = (bf16[256,768]{1,0:T(8,128)(2,1)S(1)}, bf16[256,768]{1,0:T(8,128)(2,1)}, u32[]{:S(2)}, u32[]{:S(2)}) collective-permute-start(bf16[256,768]{1,0:T(8,128)(2,1)S(1)} %collective-permute-done.9.refs_4_), channel_id=1, source_target_pairs={{0,14},{1,15},{2,0},{3,1},{4,2},{5,3},{6,4},{7,5},{8,6},{9,7},{10,... | collective-permute-start | bytes 1179656 | tf_op jit(solution)/shard_map/ppermute | solution.py:313
  46.3 4.8 %inverse.1.inverse_ref = f32[256,128]{1,0:T(8,128)} custom-call(bf16[256,8192]{1,0:T(8,128)(2,1)} %refs_2_.2, bf16[256,8192]{1,0:T(8,128)(2,1)} %refs_2_.2, bf16[256,8192]{1,0:T(8,128)(2,1)} %refs_2_.2, bf16[256,8192]{1,0:T(8,128)(2,1)} %refs_2_.2), custom_call_target="tpu_custom_call" | custom-call | flops 1073741824 | bytes 4194304 | tf_op jit(solution)/shard_map/inverse/pallas_call | solution.py:85
  51.7 4.4 %collective-permute-start.7 = (bf16[256,768]{1,0:T(8,128)(2,1)S(1)}, bf16[256,768]{1,0:T(8,128)(2,1)S(1)}, u32[]{:S(2)}, u32[]{:S(2)}) collective-permute-start(bf16[256,768]{1,0:T(8,128)(2,1)S(1)} %collective-permute-done.6.refs_9_), channel_id=1, source_target_pairs={{0,14},{1,15},{2,0},{3,1},{4,2},{5,3},{6,4},{7,5},{8,6},{9,7},{10,... | collective-permute-start | bytes 1179656 | tf_op jit(solution)/shard_map/ppermute | solution.py:313
  56.0 1.9 %collective-permute-start.3 = (bf16[256,768]{1,0:T(8,128)(2,1)S(1)}, bf16[256,768]{1,0:T(8,128)(2,1)S(1)}, u32[]{:S(2)}, u32[]{:S(2)}) collective-permute-start(bf16[256,768]{1,0:T(8,128)(2,1)S(1)} %collective-permute-done.1.refs_6_), channel_id=1, source_target_pairs={{0,2},{1,3},{2,4},{3,5},{4,6},{5,7},{6,8},{7,9},{8,10},{9,11},{10,... | collective-permute-start | bytes 1179656 | tf_op jit(solution)/shard_map/ppermute | solution.py:313
  58.0 2.8 %collective-permute-start.12 = (bf16[256,768]{1,0:T(8,128)(2,1)S(1)}, bf16[256,768]{1,0:T(8,128)(2,1)S(1)}, u32[]{:S(2)}, u32[]{:S(2)}) collective-permute-start(bf16[256,768]{1,0:T(8,128)(2,1)S(1)} %collective-permute-done.10.refs_7_), channel_id=1, source_target_pairs={{0,2},{1,3},{2,4},{3,5},{4,6},{5,7},{6,8},{7,9},{8,10},{9,11},{10,... | collective-permute-start | bytes 1179656 | tf_op jit(solution)/shard_map/ppermute | solution.py:313
  60.8 4.3 %collective-permute-start.13 = (bf16[256,768]{1,0:T(8,128)(2,1)}, bf16[256,768]{1,0:T(8,128)(2,1)S(1)}, u32[]{:S(2)}, u32[]{:S(2)}) collective-permute-start(bf16[256,768]{1,0:T(8,128)(2,1)} %collective-permute-done.11.refs_8_), channel_id=1, source_target_pairs={{0,14},{1,15},{2,0},{3,1},{4,2},{5,3},{6,4},{7,5},{8,6},{9,7},{10,... | collective-permute-start | bytes 1179656 | tf_op jit(solution)/shard_map/ppermute | solution.py:313
  65.1 2.2 %collective-permute-done.7.refs_13_ = bf16[256,768]{1,0:T(8,128)(2,1)S(1)} collective-permute-done((bf16[256,768]{1,0:T(8,128)(2,1)S(1)}, bf16[256,768]{1,0:T(8,128)(2,1)S(1)}, u32[]{:S(2)}, u32[]{:S(2)}) %collective-permute-start.7) | collective-permute-done | bytes 393248 | tf_op jit(solution)/shard_map/ppermute | solution.py:313
  67.3 5.6 %collective-permute-start.8 = (bf16[256,768]{1,0:T(8,128)(2,1)S(1)}, bf16[256,768]{1,0:T(8,128)(2,1)S(1)}, u32[]{:S(2)}, u32[]{:S(2)}) collective-permute-start(bf16[256,768]{1,0:T(8,128)(2,1)S(1)} %collective-permute-done.7.refs_13_), channel_id=1, source_target_pairs={{0,14},{1,15},{2,0},{3,1},{4,2},{5,3},{6,4},{7,5},{8,6},{9,7},{10,... | collective-permute-start | bytes 1179656 | tf_op jit(solution)/shard_map/ppermute | solution.py:313
  72.9 1.9 %collective-permute-start.4 = (bf16[256,768]{1,0:T(8,128)(2,1)S(1)}, bf16[256,768]{1,0:T(8,128)(2,1)S(1)}, u32[]{:S(2)}, u32[]{:S(2)}) collective-permute-start(bf16[256,768]{1,0:T(8,128)(2,1)S(1)} %collective-permute-done.3.refs_10_), channel_id=1, source_target_pairs={{0,2},{1,3},{2,4},{3,5},{4,6},{5,7},{6,8},{7,9},{8,10},{9,11},{10,... | collective-permute-start | bytes 1179656 | tf_op jit(solution)/shard_map/ppermute | solution.py:313
  76.6 5.9 %partial_sums.3 = (f32[256,768]{1,0:T(8,128)}, f32[256,768]{1,0:T(8,128)}) custom-call(bf16[256,768]{1,0:T(8,128)(2,1)} %get-tuple-element.13.refs_0_, bf16[256,768]{1,0:T(8,128)(2,1)} %get-tuple-element.14.refs_1_, bf16[256,768]{1,0:T(8,128)(2,1)} %copy-done.8, bf16[256,768]{1,0:T(8,128)(2,1)} %copy-done.7, bf16[256,768]{1,0:T(8,128)(2,1)} %copy-done.10, ...), custom_call_target="tpu_custom_call" | custom-call | flops 2818572288 | bytes 12320768 | tf_op jit(solution)/shard_map/partial_sums/pallas_call | solution.py:141
  86.5 2.1 %collective-permute-start.15 = (f32[256,768]{1,0:T(8,128)S(1)}, f32[256,768]{1,0:T(8,128)S(1)}, u32[]{:S(2)}, u32[]{:S(2)}) collective-permute-start(f32[256,768]{1,0:T(8,128)S(1)} %partial_sums.5), channel_id=1, source_target_pairs={{0,1},{1,0},{2,3},{3,2},{4,5},{5,4},{6,7},{7,6},{8,9},{9,8},{10,11... | collective-permute-start | bytes 2359304 | tf_op jit(solution)/shard_map/ppermute | solution.py:313
  92.6 23.7 %all_to_all.10 = bf16[32,8,640]{2,1,0:T(8,128)(2,1)S(1)} all-to-all(bf16[32,8,640]{2,1,0:T(8,128)(2,1)S(1)} %bitcast.12), channel_id=1, replica_groups=mesh['dp'=32,'fsdp'=16] {'dp'}, dimensions={0} | all-to-all | bytes 655360 | tf_op jit(solution)/shard_map/all_to_all | solution.py:301
  117.4 4.8 %all-to-all-start.1 = ((bf16[32,8,512]{2,1,0:T(8,128)(2,1)}), bf16[32,8,512]{2,1,0:T(8,128)(2,1)S(1)}, u32[]{:S(2)}, u32[]{:S(2)}) async-start(bf16[32,8,512]{2,1,0:T(8,128)(2,1)} %bitcast.5), calls=%async_computation.1 | async-start | bytes 524288 | tf_op jit(solution)/shard_map/all_to_all | solution.py:301
  122.7 11.0 %all-to-all-done.1 = bf16[32,8,512]{2,1,0:T(8,128)(2,1)S(1)} async-done(((bf16[32,8,512]{2,1,0:T(8,128)(2,1)}), bf16[32,8,512]{2,1,0:T(8,128)(2,1)S(1)}, u32[]{:S(2)}, u32[]{:S(2)}) %all-to-all-start.1) | async-done | bytes 262176 | tf_op jit(solution)/shard_map/all_to_all | solution.py:301
  (60 shorter events, 17.5 us)
Async XLA Ops:
  0.0 75.8 %collective-permute-start.14 = (bf16[256,8192]{1,0:T(8,128)(2,1)}, bf16[256,8192]{1,0:T(8,128)(2,1)}, u32[]{:S(2)}, u32[]{:S(2)}) collective-permute-start(bf16[256,8192]{1,0:T(8,128)(2,1)} %refs_2_.2), channel_id=1, source_target_pairs={{0,1},{1,0},{2,3},{3,2},{4,5},{5,4},{6,7},{7,6},{8,9},{9,8},{10,11... | collective-permute-start | bytes 12582920 | tf_op jit(solution)/shard_map/ppermute | solution.py:313
  4.2 21.1 %collective-permute-start.2 = (bf16[256,768]{1,0:T(8,128)(2,1)}, bf16[256,768]{1,0:T(8,128)(2,1)S(1)}, u32[]{:S(2)}, u32[]{:S(2)}) collective-permute-start(bf16[256,768]{1,0:T(8,128)(2,1)} %get-tuple-element.14.refs_1_), channel_id=1, source_target_pairs={{0,2},{1,3},{2,4},{3,5},{4,6},{5,7},{6,8},{7,9},{8,10},{9,11},{10,... | collective-permute-start | bytes 1179656 | tf_op jit(solution)/shard_map/ppermute | solution.py:313
  8.5 25.3 %collective-permute-start = (bf16[256,768]{1,0:T(8,128)(2,1)}, bf16[256,768]{1,0:T(8,128)(2,1)S(1)}, u32[]{:S(2)}, u32[]{:S(2)}) collective-permute-start(bf16[256,768]{1,0:T(8,128)(2,1)} %get-tuple-element.13.refs_0_), channel_id=1, source_target_pairs={{0,2},{1,3},{2,4},{3,5},{4,6},{5,7},{6,8},{7,9},{8,10},{9,11},{10,... | collective-permute-start | bytes 1179656 | tf_op jit(solution)/shard_map/ppermute | solution.py:313
  12.8 22.9 %collective-permute-start.5 = (bf16[256,768]{1,0:T(8,128)(2,1)}, bf16[256,768]{1,0:T(8,128)(2,1)S(1)}, u32[]{:S(2)}, u32[]{:S(2)}) collective-permute-start(bf16[256,768]{1,0:T(8,128)(2,1)} %get-tuple-element.14.refs_1_), channel_id=1, source_target_pairs={{0,14},{1,15},{2,0},{3,1},{4,2},{5,3},{6,4},{7,5},{8,6},{9,7},{10,... | collective-permute-start | bytes 1179656 | tf_op jit(solution)/shard_map/ppermute | solution.py:313
  19.0 21.8 %collective-permute-start.9 = (bf16[256,768]{1,0:T(8,128)(2,1)}, bf16[256,768]{1,0:T(8,128)(2,1)S(1)}, u32[]{:S(2)}, u32[]{:S(2)}) collective-permute-start(bf16[256,768]{1,0:T(8,128)(2,1)} %get-tuple-element.13.refs_0_), channel_id=1, source_target_pairs={{0,14},{1,15},{2,0},{3,1},{4,2},{5,3},{6,4},{7,5},{8,6},{9,7},{10,... | collective-permute-start | bytes 1179656 | tf_op jit(solution)/shard_map/ppermute | solution.py:313
  25.4 25.7 %copy-start.7 = (bf16[256,768]{1,0:T(8,128)(2,1)}, bf16[256,768]{1,0:T(8,128)(2,1)S(1)}, u32[]{:S(2)}) copy-start(bf16[256,768]{1,0:T(8,128)(2,1)S(1)} %collective-permute-done.2.refs_3_) | copy-start | bytes 1179652
  25.4 32.6 %collective-permute-start.10 = (bf16[256,768]{1,0:T(8,128)(2,1)S(1)}, bf16[256,768]{1,0:T(8,128)(2,1)S(1)}, u32[]{:S(2)}, u32[]{:S(2)}) collective-permute-start(bf16[256,768]{1,0:T(8,128)(2,1)S(1)} %collective-permute-done.2.refs_3_), channel_id=1, source_target_pairs={{0,2},{1,3},{2,4},{3,5},{4,6},{5,7},{6,8},{7,9},{8,10},{9,11},{10,... | collective-permute-start | bytes 1179656 | tf_op jit(solution)/shard_map/ppermute | solution.py:313
  33.8 17.3 %copy-start.8 = (bf16[256,768]{1,0:T(8,128)(2,1)}, bf16[256,768]{1,0:T(8,128)(2,1)S(1)}, u32[]{:S(2)}) copy-start(bf16[256,768]{1,0:T(8,128)(2,1)S(1)} %collective-permute-done.refs_2_) | copy-start | bytes 1179652
  33.8 22.2 %collective-permute-start.1 = (bf16[256,768]{1,0:T(8,128)(2,1)S(1)}, bf16[256,768]{1,0:T(8,128)(2,1)S(1)}, u32[]{:S(2)}, u32[]{:S(2)}) collective-permute-start(bf16[256,768]{1,0:T(8,128)(2,1)S(1)} %collective-permute-done.refs_2_), channel_id=1, source_target_pairs={{0,2},{1,3},{2,4},{3,5},{4,6},{5,7},{6,8},{7,9},{8,10},{9,11},{10,... | collective-permute-start | bytes 1179656 | tf_op jit(solution)/shard_map/ppermute | solution.py:313
  35.7 15.4 %copy-start.9 = (bf16[256,768]{1,0:T(8,128)(2,1)}, bf16[256,768]{1,0:T(8,128)(2,1)S(1)}, u32[]{:S(2)}) copy-start(bf16[256,768]{1,0:T(8,128)(2,1)S(1)} %collective-permute-done.5.refs_5_) | copy-start | bytes 1179652
  35.7 15.9 %collective-permute-start.6 = (bf16[256,768]{1,0:T(8,128)(2,1)S(1)}, bf16[256,768]{1,0:T(8,128)(2,1)S(1)}, u32[]{:S(2)}, u32[]{:S(2)}) collective-permute-start(bf16[256,768]{1,0:T(8,128)(2,1)S(1)} %collective-permute-done.5.refs_5_), channel_id=1, source_target_pairs={{0,14},{1,15},{2,0},{3,1},{4,2},{5,3},{6,4},{7,5},{8,6},{9,7},{10,... | collective-permute-start | bytes 1179656 | tf_op jit(solution)/shard_map/ppermute | solution.py:313
  40.9 10.2 %copy-start.10 = (bf16[256,768]{1,0:T(8,128)(2,1)}, bf16[256,768]{1,0:T(8,128)(2,1)S(1)}, u32[]{:S(2)}) copy-start(bf16[256,768]{1,0:T(8,128)(2,1)S(1)} %collective-permute-done.9.refs_4_) | copy-start | bytes 1179652
  40.9 19.9 %collective-permute-start.11 = (bf16[256,768]{1,0:T(8,128)(2,1)S(1)}, bf16[256,768]{1,0:T(8,128)(2,1)}, u32[]{:S(2)}, u32[]{:S(2)}) collective-permute-start(bf16[256,768]{1,0:T(8,128)(2,1)S(1)} %collective-permute-done.9.refs_4_), channel_id=1, source_target_pairs={{0,14},{1,15},{2,0},{3,1},{4,2},{5,3},{6,4},{7,5},{8,6},{9,7},{10,... | collective-permute-start | bytes 1179656 | tf_op jit(solution)/shard_map/ppermute | solution.py:313
  51.6 24.2 %copy-start.13 = (bf16[256,768]{1,0:T(8,128)(2,1)}, bf16[256,768]{1,0:T(8,128)(2,1)S(1)}, u32[]{:S(2)}) copy-start(bf16[256,768]{1,0:T(8,128)(2,1)S(1)} %collective-permute-done.6.refs_9_) | copy-start | bytes 1179652
  51.7 15.6 %collective-permute-start.7 = (bf16[256,768]{1,0:T(8,128)(2,1)S(1)}, bf16[256,768]{1,0:T(8,128)(2,1)S(1)}, u32[]{:S(2)}, u32[]{:S(2)}) collective-permute-start(bf16[256,768]{1,0:T(8,128)(2,1)S(1)} %collective-permute-done.6.refs_9_), channel_id=1, source_target_pairs={{0,14},{1,15},{2,0},{3,1},{4,2},{5,3},{6,4},{7,5},{8,6},{9,7},{10,... | collective-permute-start | bytes 1179656 | tf_op jit(solution)/shard_map/ppermute | solution.py:313
  56.0 19.8 %copy-start.12 = (bf16[256,768]{1,0:T(8,128)(2,1)}, bf16[256,768]{1,0:T(8,128)(2,1)S(1)}, u32[]{:S(2)}) copy-start(bf16[256,768]{1,0:T(8,128)(2,1)S(1)} %collective-permute-done.1.refs_6_) | copy-start | bytes 1179652
  56.0 16.8 %collective-permute-start.3 = (bf16[256,768]{1,0:T(8,128)(2,1)S(1)}, bf16[256,768]{1,0:T(8,128)(2,1)S(1)}, u32[]{:S(2)}, u32[]{:S(2)}) collective-permute-start(bf16[256,768]{1,0:T(8,128)(2,1)S(1)} %collective-permute-done.1.refs_6_), channel_id=1, source_target_pairs={{0,2},{1,3},{2,4},{3,5},{4,6},{5,7},{6,8},{7,9},{8,10},{9,11},{10,... | collective-permute-start | bytes 1179656 | tf_op jit(solution)/shard_map/ppermute | solution.py:313
  58.0 17.8 %copy-start.11 = (bf16[256,768]{1,0:T(8,128)(2,1)}, bf16[256,768]{1,0:T(8,128)(2,1)S(1)}, u32[]{:S(2)}) copy-start(bf16[256,768]{1,0:T(8,128)(2,1)S(1)} %collective-permute-done.10.refs_7_) | copy-start | bytes 1179652
  58.0 17.3 %collective-permute-start.12 = (bf16[256,768]{1,0:T(8,128)(2,1)S(1)}, bf16[256,768]{1,0:T(8,128)(2,1)S(1)}, u32[]{:S(2)}, u32[]{:S(2)}) collective-permute-start(bf16[256,768]{1,0:T(8,128)(2,1)S(1)} %collective-permute-done.10.refs_7_), channel_id=1, source_target_pairs={{0,2},{1,3},{2,4},{3,5},{4,6},{5,7},{6,8},{7,9},{8,10},{9,11},{10,... | collective-permute-start | bytes 1179656 | tf_op jit(solution)/shard_map/ppermute | solution.py:313
  60.8 15.0 %collective-permute-start.13 = (bf16[256,768]{1,0:T(8,128)(2,1)}, bf16[256,768]{1,0:T(8,128)(2,1)S(1)}, u32[]{:S(2)}, u32[]{:S(2)}) collective-permute-start(bf16[256,768]{1,0:T(8,128)(2,1)} %collective-permute-done.11.refs_8_), channel_id=1, source_target_pairs={{0,14},{1,15},{2,0},{3,1},{4,2},{5,3},{6,4},{7,5},{8,6},{9,7},{10,... | collective-permute-start | bytes 1179656 | tf_op jit(solution)/shard_map/ppermute | solution.py:313
  67.3 15.3 %collective-permute-start.8 = (bf16[256,768]{1,0:T(8,128)(2,1)S(1)}, bf16[256,768]{1,0:T(8,128)(2,1)S(1)}, u32[]{:S(2)}, u32[]{:S(2)}) collective-permute-start(bf16[256,768]{1,0:T(8,128)(2,1)S(1)} %collective-permute-done.7.refs_13_), channel_id=1, source_target_pairs={{0,14},{1,15},{2,0},{3,1},{4,2},{5,3},{6,4},{7,5},{8,6},{9,7},{10,... | collective-permute-start | bytes 1179656 | tf_op jit(solution)/shard_map/ppermute | solution.py:313
  72.9 10.9 %collective-permute-start.4 = (bf16[256,768]{1,0:T(8,128)(2,1)S(1)}, bf16[256,768]{1,0:T(8,128)(2,1)S(1)}, u32[]{:S(2)}, u32[]{:S(2)}) collective-permute-start(bf16[256,768]{1,0:T(8,128)(2,1)S(1)} %collective-permute-done.3.refs_10_), channel_id=1, source_target_pairs={{0,2},{1,3},{2,4},{3,5},{4,6},{5,7},{6,8},{7,9},{8,10},{9,11},{10,... | collective-permute-start | bytes 1179656 | tf_op jit(solution)/shard_map/ppermute | solution.py:313
  86.5 4.3 %collective-permute-start.15 = (f32[256,768]{1,0:T(8,128)S(1)}, f32[256,768]{1,0:T(8,128)S(1)}, u32[]{:S(2)}, u32[]{:S(2)}) collective-permute-start(f32[256,768]{1,0:T(8,128)S(1)} %partial_sums.5), channel_id=1, source_target_pairs={{0,1},{1,0},{2,3},{3,2},{4,5},{5,4},{6,7},{7,6},{8,9},{9,8},{10,11... | collective-permute-start | bytes 2359304 | tf_op jit(solution)/shard_map/ppermute | solution.py:313
  117.4 16.2 %all-to-all-start.1 = ((bf16[32,8,512]{2,1,0:T(8,128)(2,1)}), bf16[32,8,512]{2,1,0:T(8,128)(2,1)S(1)}, u32[]{:S(2)}, u32[]{:S(2)}) async-start(bf16[32,8,512]{2,1,0:T(8,128)(2,1)} %bitcast.5), calls=%async_computation.1 | async-start | bytes 524288 | tf_op jit(solution)/shard_map/all_to_all | solution.py:301
  (11 other events, 44.0 us)

commit v6 on v5

--- a/solution.py
+++ b/solution.py
@@ -2,6 +2,7 @@
 
 import jax
 import jax.numpy as jnp
+import numpy as np
 from jax import lax
 from jax.experimental import pallas as pl
 from jax.experimental.pallas import tpu as pltpu
@@ -50,28 +51,24 @@
 
 
 def inverse_kernel(*refs):
-    *rows_refs, inverse_ref, products = refs
+    *rows_refs, inverse_ref, squares = refs
     step = pl.program_id(0)
-    part = sum(
-        lax.dot_general(r[...], r[...], (((1,), (1,)), ((), ())), preferred_element_type=f32)
-        for r in rows_refs
-    )
 
     @pl.when(step == 0)
     def _():
-        products[...] = part
-
-    @pl.when(step > 0)
-    def _():
-        products[...] += part
+        squares[...] = jnp.zeros_like(squares)
+
+    total = squares[...]
+    for ref in rows_refs:
+        for i in range(ref.shape[1] // HD):
+            total += jnp.square(ref[:, i * HD : (i + 1) * HD].astype(f32))
+    squares[...] = total
 
     @pl.when(step == pl.num_programs(0) - 1)
     def _():
         depth = pl.num_programs(0) * sum(r.shape[1] for r in rows_refs)
-        row = lax.broadcasted_iota(jnp.int32, products.shape, 0)
-        column = lax.broadcasted_iota(jnp.int32, products.shape, 1)
-        squares = jnp.sum(jnp.where(row == column, products[...], 0.0), axis=1, keepdims=True)
-        inverse_ref[...] = jnp.broadcast_to(lax.rsqrt(squares / depth + norm_eps), inverse_ref.shape)
+        mean = jnp.sum(squares[...], axis=1, keepdims=True) / depth
+        inverse_ref[...] = jnp.broadcast_to(lax.rsqrt(mean + norm_eps), inverse_ref.shape)
 
 
 def inverses(rows):
@@ -88,10 +85,10 @@
         grid=(steps,),
         in_specs=[part(s) for s in range(streams)],
         out_specs=pl.BlockSpec((tokens, HD), lambda i: (0, 0)),
-        scratch_shapes=[pltpu.VMEM((tokens, tokens), f32)],
+        scratch_shapes=[pltpu.VMEM((tokens, HD), f32)],
         compiler_params=pltpu.CompilerParams(vmem_limit_bytes=60 << 20),
         cost_estimate=pl.CostEstimate(
-            flops=2 * tokens * tokens * depth, bytes_accessed=2 * tokens * depth, transcendentals=0
+            flops=2 * tokens * depth, bytes_accessed=2 * tokens * depth, transcendentals=0
         ),
         name="inverse",
     )(*[rows] * streams)
@@ -113,6 +110,8 @@
         copies.append(pltpu.make_async_copy(source, target, arrived.at[len(copies)]))
         copies[-1].start()
 
+    for source, out_ref in zip(before, out_refs):
+        copy(source, out_ref)
     for i, distance in enumerate(distances):
         origin = lax.rem(place + (ring + distance), ring)
         start = pl.multiple_of((2 * origin + core) * depth, depth)
@@ -122,14 +121,15 @@
             rest = pl.ds(h * (depth // 2), depth // 2)
             copy(halves[2 * i + h], weights.at[i, rest, :])
     for i in range(count):
-        for c in copies[i * (sides + 2) : (i + 1) * (sides + 2)]:
+        known = len(before) + (i + 1) * (sides + 2)
+        for c in copies[0 if i == 0 else known - sides - 2 : known]:
             c.wait()
         for side in range(sides):
             part = jnp.dot(columns[side * count + i], weights[i], preferred_element_type=f32)
-            if i:
+            if i or carried:
                 out_refs[side][...] += part
             else:
-                out_refs[side][...] = before[side][...] + part if carried else part
+                out_refs[side][...] = part
 
 
 def partial(blocks, rows, before, vmem):
@@ -141,13 +141,12 @@
     return pl.pallas_call(
         functools.partial(partial_kernel, [d for d, _ in blocks], sides, carried),
         out_shape=[shape] * sides,
-        in_specs=[pl.BlockSpec(memory_space=pl.ANY)] * (len(halves) + sides)
-        + [VMEM] * (sides * carried),
+        in_specs=[pl.BlockSpec(memory_space=pl.ANY)] * (len(halves) + sides + sides * carried),
         out_specs=[VMEM] * sides,
         scratch_shapes=[
             pltpu.VMEM((sides * count, tokens, depth), bf16),
             pltpu.VMEM((count, depth, WIDE), bf16),
-            pltpu.SemaphoreType.DMA((count * (sides + 2),)),
+            pltpu.SemaphoreType.DMA((count * (sides + 2) + sides * carried,)),
         ],
         compiler_params=pltpu.CompilerParams(vmem_limit_bytes=vmem << 20),
         cost_estimate=pl.CostEstimate(
@@ -164,7 +163,15 @@
 ):
     tokens = out_ref.shape[0]
     inverse = inverse_ref[...]
-    cosine, sine = cosine_ref[...] * inverse, sine_ref[...] * inverse
+
+    def by_position(table_ref):
+        table = table_ref[...]
+        place = lax.broadcasted_iota(jnp.int32, table.shape, 0)
+        leads = [lengths_ref[2 * k] for k in range(tokens // PAIR)]
+        pairs = [jnp.where(place < n, table, pltpu.roll(table, n, 0)) for n in leads]
+        return jnp.concatenate(pairs, axis=0) * inverse
+
+    cosine, sine = by_position(cosine_ref), by_position(sine_ref)
 
     def product(head):
         own = slice(head * HD, (head + 1) * HD)
@@ -221,16 +228,12 @@
     )(lengths, learner, slot_offset, mine, other, inverse, cosine, sine)
 
 
-def rotary(lengths, tokens):
-    slot = jnp.arange(tokens, dtype=jnp.int32)
-    place = slot % PAIR
-    lead = sum(jnp.where(slot // PAIR == k, lengths[2 * k], 0) for k in range(tokens // PAIR))
-    position = jnp.where(place < lead, place, place - lead)
-    lane = jnp.arange(HD, dtype=jnp.int32)
-    frequency = rope_base ** (-(lane % (HD // 2)).astype(f32) * 2.0 / HD)
-    angles = position.astype(f32)[:, None] * frequency[None, :]
-    sign = jnp.where(lane < HD // 2, -1.0, 1.0)
-    return jnp.cos(angles), jnp.sin(angles) * sign
+def rotary():
+    lane = np.arange(HD)
+    frequency = rope_base ** (-(lane % (HD // 2)) * 2.0 / HD)
+    angles = np.arange(PAIR)[:, None] * frequency[None, :]
+    sine = np.where(lane < HD // 2, -1.0, 1.0) * np.sin(angles)
+    return np.cos(angles).astype(np.float32), sine.astype(np.float32)
 
 
 def ranks(spread_ref):
@@ -317,24 +320,22 @@
 
     held = fold(norm_gain, query_weight, keyval_weight)
     got = send(hidden, swap)
+    inverse = inverses(after(hidden, held[0]))
     above, below = list(held), list(held)
     blocks = [(0, held)]
     for step in range(1, ring // 2):
         above = [send(w, up) for w in above]
         below = [send(w, down) for w in below]
         if step == 1:
-            inverse = inverses(after(hidden, above[1]))
-            cosine, sine = rotary(after(lengths, above[1]), tokens)
-        if step == 2:
-            above[0] = after(above[0], inverse, cosine, sine)
+            above[0] = after(above[0], inverse)
         blocks += [(-step, list(above)), (step, list(below))]
     far = [send(above[0], up), send(below[1], down)]
-    sums = partial(blocks, (hidden, got), None, 60)
+    sums = partial(blocks, (hidden, got), None, 28)
     far[1] = after(far[1], *sums)
     [other] = partial([(ring // 2, far)], (got,), sums[1:], 28)
     other = send(other, swap)
     [mine] = partial([(ring // 2, far)], (hidden,), sums[:1], 28)
-    mixed = attend(lengths, learner, slot_offset, mine, other, inverse, cosine, sine)
+    mixed = attend(lengths, learner, slot_offset, mine, other, inverse, *rotary())
     spread = exchange(mixed)
     landed = exchange(arrange(spread))
     return jnp.dot(slots(spread), landed, preferred_element_type=f32).astype(bf16)

time: 135 us -> 133 us (0.985)
  starting transfers between devices: 59.8 us -> 65.3 us
  waiting for transfers between devices: 25.7 us -> 21.2 us
  other arithmetic: 1.89 us -> 0 us
    ppermute x16, starting transfers between devices: 55.1 us -> 60.6 us  [send(): return lax.ppermute(values, 'fsdp', pairs)]
    ppermute x16, waiting for transfers between devices: 14.8 us -> 10.3 us  [send(): return lax.ppermute(values, 'fsdp', pairs)]
    slice x1 -> x0, local copies, waits for them, and re-layouts: 1.39 us -> none  [rotary(): lengths[2 * k]]
  transfers between devices with their start and end apart: 17 -> 17, of which waited for: 8 -> 7; matrix products, arithmetic and copies ran while one was open for 2% -> 0% of each run, Pallas kernels for 11% -> 11%
where the time goes in v6:
time: 133 us; the launch traced here: 132 us
  starting transfers between devices  65.3 us (49%)
  blocking collectives  23.7 us (18%)
  waiting for transfers between devices  21.2 us (16%)
  Pallas kernels  18.7 us (14%)
  local copies, waits for them, and re-layouts  2.24 us (2%)
    ppermute x16, starting transfers between devices, send(): return lax.ppermute(values, 'fsdp', pairs)  60.6 us
    all_to_all x1, blocking collectives, exchange(): lax.all_to_all(blocks, 'dp', split_axis=0, concat_axis=0, tiled=True)  23.7 us
    all_to_all x1, waiting for transfers between devices, exchange(): lax.all_to_all(blocks, 'dp', split_axis=0, concat_axis=0, tiled=True)  11 us
    ppermute x16, waiting for transfers between devices, send(): return lax.ppermute(values, 'fsdp', pairs)  10.3 us
    pallas_call x3, Pallas kernels, partial(): pl.pallas_call(functools.partial(partial_kernel, [d for d, _ in blocks],...  9.02 us
    all_to_all x1, starting transfers between devices, exchange(): lax.all_to_all(blocks, 'dp', split_axis=0, concat_axis=0, tiled=True)  4.75 us
    pallas_call x1, Pallas kernels, inverses(): pl.pallas_call(inverse_kernel, out_shape=jax.ShapeDtypeStruct((tokens, HD...  4.02 us
  transfers between devices with their start and end apart: 17, of which 7 were waited for; matrix products, arithmetic and copies ran while one was open for 0% of the time, Pallas kernels for 11%

profile of v6, /device:TPU:8, one launch (start us, length us, event | category | flops | bytes accessed | tf_op | source)
XLA Modules:
  0.0 132.5 jit_solution(14728614401935304771)
XLA Ops:
  0.0 1.9 %collective-permute-start.14 = (bf16[256,8192]{1,0:T(8,128)(2,1)}, bf16[256,8192]{1,0:T(8,128)(2,1)}, u32[]{:S(2)}, u32[]{:S(2)}) collective-permute-start(bf16[256,8192]{1,0:T(8,128)(2,1)} %refs_2_.2), channel_id=1, source_target_pairs={{0,1},{1,0},{2,3},{3,2},{4,5},{5,4},{6,7},{7,6},{8,9},{9,8},{10,11... | collective-permute-start | bytes 12582920 | tf_op jit(solution)/shard_map/ppermute | solution.py:316
  1.9 2.3 %fold_gain.1 = (bf16[256,768]{1,0:T(8,128)(2,1)}, bf16[256,768]{1,0:T(8,128)(2,1)}) custom-call(bf16[512]{0:T(512)(128)(2,1)} %gain_ref.1, bf16[512,512]{1,0:T(8,128)(2,1)} %query_ref.1, bf16[512,256]{1,0:T(8,128)(2,1)} %keyval_ref.1), custom_call_target="tpu_custom_call" | custom-call | tf_op jit(solution)/shard_map/fold_gain/pallas_call | solution.py:44
  4.2 10.9 %collective-permute-start.4 = (bf16[256,768]{1,0:T(8,128)(2,1)}, bf16[256,768]{1,0:T(8,128)(2,1)S(1)}, u32[]{:S(2)}, u32[]{:S(2)}) collective-permute-start(bf16[256,768]{1,0:T(8,128)(2,1)} %get-tuple-element.15.refs_1_), channel_id=1, source_target_pairs={{0,14},{1,15},{2,0},{3,1},{4,2},{5,3},{6,4},{7,5},{8,6},{9,7},{10,... | collective-permute-start | bytes 1179656 | tf_op jit(solution)/shard_map/ppermute | solution.py:316
  15.2 2.1 %collective-permute-start = (bf16[256,768]{1,0:T(8,128)(2,1)}, bf16[256,768]{1,0:T(8,128)(2,1)S(1)}, u32[]{:S(2)}, u32[]{:S(2)}) collective-permute-start(bf16[256,768]{1,0:T(8,128)(2,1)} %get-tuple-element.12.refs_0_), channel_id=1, source_target_pairs={{0,2},{1,3},{2,4},{3,5},{4,6},{5,7},{6,8},{7,9},{8,10},{9,11},{10,... | collective-permute-start | bytes 1179656 | tf_op jit(solution)/shard_map/ppermute | solution.py:316
  17.3 5.1 %collective-permute-start.9 = (bf16[256,768]{1,0:T(8,128)(2,1)}, bf16[256,768]{1,0:T(8,128)(2,1)S(1)}, u32[]{:S(2)}, u32[]{:S(2)}) collective-permute-start(bf16[256,768]{1,0:T(8,128)(2,1)} %get-tuple-element.12.refs_0_), channel_id=1, source_target_pairs={{0,14},{1,15},{2,0},{3,1},{4,2},{5,3},{6,4},{7,5},{8,6},{9,7},{10,... | collective-permute-start | bytes 1179656 | tf_op jit(solution)/shard_map/ppermute | solution.py:316
  22.4 1.9 %collective-permute-start.8 = (bf16[256,768]{1,0:T(8,128)(2,1)}, bf16[256,768]{1,0:T(8,128)(2,1)S(1)}, u32[]{:S(2)}, u32[]{:S(2)}) collective-permute-start(bf16[256,768]{1,0:T(8,128)(2,1)} %get-tuple-element.15.refs_1_), channel_id=1, source_target_pairs={{0,2},{1,3},{2,4},{3,5},{4,6},{5,7},{6,8},{7,9},{8,10},{9,11},{10,... | collective-permute-start | bytes 1179656 | tf_op jit(solution)/shard_map/ppermute | solution.py:316
  24.3 4.0 %inverse.1.inverse_ref = f32[256,128]{1,0:T(8,128)} custom-call(bf16[256,8192]{1,0:T(8,128)(2,1)} %refs_2_.2, bf16[256,8192]{1,0:T(8,128)(2,1)} %refs_2_.2, bf16[256,8192]{1,0:T(8,128)(2,1)} %refs_2_.2, bf16[256,8192]{1,0:T(8,128)(2,1)} %refs_2_.2), custom_call_target="tpu_custom_call" | custom-call | flops 4194304 | bytes 4194304 | tf_op jit(solution)/shard_map/inverse/pallas_call | solution.py:82
  28.3 5.1 %collective-permute-start.5 = (bf16[256,768]{1,0:T(8,128)(2,1)S(1)}, bf16[256,768]{1,0:T(8,128)(2,1)S(1)}, u32[]{:S(2)}, u32[]{:S(2)}) collective-permute-start(bf16[256,768]{1,0:T(8,128)(2,1)S(1)} %collective-permute-done.4.refs_5_), channel_id=1, source_target_pairs={{0,14},{1,15},{2,0},{3,1},{4,2},{5,3},{6,4},{7,5},{8,6},{9,7},{10,... | collective-permute-start | bytes 1179656 | tf_op jit(solution)/shard_map/ppermute | solution.py:316
  33.5 1.9 %collective-permute-start.1 = (bf16[256,768]{1,0:T(8,128)(2,1)S(1)}, bf16[256,768]{1,0:T(8,128)(2,1)S(1)}, u32[]{:S(2)}, u32[]{:S(2)}) collective-permute-start(bf16[256,768]{1,0:T(8,128)(2,1)S(1)} %collective-permute-done.refs_2_), channel_id=1, source_target_pairs={{0,2},{1,3},{2,4},{3,5},{4,6},{5,7},{6,8},{7,9},{8,10},{9,11},{10,... | collective-permute-start | bytes 1179656 | tf_op jit(solution)/shard_map/ppermute | solution.py:316
  35.4 5.1 %collective-permute-start.11 = (bf16[256,768]{1,0:T(8,128)(2,1)S(1)}, bf16[256,768]{1,0:T(8,128)(2,1)S(1)}, u32[]{:S(2)}, u32[]{:S(2)}) collective-permute-start(bf16[256,768]{1,0:T(8,128)(2,1)S(1)} %collective-permute-done.9.refs_4_), channel_id=1, source_target_pairs={{0,14},{1,15},{2,0},{3,1},{4,2},{5,3},{6,4},{7,5},{8,6},{9,7},{10,... | collective-permute-start | bytes 1179656 | tf_op jit(solution)/shard_map/ppermute | solution.py:316
  40.6 1.9 %collective-permute-start.10 = (bf16[256,768]{1,0:T(8,128)(2,1)S(1)}, bf16[256,768]{1,0:T(8,128)(2,1)S(1)}, u32[]{:S(2)}, u32[]{:S(2)}) collective-permute-start(bf16[256,768]{1,0:T(8,128)(2,1)S(1)} %collective-permute-done.8.refs_3_), channel_id=1, source_target_pairs={{0,2},{1,3},{2,4},{3,5},{4,6},{5,7},{6,8},{7,9},{8,10},{9,11},{10,... | collective-permute-start | bytes 1179656 | tf_op jit(solution)/shard_map/ppermute | solution.py:316
  43.0 5.6 %collective-permute-start.6 = (bf16[256,768]{1,0:T(8,128)(2,1)S(1)}, bf16[256,768]{1,0:T(8,128)(2,1)S(1)}, u32[]{:S(2)}, u32[]{:S(2)}) collective-permute-start(bf16[256,768]{1,0:T(8,128)(2,1)S(1)} %collective-permute-done.5.refs_9_), channel_id=1, source_target_pairs={{0,14},{1,15},{2,0},{3,1},{4,2},{5,3},{6,4},{7,5},{8,6},{9,7},{10,... | collective-permute-start | bytes 1179656 | tf_op jit(solution)/shard_map/ppermute | solution.py:316
  48.6 1.9 %collective-permute-start.2 = (bf16[256,768]{1,0:T(8,128)(2,1)S(1)}, bf16[256,768]{1,0:T(8,128)(2,1)S(1)}, u32[]{:S(2)}, u32[]{:S(2)}) collective-permute-start(bf16[256,768]{1,0:T(8,128)(2,1)S(1)} %collective-permute-done.1.refs_6_), channel_id=1, source_target_pairs={{0,2},{1,3},{2,4},{3,5},{4,6},{5,7},{6,8},{7,9},{8,10},{9,11},{10,... | collective-permute-start | bytes 1179656 | tf_op jit(solution)/shard_map/ppermute | solution.py:316
  51.5 5.6 %collective-permute-start.13 = (bf16[256,768]{1,0:T(8,128)(2,1)S(1)}, bf16[256,768]{1,0:T(8,128)(2,1)S(1)}, u32[]{:S(2)}, u32[]{:S(2)}) collective-permute-start(bf16[256,768]{1,0:T(8,128)(2,1)S(1)} %collective-permute-done.11.refs_8_), channel_id=1, source_target_pairs={{0,14},{1,15},{2,0},{3,1},{4,2},{5,3},{6,4},{7,5},{8,6},{9,7},{10,... | collective-permute-start | bytes 1179656 | tf_op jit(solution)/shard_map/ppermute | solution.py:316
  57.1 1.9 %collective-permute-start.12 = (bf16[256,768]{1,0:T(8,128)(2,1)S(1)}, bf16[256,768]{1,0:T(8,128)(2,1)S(1)}, u32[]{:S(2)}, u32[]{:S(2)}) collective-permute-start(bf16[256,768]{1,0:T(8,128)(2,1)S(1)} %collective-permute-done.10.refs_7_), channel_id=1, source_target_pairs={{0,2},{1,3},{2,4},{3,5},{4,6},{5,7},{6,8},{7,9},{8,10},{9,11},{10,... | collective-permute-start | bytes 1179656 | tf_op jit(solution)/shard_map/ppermute | solution.py:316
  59.9 5.6 %collective-permute-start.7 = (bf16[256,768]{1,0:T(8,128)(2,1)S(1)}, bf16[256,768]{1,0:T(8,128)(2,1)S(1)}, u32[]{:S(2)}, u32[]{:S(2)}) collective-permute-start(bf16[256,768]{1,0:T(8,128)(2,1)S(1)} %collective-permute-done.6.refs_13_), channel_id=1, source_target_pairs={{0,14},{1,15},{2,0},{3,1},{4,2},{5,3},{6,4},{7,5},{8,6},{9,7},{10,... | collective-permute-start | bytes 1179656 | tf_op jit(solution)/shard_map/ppermute | solution.py:316
  65.5 1.9 %collective-permute-start.3 = (bf16[256,768]{1,0:T(8,128)(2,1)S(1)}, bf16[256,768]{1,0:T(8,128)(2,1)S(1)}, u32[]{:S(2)}, u32[]{:S(2)}) collective-permute-start(bf16[256,768]{1,0:T(8,128)(2,1)S(1)} %collective-permute-done.2.refs_10_), channel_id=1, source_target_pairs={{0,2},{1,3},{2,4},{3,5},{4,6},{5,7},{6,8},{7,9},{8,10},{9,11},{10,... | collective-permute-start | bytes 1179656 | tf_op jit(solution)/shard_map/ppermute | solution.py:316
  68.3 5.6 %collective-permute-done.12.refs_11_ = bf16[256,768]{1,0:T(8,128)(2,1)S(1)} collective-permute-done((bf16[256,768]{1,0:T(8,128)(2,1)S(1)}, bf16[256,768]{1,0:T(8,128)(2,1)S(1)}, u32[]{:S(2)}, u32[]{:S(2)}) %collective-permute-start.12) | collective-permute-done | bytes 393248 | tf_op jit(solution)/shard_map/ppermute | solution.py:316
  74.0 2.2 %copy-done = bf16[256,8192]{1,0:T(8,128)(2,1)S(1)} copy-done((bf16[256,8192]{1,0:T(8,128)(2,1)S(1)}, bf16[256,8192]{1,0:T(8,128)(2,1)}, u32[]{:S(2)}) %copy-start) | copy-done | bytes 4194328
  76.1 6.6 %partial_sums.3 = (f32[256,768]{1,0:T(8,128)S(1)}, f32[256,768]{1,0:T(8,128)S(1)}) custom-call(bf16[256,768]{1,0:T(8,128)(2,1)S(1)} %copy-done.3, bf16[256,768]{1,0:T(8,128)(2,1)S(1)} %copy-done.4, bf16[256,768]{1,0:T(8,128)(2,1)S(1)} %collective-permute-done.refs_2_, bf16[256,768]{1,0:T(8,128)(2,1)S(1)} %collective-permute-done.8.refs_3_, ...), custom_call_target="tpu_custom_call" | custom-call | flops 2818572288 | bytes 12320768 | tf_op jit(solution)/shard_map/partial_sums/pallas_call | solution.py:141
  84.4 2.1 %collective-permute-start.15 = (f32[256,768]{1,0:T(8,128)S(1)}, f32[256,768]{1,0:T(8,128)S(1)}, u32[]{:S(2)}, u32[]{:S(2)}) collective-permute-start(f32[256,768]{1,0:T(8,128)S(1)} %partial_sums.5), channel_id=1, source_target_pairs={{0,1},{1,0},{2,3},{3,2},{4,5},{5,4},{6,7},{7,6},{8,9},{9,8},{10,11... | collective-permute-start | bytes 2359304 | tf_op jit(solution)/shard_map/ppermute | solution.py:316
  90.5 23.7 %all_to_all.10 = bf16[32,8,640]{2,1,0:T(8,128)(2,1)S(1)} all-to-all(bf16[32,8,640]{2,1,0:T(8,128)(2,1)S(1)} %bitcast.10), channel_id=1, replica_groups=mesh['dp'=32,'fsdp'=16] {'dp'}, dimensions={0} | all-to-all | bytes 655360 | tf_op jit(solution)/shard_map/all_to_all | solution.py:304
  115.3 4.8 %all-to-all-start.1 = ((bf16[32,8,512]{2,1,0:T(8,128)(2,1)}), bf16[32,8,512]{2,1,0:T(8,128)(2,1)S(1)}, u32[]{:S(2)}, u32[]{:S(2)}) async-start(bf16[32,8,512]{2,1,0:T(8,128)(2,1)} %bitcast.3), calls=%async_computation.1 | async-start | bytes 524288 | tf_op jit(solution)/shard_map/all_to_all | solution.py:304
  120.6 11.0 %all-to-all-done.1 = bf16[32,8,512]{2,1,0:T(8,128)(2,1)S(1)} async-done(((bf16[32,8,512]{2,1,0:T(8,128)(2,1)}), bf16[32,8,512]{2,1,0:T(8,128)(2,1)S(1)}, u32[]{:S(2)}, u32[]{:S(2)}) %all-to-all-start.1) | async-done | bytes 262176 | tf_op jit(solution)/shard_map/all_to_all | solution.py:304
  (40 shorter events, 11.5 us)
Async XLA Ops:
  0.0 73.9 %collective-permute-start.14 = (bf16[256,8192]{1,0:T(8,128)(2,1)}, bf16[256,8192]{1,0:T(8,128)(2,1)}, u32[]{:S(2)}, u32[]{:S(2)}) collective-permute-start(bf16[256,8192]{1,0:T(8,128)(2,1)} %refs_2_.2), channel_id=1, source_target_pairs={{0,1},{1,0},{2,3},{3,2},{4,5},{5,4},{6,7},{7,6},{8,9},{9,8},{10,11... | collective-permute-start | bytes 12582920 | tf_op jit(solution)/shard_map/ppermute | solution.py:316
  4.2 24.1 %collective-permute-start.4 = (bf16[256,768]{1,0:T(8,128)(2,1)}, bf16[256,768]{1,0:T(8,128)(2,1)S(1)}, u32[]{:S(2)}, u32[]{:S(2)}) collective-permute-start(bf16[256,768]{1,0:T(8,128)(2,1)} %get-tuple-element.15.refs_1_), channel_id=1, source_target_pairs={{0,14},{1,15},{2,0},{3,1},{4,2},{5,3},{6,4},{7,5},{8,6},{9,7},{10,... | collective-permute-start | bytes 1179656 | tf_op jit(solution)/shard_map/ppermute | solution.py:316
  15.2 58.8 %copy-start.3 = (bf16[256,768]{1,0:T(8,128)(2,1)S(1)}, bf16[256,768]{1,0:T(8,128)(2,1)}, u32[]{:S(2)}) copy-start(bf16[256,768]{1,0:T(8,128)(2,1)} %get-tuple-element.12.refs_0_) | copy-start | bytes 1179652
  15.2 58.7 %copy-start.4 = (bf16[256,768]{1,0:T(8,128)(2,1)S(1)}, bf16[256,768]{1,0:T(8,128)(2,1)}, u32[]{:S(2)}) copy-start(bf16[256,768]{1,0:T(8,128)(2,1)} %get-tuple-element.15.refs_1_) | copy-start | bytes 1179652
  15.2 18.3 %collective-permute-start = (bf16[256,768]{1,0:T(8,128)(2,1)}, bf16[256,768]{1,0:T(8,128)(2,1)S(1)}, u32[]{:S(2)}, u32[]{:S(2)}) collective-permute-start(bf16[256,768]{1,0:T(8,128)(2,1)} %get-tuple-element.12.refs_0_), channel_id=1, source_target_pairs={{0,2},{1,3},{2,4},{3,5},{4,6},{5,7},{6,8},{7,9},{8,10},{9,11},{10,... | collective-permute-start | bytes 1179656 | tf_op jit(solution)/shard_map/ppermute | solution.py:316
  17.3 18.2 %collective-permute-start.9 = (bf16[256,768]{1,0:T(8,128)(2,1)}, bf16[256,768]{1,0:T(8,128)(2,1)S(1)}, u32[]{:S(2)}, u32[]{:S(2)}) collective-permute-start(bf16[256,768]{1,0:T(8,128)(2,1)} %get-tuple-element.12.refs_0_), channel_id=1, source_target_pairs={{0,14},{1,15},{2,0},{3,1},{4,2},{5,3},{6,4},{7,5},{8,6},{9,7},{10,... | collective-permute-start | bytes 1179656 | tf_op jit(solution)/shard_map/ppermute | solution.py:316
  22.4 18.2 %collective-permute-start.8 = (bf16[256,768]{1,0:T(8,128)(2,1)}, bf16[256,768]{1,0:T(8,128)(2,1)S(1)}, u32[]{:S(2)}, u32[]{:S(2)}) collective-permute-start(bf16[256,768]{1,0:T(8,128)(2,1)} %get-tuple-element.15.refs_1_), channel_id=1, source_target_pairs={{0,2},{1,3},{2,4},{3,5},{4,6},{5,7},{6,8},{7,9},{8,10},{9,11},{10,... | collective-permute-start | bytes 1179656 | tf_op jit(solution)/shard_map/ppermute | solution.py:316
  28.3 14.7 %collective-permute-start.5 = (bf16[256,768]{1,0:T(8,128)(2,1)S(1)}, bf16[256,768]{1,0:T(8,128)(2,1)S(1)}, u32[]{:S(2)}, u32[]{:S(2)}) collective-permute-start(bf16[256,768]{1,0:T(8,128)(2,1)S(1)} %collective-permute-done.4.refs_5_), channel_id=1, source_target_pairs={{0,14},{1,15},{2,0},{3,1},{4,2},{5,3},{6,4},{7,5},{8,6},{9,7},{10,... | collective-permute-start | bytes 1179656 | tf_op jit(solution)/shard_map/ppermute | solution.py:316
  33.5 15.2 %collective-permute-start.1 = (bf16[256,768]{1,0:T(8,128)(2,1)S(1)}, bf16[256,768]{1,0:T(8,128)(2,1)S(1)}, u32[]{:S(2)}, u32[]{:S(2)}) collective-permute-start(bf16[256,768]{1,0:T(8,128)(2,1)S(1)} %collective-permute-done.refs_2_), channel_id=1, source_target_pairs={{0,2},{1,3},{2,4},{3,5},{4,6},{5,7},{6,8},{7,9},{8,10},{9,11},{10,... | collective-permute-start | bytes 1179656 | tf_op jit(solution)/shard_map/ppermute | solution.py:316
  35.4 16.0 %collective-permute-start.11 = (bf16[256,768]{1,0:T(8,128)(2,1)S(1)}, bf16[256,768]{1,0:T(8,128)(2,1)S(1)}, u32[]{:S(2)}, u32[]{:S(2)}) collective-permute-start(bf16[256,768]{1,0:T(8,128)(2,1)S(1)} %collective-permute-done.9.refs_4_), channel_id=1, source_target_pairs={{0,14},{1,15},{2,0},{3,1},{4,2},{5,3},{6,4},{7,5},{8,6},{9,7},{10,... | collective-permute-start | bytes 1179656 | tf_op jit(solution)/shard_map/ppermute | solution.py:316
  40.6 16.5 %collective-permute-start.10 = (bf16[256,768]{1,0:T(8,128)(2,1)S(1)}, bf16[256,768]{1,0:T(8,128)(2,1)S(1)}, u32[]{:S(2)}, u32[]{:S(2)}) collective-permute-start(bf16[256,768]{1,0:T(8,128)(2,1)S(1)} %collective-permute-done.8.refs_3_), channel_id=1, source_target_pairs={{0,2},{1,3},{2,4},{3,5},{4,6},{5,7},{6,8},{7,9},{8,10},{9,11},{10,... | collective-permute-start | bytes 1179656 | tf_op jit(solution)/shard_map/ppermute | solution.py:316
  43.0 16.9 %collective-permute-start.6 = (bf16[256,768]{1,0:T(8,128)(2,1)S(1)}, bf16[256,768]{1,0:T(8,128)(2,1)S(1)}, u32[]{:S(2)}, u32[]{:S(2)}) collective-permute-start(bf16[256,768]{1,0:T(8,128)(2,1)S(1)} %collective-permute-done.5.refs_9_), channel_id=1, source_target_pairs={{0,14},{1,15},{2,0},{3,1},{4,2},{5,3},{6,4},{7,5},{8,6},{9,7},{10,... | collective-permute-start | bytes 1179656 | tf_op jit(solution)/shard_map/ppermute | solution.py:316
  48.6 16.9 %collective-permute-start.2 = (bf16[256,768]{1,0:T(8,128)(2,1)S(1)}, bf16[256,768]{1,0:T(8,128)(2,1)S(1)}, u32[]{:S(2)}, u32[]{:S(2)}) collective-permute-start(bf16[256,768]{1,0:T(8,128)(2,1)S(1)} %collective-permute-done.1.refs_6_), channel_id=1, source_target_pairs={{0,2},{1,3},{2,4},{3,5},{4,6},{5,7},{6,8},{7,9},{8,10},{9,11},{10,... | collective-permute-start | bytes 1179656 | tf_op jit(solution)/shard_map/ppermute | solution.py:316
  51.5 16.9 %collective-permute-start.13 = (bf16[256,768]{1,0:T(8,128)(2,1)S(1)}, bf16[256,768]{1,0:T(8,128)(2,1)S(1)}, u32[]{:S(2)}, u32[]{:S(2)}) collective-permute-start(bf16[256,768]{1,0:T(8,128)(2,1)S(1)} %collective-permute-done.11.refs_8_), channel_id=1, source_target_pairs={{0,14},{1,15},{2,0},{3,1},{4,2},{5,3},{6,4},{7,5},{8,6},{9,7},{10,... | collective-permute-start | bytes 1179656 | tf_op jit(solution)/shard_map/ppermute | solution.py:316
  57.1 16.9 %collective-permute-start.12 = (bf16[256,768]{1,0:T(8,128)(2,1)S(1)}, bf16[256,768]{1,0:T(8,128)(2,1)S(1)}, u32[]{:S(2)}, u32[]{:S(2)}) collective-permute-start(bf16[256,768]{1,0:T(8,128)(2,1)S(1)} %collective-permute-done.10.refs_7_), channel_id=1, source_target_pairs={{0,2},{1,3},{2,4},{3,5},{4,6},{5,7},{6,8},{7,9},{8,10},{9,11},{10,... | collective-permute-start | bytes 1179656 | tf_op jit(solution)/shard_map/ppermute | solution.py:316
  59.9 22.8 %collective-permute-start.7 = (bf16[256,768]{1,0:T(8,128)(2,1)S(1)}, bf16[256,768]{1,0:T(8,128)(2,1)S(1)}, u32[]{:S(2)}, u32[]{:S(2)}) collective-permute-start(bf16[256,768]{1,0:T(8,128)(2,1)S(1)} %collective-permute-done.6.refs_13_), channel_id=1, source_target_pairs={{0,14},{1,15},{2,0},{3,1},{4,2},{5,3},{6,4},{7,5},{8,6},{9,7},{10,... | collective-permute-start | bytes 1179656 | tf_op jit(solution)/shard_map/ppermute | solution.py:316
  65.5 17.2 %collective-permute-start.3 = (bf16[256,768]{1,0:T(8,128)(2,1)S(1)}, bf16[256,768]{1,0:T(8,128)(2,1)S(1)}, u32[]{:S(2)}, u32[]{:S(2)}) collective-permute-start(bf16[256,768]{1,0:T(8,128)(2,1)S(1)} %collective-permute-done.2.refs_10_), channel_id=1, source_target_pairs={{0,2},{1,3},{2,4},{3,5},{4,6},{5,7},{6,8},{7,9},{8,10},{9,11},{10,... | collective-permute-start | bytes 1179656 | tf_op jit(solution)/shard_map/ppermute | solution.py:316
  84.3 4.4 %copy-start.2 = (f32[256,128]{1,0:T(8,128)S(1)}, f32[256,128]{1,0:T(8,128)}, u32[]{:S(2)}) copy-start(f32[256,128]{1,0:T(8,128)} %inverse.1.inverse_ref) | copy-start | bytes 393220
  84.3 4.4 %copy-start.5 = (f32[128,128]{1,0:T(8,128)S(1)}, f32[128,128]{1,0:T(8,128)}, u32[]{:S(2)}) copy-start(f32[128,128]{1,0:T(8,128)} %constant.10.clone.cosine_ref) | copy-start | bytes 196612
  84.3 4.4 %copy-start.6 = (f32[128,128]{1,0:T(8,128)S(1)}, f32[128,128]{1,0:T(8,128)}, u32[]{:S(2)}) copy-start(f32[128,128]{1,0:T(8,128)} %constant.11.clone.sine_ref) | copy-start | bytes 196612
  84.4 4.4 %copy-start.7 = (s32[4]{0:T(128)S(1)}, s32[4]{0:T(128)}, u32[]{:S(2)}) copy-start(s32[4]{0:T(128)} %lengths_ref.1) | copy-start | bytes 52
  84.4 4.4 %copy-start.8 = (s32[4]{0:T(128)S(1)}, s32[4]{0:T(128)}, u32[]{:S(2)}) copy-start(s32[4]{0:T(128)} %learner_ref.1) | copy-start | bytes 52
  84.4 4.3 %collective-permute-start.15 = (f32[256,768]{1,0:T(8,128)S(1)}, f32[256,768]{1,0:T(8,128)S(1)}, u32[]{:S(2)}, u32[]{:S(2)}) collective-permute-start(f32[256,768]{1,0:T(8,128)S(1)} %partial_sums.5), channel_id=1, source_target_pairs={{0,1},{1,0},{2,3},{3,2},{4,5},{5,4},{6,7},{7,6},{8,9},{9,8},{10,11... | collective-permute-start | bytes 2359304 | tf_op jit(solution)/shard_map/ppermute | solution.py:316
  115.3 16.2 %all-to-all-start.1 = ((bf16[32,8,512]{2,1,0:T(8,128)(2,1)}), bf16[32,8,512]{2,1,0:T(8,128)(2,1)S(1)}, u32[]{:S(2)}, u32[]{:S(2)}) async-start(bf16[32,8,512]{2,1,0:T(8,128)(2,1)} %bitcast.3), calls=%async_computation.1 | async-start | bytes 524288 | tf_op jit(solution)/shard_map/all_to_all | solution.py:304
  (3 other events, 10.3 us)

commit v7 on v6

--- a/solution.py
+++ b/solution.py
@@ -50,48 +50,34 @@
     )(gain, query_weight, keyval_weight)
 
 
-def inverse_kernel(*refs):
-    *rows_refs, inverse_ref, squares = refs
-    step = pl.program_id(0)
-
-    @pl.when(step == 0)
-    def _():
-        squares[...] = jnp.zeros_like(squares)
-
-    total = squares[...]
-    for ref in rows_refs:
-        for i in range(ref.shape[1] // HD):
-            total += jnp.square(ref[:, i * HD : (i + 1) * HD].astype(f32))
-    squares[...] = total
-
-    @pl.when(step == pl.num_programs(0) - 1)
-    def _():
-        depth = pl.num_programs(0) * sum(r.shape[1] for r in rows_refs)
-        mean = jnp.sum(squares[...], axis=1, keepdims=True) / depth
-        inverse_ref[...] = jnp.broadcast_to(lax.rsqrt(mean + norm_eps), inverse_ref.shape)
+def inverse_kernel(rows_ref, inverse_ref):
+    tokens, depth = rows_ref.shape
+    chunk = 4 * HD
+
+    def add(i, total):
+        rows = rows_ref[:, pl.ds(pl.multiple_of(i * chunk, chunk), chunk)]
+        for j in range(0, chunk, HD):
+            total += jnp.square(rows[:, j : j + HD].astype(f32))
+        return total
+
+    total = lax.fori_loop(0, depth // chunk, add, jnp.zeros((tokens, HD), f32))
+    mean = jnp.sum(total, axis=1, keepdims=True) / depth
+    inverse_ref[...] = jnp.broadcast_to(lax.rsqrt(mean + norm_eps), inverse_ref.shape)
 
 
 def inverses(rows):
     tokens, depth = rows.shape
-    steps, streams = 4, 4
-    block = depth // (steps * streams)
-
-    def part(stream):
-        return pl.BlockSpec((tokens, block), lambda i: (0, stream * steps + i))
-
     return pl.pallas_call(
         inverse_kernel,
         out_shape=jax.ShapeDtypeStruct((tokens, HD), f32),
-        grid=(steps,),
-        in_specs=[part(s) for s in range(streams)],
-        out_specs=pl.BlockSpec((tokens, HD), lambda i: (0, 0)),
-        scratch_shapes=[pltpu.VMEM((tokens, HD), f32)],
-        compiler_params=pltpu.CompilerParams(vmem_limit_bytes=60 << 20),
+        in_specs=[VMEM],
+        out_specs=VMEM,
+        compiler_params=pltpu.CompilerParams(vmem_limit_bytes=24 << 20),
         cost_estimate=pl.CostEstimate(
             flops=2 * tokens * depth, bytes_accessed=2 * tokens * depth, transcendentals=0
         ),
         name="inverse",
-    )(*[rows] * streams)
+    )(rows)
 
 
 def partial_kernel(distances, sides, carried, *refs):
@@ -99,63 +85,63 @@
     halves, refs = refs[: 2 * count], refs[2 * count :]
     rows, refs = refs[:sides], refs[sides:]
     before, refs = refs[: sides * carried], refs[sides * carried :]
-    out_refs, (columns, weights, arrived) = refs[:sides], refs[sides:]
-    depth = columns.shape[2]
+    out_refs, (columns, arrived) = refs[:sides], refs[sides:]
+    half = halves[0].shape[0]
     index = lax.axis_index("fsdp")
     place, core = lax.div(index, 2), lax.rem(index, 2)
     ring = lax.axis_size("fsdp") // 2
     copies = []
-
-    def copy(source, target):
-        copies.append(pltpu.make_async_copy(source, target, arrived.at[len(copies)]))
-        copies[-1].start()
-
-    for source, out_ref in zip(before, out_refs):
-        copy(source, out_ref)
-    for i, distance in enumerate(distances):
-        origin = lax.rem(place + (ring + distance), ring)
-        start = pl.multiple_of((2 * origin + core) * depth, depth)
-        for side in range(sides):
-            copy(rows[side].at[:, pl.ds(start, depth)], columns.at[side * count + i])
-        for h in range(2):
-            rest = pl.ds(h * (depth // 2), depth // 2)
-            copy(halves[2 * i + h], weights.at[i, rest, :])
-    for i in range(count):
-        known = len(before) + (i + 1) * (sides + 2)
-        for c in copies[0 if i == 0 else known - sides - 2 : known]:
-            c.wait()
-        for side in range(sides):
-            part = jnp.dot(columns[side * count + i], weights[i], preferred_element_type=f32)
-            if i or carried:
-                out_refs[side][...] += part
-            else:
-                out_refs[side][...] = part
-
-
-def partial(blocks, rows, before, vmem):
+    for side in range(sides):
+        for i, distance in enumerate(distances):
+            origin = lax.rem(place + (ring + distance), ring)
+            start = pl.multiple_of((2 * origin + core) * (2 * half), 2 * half)
+            at = side * count + i
+            copies.append(
+                pltpu.make_async_copy(
+                    rows[side].at[:, pl.ds(start, 2 * half)], columns.at[at], arrived.at[at]
+                )
+            )
+            copies[-1].start()
+    for side in range(sides):
+        total = before[side][...] if carried else None
+        for i in range(count):
+            at = side * count + i
+            copies[at].wait()
+            for h in range(2):
+                part = jnp.dot(
+                    columns[at, :, h * half : (h + 1) * half],
+                    halves[2 * i + h][...],
+                    preferred_element_type=f32,
+                )
+                total = part if total is None else total + part
+        out_refs[side][...] = total
+
+
+def partial(blocks, rows, before):
     count, sides = len(blocks), len(rows)
     halves = [w for _, pair in blocks for w in pair]
     tokens, depth = rows[0].shape[0], 2 * halves[0].shape[0]
     carried = before is not None
-    shape = jax.ShapeDtypeStruct((tokens, WIDE), f32)
+    operands = [*halves, *rows, *(before or [])]
     return pl.pallas_call(
         functools.partial(partial_kernel, [d for d, _ in blocks], sides, carried),
-        out_shape=[shape] * sides,
-        in_specs=[pl.BlockSpec(memory_space=pl.ANY)] * (len(halves) + sides + sides * carried),
+        out_shape=[jax.ShapeDtypeStruct((tokens, WIDE), f32)] * sides,
+        in_specs=[VMEM] * len(halves)
+        + [pl.BlockSpec(memory_space=pl.ANY)] * sides
+        + [VMEM] * (sides * carried),
         out_specs=[VMEM] * sides,
         scratch_shapes=[
             pltpu.VMEM((sides * count, tokens, depth), bf16),
-            pltpu.VMEM((count, depth, WIDE), bf16),
-            pltpu.SemaphoreType.DMA((count * (sides + 2) + sides * carried,)),
+            pltpu.SemaphoreType.DMA((sides * count,)),
         ],
-        compiler_params=pltpu.CompilerParams(vmem_limit_bytes=vmem << 20),
+        compiler_params=pltpu.CompilerParams(vmem_limit_bytes=28 << 20),
         cost_estimate=pl.CostEstimate(
             flops=2 * tokens * depth * WIDE * count * sides,
             bytes_accessed=2 * depth * (sides * tokens + WIDE) * count + 8 * tokens * WIDE * sides,
             transcendentals=0,
         ),
         name="partial_sums",
-    )(*halves, *rows, *(before or []))
+    )(*operands)
 
 
 def attend_kernel(
@@ -320,21 +306,21 @@
 
     held = fold(norm_gain, query_weight, keyval_weight)
     got = send(hidden, swap)
-    inverse = inverses(after(hidden, held[0]))
     above, below = list(held), list(held)
     blocks = [(0, held)]
     for step in range(1, ring // 2):
         above = [send(w, up) for w in above]
         below = [send(w, down) for w in below]
-        if step == 1:
-            above[0] = after(above[0], inverse)
         blocks += [(-step, list(above)), (step, list(below))]
     far = [send(above[0], up), send(below[1], down)]
-    sums = partial(blocks, (hidden, got), None, 28)
-    far[1] = after(far[1], *sums)
-    [other] = partial([(ring // 2, far)], (got,), sums[1:], 28)
+    both = (hidden, got)
+    sums = partial(blocks[:-2], both, None)
+    sums = partial([(d, (a, after(b, *sums))) for d, (a, b) in blocks[-2:]], both, sums)
+    inverse = inverses(after(hidden, sums[0]))
+    far[1] = after(far[1], *sums, inverse)
+    [other] = partial([(ring // 2, far)], (got,), sums[1:])
     other = send(other, swap)
-    [mine] = partial([(ring // 2, far)], (hidden,), sums[:1], 28)
+    [mine] = partial([(ring // 2, far)], (hidden,), sums[:1])
     mixed = attend(lengths, learner, slot_offset, mine, other, inverse, *rotary())
     spread = exchange(mixed)
     landed = exchange(arrange(spread))

time: 133 us -> 132 us (level)
  starting transfers between devices: 65.3 us -> 62 us
  Pallas kernels: 18.7 us -> 16 us
  waiting for transfers between devices: 21.2 us -> 23.9 us
  local copies, waits for them, and re-layouts: 2.24 us -> 4.21 us
    ppermute x16, starting transfers between devices: 60.6 us -> 57.2 us  [send(): return lax.ppermute(values, 'fsdp', pairs)]
    ppermute x16, waiting for transfers between devices: 10.3 us -> 13 us  [send(): return lax.ppermute(values, 'fsdp', pairs)]
    pallas_call x1, Pallas kernels: 4.02 us -> 1.44 us  [inverses(): pl.pallas_call(inverse_kernel, out_shape=jax.ShapeDtypeStruct((tokens, HD...]
    unnamed x20 -> x18, local copies, waits for them, and re-layouts: 2.24 us -> 4.21 us
    pallas_call x3 -> x4, Pallas kernels: 9.02 us -> 8.84 us  [partial(): pl.pallas_call(functools.partial(partial_kernel, [d for d, _ in blocks],...]
  transfers between devices with their start and end apart: 17 -> 17, of which waited for: 7 -> 6; matrix products, arithmetic and copies ran while one was open for 0% -> 0% of each run, Pallas kernels for 11% -> 9%
where the time goes in v7:
time: 132 us; the launch traced here: 131 us
  starting transfers between devices  62 us (47%)
  waiting for transfers between devices  23.9 us (18%)
  blocking collectives  23.7 us (18%)
  Pallas kernels  16 us (12%)
  local copies, waits for them, and re-layouts  4.21 us (3%)
    ppermute x16, starting transfers between devices, send(): return lax.ppermute(values, 'fsdp', pairs)  57.2 us
    all_to_all x1, blocking collectives, exchange(): lax.all_to_all(blocks, 'dp', split_axis=0, concat_axis=0, tiled=True)  23.7 us
    ppermute x16, waiting for transfers between devices, send(): return lax.ppermute(values, 'fsdp', pairs)  13 us
    all_to_all x1, waiting for transfers between devices, exchange(): lax.all_to_all(blocks, 'dp', split_axis=0, concat_axis=0, tiled=True)  10.9 us
    pallas_call x4, Pallas kernels, partial(): pl.pallas_call(functools.partial(partial_kernel, [d for d, _ in blocks],...  8.84 us
    all_to_all x1, starting transfers between devices, exchange(): lax.all_to_all(blocks, 'dp', split_axis=0, concat_axis=0, tiled=True)  4.77 us
    unnamed x18, local copies, waits for them, and re-layouts  4.21 us
  transfers between devices with their start and end apart: 17, of which 6 were waited for; matrix products, arithmetic and copies ran while one was open for 0% of the time, Pallas kernels for 9%

profile of v7, /device:TPU:8, one launch (start us, length us, event | category | flops | bytes accessed | tf_op | source)
XLA Modules:
  0.0 131.0 jit_solution(12890739149233925576)
XLA Ops:
  0.0 1.9 %collective-permute-start.13 = (bf16[256,8192]{1,0:T(8,128)(2,1)}, bf16[256,8192]{1,0:T(8,128)(2,1)}, u32[]{:S(2)}, u32[]{:S(2)}) collective-permute-start(bf16[256,8192]{1,0:T(8,128)(2,1)} %refs_2_.1), channel_id=1, source_target_pairs={{0,1},{1,0},{2,3},{3,2},{4,5},{5,4},{6,7},{7,6},{8,9},{9,8},{10,11... | collective-permute-start | bytes 12582920 | tf_op jit(solution)/shard_map/ppermute | solution.py:302
  1.9 2.3 %fold_gain.1 = (bf16[256,768]{1,0:T(8,128)(2,1)}, bf16[256,768]{1,0:T(8,128)(2,1)}) custom-call(bf16[512]{0:T(512)(128)(2,1)} %gain_ref.1, bf16[512,512]{1,0:T(8,128)(2,1)} %query_ref.1, bf16[512,256]{1,0:T(8,128)(2,1)} %keyval_ref.1), custom_call_target="tpu_custom_call" | custom-call | tf_op jit(solution)/shard_map/fold_gain/pallas_call | solution.py:44
  4.2 10.9 %collective-permute-start.4 = (bf16[256,768]{1,0:T(8,128)(2,1)}, bf16[256,768]{1,0:T(8,128)(2,1)S(1)}, u32[]{:S(2)}, u32[]{:S(2)}) collective-permute-start(bf16[256,768]{1,0:T(8,128)(2,1)} %get-tuple-element.16.refs_1_), channel_id=1, source_target_pairs={{0,14},{1,15},{2,0},{3,1},{4,2},{5,3},{6,4},{7,5},{8,6},{9,7},{10,... | collective-permute-start | bytes 1179656 | tf_op jit(solution)/shard_map/ppermute | solution.py:302
  15.2 1.9 %collective-permute-start = (bf16[256,768]{1,0:T(8,128)(2,1)}, bf16[256,768]{1,0:T(8,128)(2,1)S(1)}, u32[]{:S(2)}, u32[]{:S(2)}) collective-permute-start(bf16[256,768]{1,0:T(8,128)(2,1)} %get-tuple-element.15.refs_0_), channel_id=1, source_target_pairs={{0,2},{1,3},{2,4},{3,5},{4,6},{5,7},{6,8},{7,9},{8,10},{9,11},{10,... | collective-permute-start | bytes 1179656 | tf_op jit(solution)/shard_map/ppermute | solution.py:302
  17.1 1.9 %collective-permute-start.8 = (bf16[256,768]{1,0:T(8,128)(2,1)}, bf16[256,768]{1,0:T(8,128)(2,1)S(1)}, u32[]{:S(2)}, u32[]{:S(2)}) collective-permute-start(bf16[256,768]{1,0:T(8,128)(2,1)} %get-tuple-element.16.refs_1_), channel_id=1, source_target_pairs={{0,2},{1,3},{2,4},{3,5},{4,6},{5,7},{6,8},{7,9},{8,10},{9,11},{10,... | collective-permute-start | bytes 1179656 | tf_op jit(solution)/shard_map/ppermute | solution.py:302
  19.0 5.1 %collective-permute-start.11 = (bf16[256,768]{1,0:T(8,128)(2,1)}, bf16[256,768]{1,0:T(8,128)(2,1)S(1)}, u32[]{:S(2)}, u32[]{:S(2)}) collective-permute-start(bf16[256,768]{1,0:T(8,128)(2,1)} %get-tuple-element.15.refs_0_), channel_id=1, source_target_pairs={{0,14},{1,15},{2,0},{3,1},{4,2},{5,3},{6,4},{7,5},{8,6},{9,7},{10,... | collective-permute-start | bytes 1179656 | tf_op jit(solution)/shard_map/ppermute | solution.py:302
  24.5 5.5 %collective-permute-start.5 = (bf16[256,768]{1,0:T(8,128)(2,1)S(1)}, bf16[256,768]{1,0:T(8,128)(2,1)S(1)}, u32[]{:S(2)}, u32[]{:S(2)}) collective-permute-start(bf16[256,768]{1,0:T(8,128)(2,1)S(1)} %collective-permute-done.4.refs_5_), channel_id=1, source_target_pairs={{0,14},{1,15},{2,0},{3,1},{4,2},{5,3},{6,4},{7,5},{8,6},{9,7},{10,... | collective-permute-start | bytes 1179656 | tf_op jit(solution)/shard_map/ppermute | solution.py:302
  30.4 1.9 %collective-permute-start.1 = (bf16[256,768]{1,0:T(8,128)(2,1)S(1)}, bf16[256,768]{1,0:T(8,128)(2,1)S(1)}, u32[]{:S(2)}, u32[]{:S(2)}) collective-permute-start(bf16[256,768]{1,0:T(8,128)(2,1)S(1)} %collective-permute-done.refs_2_), channel_id=1, source_target_pairs={{0,2},{1,3},{2,4},{3,5},{4,6},{5,7},{6,8},{7,9},{8,10},{9,11},{10,... | collective-permute-start | bytes 1179656 | tf_op jit(solution)/shard_map/ppermute | solution.py:302
  32.4 6.5 %collective-permute-done.8.refs_3_ = bf16[256,768]{1,0:T(8,128)(2,1)S(1)} collective-permute-done((bf16[256,768]{1,0:T(8,128)(2,1)}, bf16[256,768]{1,0:T(8,128)(2,1)S(1)}, u32[]{:S(2)}, u32[]{:S(2)}) %collective-permute-start.8) | collective-permute-done | bytes 393248 | tf_op jit(solution)/shard_map/ppermute | solution.py:302
  38.9 1.9 %collective-permute-start.9 = (bf16[256,768]{1,0:T(8,128)(2,1)S(1)}, bf16[256,768]{1,0:T(8,128)(2,1)S(1)}, u32[]{:S(2)}, u32[]{:S(2)}) collective-permute-start(bf16[256,768]{1,0:T(8,128)(2,1)S(1)} %collective-permute-done.8.refs_3_), channel_id=1, source_target_pairs={{0,2},{1,3},{2,4},{3,5},{4,6},{5,7},{6,8},{7,9},{8,10},{9,11},{10,... | collective-permute-start | bytes 1179656 | tf_op jit(solution)/shard_map/ppermute | solution.py:302
  40.8 5.1 %collective-permute-start.12 = (bf16[256,768]{1,0:T(8,128)(2,1)S(1)}, bf16[256,768]{1,0:T(8,128)(2,1)S(1)}, u32[]{:S(2)}, u32[]{:S(2)}) collective-permute-start(bf16[256,768]{1,0:T(8,128)(2,1)S(1)} %collective-permute-done.11.refs_4_), channel_id=1, source_target_pairs={{0,14},{1,15},{2,0},{3,1},{4,2},{5,3},{6,4},{7,5},{8,6},{9,7},{10,... | collective-permute-start | bytes 1179656 | tf_op jit(solution)/shard_map/ppermute | solution.py:302
  45.9 1.9 %collective-permute-start.6 = (bf16[256,768]{1,0:T(8,128)(2,1)S(1)}, bf16[256,768]{1,0:T(8,128)(2,1)S(1)}, u32[]{:S(2)}, u32[]{:S(2)}) collective-permute-start(bf16[256,768]{1,0:T(8,128)(2,1)S(1)} %collective-permute-done.5.refs_9_), channel_id=1, source_target_pairs={{0,14},{1,15},{2,0},{3,1},{4,2},{5,3},{6,4},{7,5},{8,6},{9,7},{10,... | collective-permute-start | bytes 1179656 | tf_op jit(solution)/shard_map/ppermute | solution.py:302
  47.9 3.9 %collective-permute-start.2 = (bf16[256,768]{1,0:T(8,128)(2,1)S(1)}, bf16[256,768]{1,0:T(8,128)(2,1)S(1)}, u32[]{:S(2)}, u32[]{:S(2)}) collective-permute-start(bf16[256,768]{1,0:T(8,128)(2,1)S(1)} %collective-permute-done.1.refs_6_), channel_id=1, source_target_pairs={{0,2},{1,3},{2,4},{3,5},{4,6},{5,7},{6,8},{7,9},{8,10},{9,11},{10,... | collective-permute-start | bytes 1179656 | tf_op jit(solution)/shard_map/ppermute | solution.py:302
  51.8 3.9 %collective-permute-done.9.refs_7_ = bf16[256,768]{1,0:T(8,128)(2,1)S(1)} collective-permute-done((bf16[256,768]{1,0:T(8,128)(2,1)S(1)}, bf16[256,768]{1,0:T(8,128)(2,1)S(1)}, u32[]{:S(2)}, u32[]{:S(2)}) %collective-permute-start.9) | collective-permute-done | bytes 393248 | tf_op jit(solution)/shard_map/ppermute | solution.py:302
  57.6 5.1 %collective-permute-start.14 = (bf16[256,768]{1,0:T(8,128)(2,1)S(1)}, bf16[256,768]{1,0:T(8,128)(2,1)S(1)}, u32[]{:S(2)}, u32[]{:S(2)}) collective-permute-start(bf16[256,768]{1,0:T(8,128)(2,1)S(1)} %collective-permute-done.12.refs_8_), channel_id=1, source_target_pairs={{0,14},{1,15},{2,0},{3,1},{4,2},{5,3},{6,4},{7,5},{8,6},{9,7},{10,... | collective-permute-start | bytes 1179656 | tf_op jit(solution)/shard_map/ppermute | solution.py:302
  62.8 4.1 %collective-permute-start.7 = (bf16[256,768]{1,0:T(8,128)(2,1)S(1)}, bf16[256,768]{1,0:T(8,128)(2,1)S(1)}, u32[]{:S(2)}, u32[]{:S(2)}) collective-permute-start(bf16[256,768]{1,0:T(8,128)(2,1)S(1)} %collective-permute-done.6.refs_3_), channel_id=1, source_target_pairs={{0,14},{1,15},{2,0},{3,1},{4,2},{5,3},{6,4},{7,5},{8,6},{9,7},{10,... | collective-permute-start | bytes 1179656 | tf_op jit(solution)/shard_map/ppermute | solution.py:302
  66.9 1.9 %collective-permute-start.3 = (bf16[256,768]{1,0:T(8,128)(2,1)S(1)}, bf16[256,768]{1,0:T(8,128)(2,1)S(1)}, u32[]{:S(2)}, u32[]{:S(2)}) collective-permute-start(bf16[256,768]{1,0:T(8,128)(2,1)S(1)} %collective-permute-done.2.refs_0_), channel_id=1, source_target_pairs={{0,2},{1,3},{2,4},{3,5},{4,6},{5,7},{6,8},{7,9},{8,10},{9,11},{10,... | collective-permute-start | bytes 1179656 | tf_op jit(solution)/shard_map/ppermute | solution.py:302
  68.8 2.2 %copy-done = bf16[256,8192]{1,0:T(8,128)(2,1)S(1)} copy-done((bf16[256,8192]{1,0:T(8,128)(2,1)S(1)}, bf16[256,8192]{1,0:T(8,128)(2,1)}, u32[]{:S(2)}) %copy-start) | copy-done | bytes 4194328
  73.0 4.8 %partial_sums.4 = (f32[256,768]{1,0:T(8,128)S(1)}, f32[256,768]{1,0:T(8,128)S(1)}) custom-call(bf16[256,768]{1,0:T(8,128)(2,1)S(1)} %copy-done.2, bf16[256,768]{1,0:T(8,128)(2,1)S(1)} %copy-done.3, bf16[256,768]{1,0:T(8,128)(2,1)S(1)} %collective-permute-done.refs_2_, bf16[256,768]{1,0:T(8,128)(2,1)S(1)} %collective-permute-done.8.refs_3_, ...), custom_call_target="tpu_custom_call" | custom-call | flops 2013265920 | bytes 9699328 | tf_op jit(solution)/shard_map/partial_sums/pallas_call | solution.py:126
  77.9 2.2 %partial_sums.5 = (f32[256,768]{1,0:T(8,128)S(1)}, f32[256,768]{1,0:T(8,128)S(1)}) custom-call(bf16[256,768]{1,0:T(8,128)(2,1)S(1)} %collective-permute-done.2.refs_0_, bf16[256,768]{1,0:T(8,128)(2,1)S(1)} %collective-permute-done.10.refs_1_, bf16[256,768]{1,0:T(8,128)(2,1)S(1)} %collective-permute-done.14.refs_2_, ...), custom_call_target="tpu_custom_call" | custom-call | flops 805306368 | bytes 5767168 | tf_op jit(solution)/shard_map/partial_sums/pallas_call | solution.py:126
  83.0 2.1 %collective-permute-start.15 = (f32[256,768]{1,0:T(8,128)S(1)}, f32[256,768]{1,0:T(8,128)S(1)}, u32[]{:S(2)}, u32[]{:S(2)}) collective-permute-start(f32[256,768]{1,0:T(8,128)S(1)} %partial_sums.7), channel_id=1, source_target_pairs={{0,1},{1,0},{2,3},{3,2},{4,5},{5,4},{6,7},{7,6},{8,9},{9,8},{10,11... | collective-permute-start | bytes 2359304 | tf_op jit(solution)/shard_map/ppermute | solution.py:302
  89.1 23.7 %all_to_all.10 = bf16[32,8,640]{2,1,0:T(8,128)(2,1)S(1)} all-to-all(bf16[32,8,640]{2,1,0:T(8,128)(2,1)S(1)} %bitcast.10), channel_id=1, replica_groups=mesh['dp'=32,'fsdp'=16] {'dp'}, dimensions={0} | all-to-all | bytes 655360 | tf_op jit(solution)/shard_map/all_to_all | solution.py:290
  113.9 4.8 %all-to-all-start.1 = ((bf16[32,8,512]{2,1,0:T(8,128)(2,1)}), bf16[32,8,512]{2,1,0:T(8,128)(2,1)S(1)}, u32[]{:S(2)}, u32[]{:S(2)}) async-start(bf16[32,8,512]{2,1,0:T(8,128)(2,1)} %bitcast.3), calls=%async_computation.1 | async-start | bytes 524288 | tf_op jit(solution)/shard_map/all_to_all | solution.py:290
  119.2 10.9 %all-to-all-done.1 = bf16[32,8,512]{2,1,0:T(8,128)(2,1)S(1)} async-done(((bf16[32,8,512]{2,1,0:T(8,128)(2,1)}), bf16[32,8,512]{2,1,0:T(8,128)(2,1)S(1)}, u32[]{:S(2)}, u32[]{:S(2)}) %all-to-all-start.1) | async-done | bytes 262176 | tf_op jit(solution)/shard_map/all_to_all | solution.py:290
  (39 shorter events, 14.1 us)
Async XLA Ops:
  0.0 68.8 %collective-permute-start.13 = (bf16[256,8192]{1,0:T(8,128)(2,1)}, bf16[256,8192]{1,0:T(8,128)(2,1)}, u32[]{:S(2)}, u32[]{:S(2)}) collective-permute-start(bf16[256,8192]{1,0:T(8,128)(2,1)} %refs_2_.1), channel_id=1, source_target_pairs={{0,1},{1,0},{2,3},{3,2},{4,5},{5,4},{6,7},{7,6},{8,9},{9,8},{10,11... | collective-permute-start | bytes 12582920 | tf_op jit(solution)/shard_map/ppermute | solution.py:302
  4.2 20.3 %collective-permute-start.4 = (bf16[256,768]{1,0:T(8,128)(2,1)}, bf16[256,768]{1,0:T(8,128)(2,1)S(1)}, u32[]{:S(2)}, u32[]{:S(2)}) collective-permute-start(bf16[256,768]{1,0:T(8,128)(2,1)} %get-tuple-element.16.refs_1_), channel_id=1, source_target_pairs={{0,14},{1,15},{2,0},{3,1},{4,2},{5,3},{6,4},{7,5},{8,6},{9,7},{10,... | collective-permute-start | bytes 1179656 | tf_op jit(solution)/shard_map/ppermute | solution.py:302
  15.2 15.3 %collective-permute-start = (bf16[256,768]{1,0:T(8,128)(2,1)}, bf16[256,768]{1,0:T(8,128)(2,1)S(1)}, u32[]{:S(2)}, u32[]{:S(2)}) collective-permute-start(bf16[256,768]{1,0:T(8,128)(2,1)} %get-tuple-element.15.refs_0_), channel_id=1, source_target_pairs={{0,2},{1,3},{2,4},{3,5},{4,6},{5,7},{6,8},{7,9},{8,10},{9,11},{10,... | collective-permute-start | bytes 1179656 | tf_op jit(solution)/shard_map/ppermute | solution.py:302
  17.1 21.8 %collective-permute-start.8 = (bf16[256,768]{1,0:T(8,128)(2,1)}, bf16[256,768]{1,0:T(8,128)(2,1)S(1)}, u32[]{:S(2)}, u32[]{:S(2)}) collective-permute-start(bf16[256,768]{1,0:T(8,128)(2,1)} %get-tuple-element.16.refs_1_), channel_id=1, source_target_pairs={{0,2},{1,3},{2,4},{3,5},{4,6},{5,7},{6,8},{7,9},{8,10},{9,11},{10,... | collective-permute-start | bytes 1179656 | tf_op jit(solution)/shard_map/ppermute | solution.py:302
  19.0 21.8 %collective-permute-start.11 = (bf16[256,768]{1,0:T(8,128)(2,1)}, bf16[256,768]{1,0:T(8,128)(2,1)S(1)}, u32[]{:S(2)}, u32[]{:S(2)}) collective-permute-start(bf16[256,768]{1,0:T(8,128)(2,1)} %get-tuple-element.15.refs_0_), channel_id=1, source_target_pairs={{0,14},{1,15},{2,0},{3,1},{4,2},{5,3},{6,4},{7,5},{8,6},{9,7},{10,... | collective-permute-start | bytes 1179656 | tf_op jit(solution)/shard_map/ppermute | solution.py:302
  24.5 21.4 %collective-permute-start.5 = (bf16[256,768]{1,0:T(8,128)(2,1)S(1)}, bf16[256,768]{1,0:T(8,128)(2,1)S(1)}, u32[]{:S(2)}, u32[]{:S(2)}) collective-permute-start(bf16[256,768]{1,0:T(8,128)(2,1)S(1)} %collective-permute-done.4.refs_5_), channel_id=1, source_target_pairs={{0,14},{1,15},{2,0},{3,1},{4,2},{5,3},{6,4},{7,5},{8,6},{9,7},{10,... | collective-permute-start | bytes 1179656 | tf_op jit(solution)/shard_map/ppermute | solution.py:302
  30.4 17.4 %collective-permute-start.1 = (bf16[256,768]{1,0:T(8,128)(2,1)S(1)}, bf16[256,768]{1,0:T(8,128)(2,1)S(1)}, u32[]{:S(2)}, u32[]{:S(2)}) collective-permute-start(bf16[256,768]{1,0:T(8,128)(2,1)S(1)} %collective-permute-done.refs_2_), channel_id=1, source_target_pairs={{0,2},{1,3},{2,4},{3,5},{4,6},{5,7},{6,8},{7,9},{8,10},{9,11},{10,... | collective-permute-start | bytes 1179656 | tf_op jit(solution)/shard_map/ppermute | solution.py:302
  38.9 16.9 %collective-permute-start.9 = (bf16[256,768]{1,0:T(8,128)(2,1)S(1)}, bf16[256,768]{1,0:T(8,128)(2,1)S(1)}, u32[]{:S(2)}, u32[]{:S(2)}) collective-permute-start(bf16[256,768]{1,0:T(8,128)(2,1)S(1)} %collective-permute-done.8.refs_3_), channel_id=1, source_target_pairs={{0,2},{1,3},{2,4},{3,5},{4,6},{5,7},{6,8},{7,9},{8,10},{9,11},{10,... | collective-permute-start | bytes 1179656 | tf_op jit(solution)/shard_map/ppermute | solution.py:302
  40.8 16.8 %collective-permute-start.12 = (bf16[256,768]{1,0:T(8,128)(2,1)S(1)}, bf16[256,768]{1,0:T(8,128)(2,1)S(1)}, u32[]{:S(2)}, u32[]{:S(2)}) collective-permute-start(bf16[256,768]{1,0:T(8,128)(2,1)S(1)} %collective-permute-done.11.refs_4_), channel_id=1, source_target_pairs={{0,14},{1,15},{2,0},{3,1},{4,2},{5,3},{6,4},{7,5},{8,6},{9,7},{10,... | collective-permute-start | bytes 1179656 | tf_op jit(solution)/shard_map/ppermute | solution.py:302
  45.9 16.8 %collective-permute-start.6 = (bf16[256,768]{1,0:T(8,128)(2,1)S(1)}, bf16[256,768]{1,0:T(8,128)(2,1)S(1)}, u32[]{:S(2)}, u32[]{:S(2)}) collective-permute-start(bf16[256,768]{1,0:T(8,128)(2,1)S(1)} %collective-permute-done.5.refs_9_), channel_id=1, source_target_pairs={{0,14},{1,15},{2,0},{3,1},{4,2},{5,3},{6,4},{7,5},{8,6},{9,7},{10,... | collective-permute-start | bytes 1179656 | tf_op jit(solution)/shard_map/ppermute | solution.py:302
  47.9 19.0 %collective-permute-start.2 = (bf16[256,768]{1,0:T(8,128)(2,1)S(1)}, bf16[256,768]{1,0:T(8,128)(2,1)S(1)}, u32[]{:S(2)}, u32[]{:S(2)}) collective-permute-start(bf16[256,768]{1,0:T(8,128)(2,1)S(1)} %collective-permute-done.1.refs_6_), channel_id=1, source_target_pairs={{0,2},{1,3},{2,4},{3,5},{4,6},{5,7},{6,8},{7,9},{8,10},{9,11},{10,... | collective-permute-start | bytes 1179656 | tf_op jit(solution)/shard_map/ppermute | solution.py:302
  55.7 22.1 %collective-permute-start.10 = (bf16[256,768]{1,0:T(8,128)(2,1)S(1)}, bf16[256,768]{1,0:T(8,128)(2,1)S(1)}, u32[]{:S(2)}, u32[]{:S(2)}) collective-permute-start(bf16[256,768]{1,0:T(8,128)(2,1)S(1)} %collective-permute-done.9.refs_7_), channel_id=1, source_target_pairs={{0,2},{1,3},{2,4},{3,5},{4,6},{5,7},{6,8},{7,9},{8,10},{9,11},{10,... | collective-permute-start | bytes 1179656 | tf_op jit(solution)/shard_map/ppermute | solution.py:302
  57.6 20.2 %collective-permute-start.14 = (bf16[256,768]{1,0:T(8,128)(2,1)S(1)}, bf16[256,768]{1,0:T(8,128)(2,1)S(1)}, u32[]{:S(2)}, u32[]{:S(2)}) collective-permute-start(bf16[256,768]{1,0:T(8,128)(2,1)S(1)} %collective-permute-done.12.refs_8_), channel_id=1, source_target_pairs={{0,14},{1,15},{2,0},{3,1},{4,2},{5,3},{6,4},{7,5},{8,6},{9,7},{10,... | collective-permute-start | bytes 1179656 | tf_op jit(solution)/shard_map/ppermute | solution.py:302
  62.8 18.7 %collective-permute-start.7 = (bf16[256,768]{1,0:T(8,128)(2,1)S(1)}, bf16[256,768]{1,0:T(8,128)(2,1)S(1)}, u32[]{:S(2)}, u32[]{:S(2)}) collective-permute-start(bf16[256,768]{1,0:T(8,128)(2,1)S(1)} %collective-permute-done.6.refs_3_), channel_id=1, source_target_pairs={{0,14},{1,15},{2,0},{3,1},{4,2},{5,3},{6,4},{7,5},{8,6},{9,7},{10,... | collective-permute-start | bytes 1179656 | tf_op jit(solution)/shard_map/ppermute | solution.py:302
  66.9 14.7 %collective-permute-start.3 = (bf16[256,768]{1,0:T(8,128)(2,1)S(1)}, bf16[256,768]{1,0:T(8,128)(2,1)S(1)}, u32[]{:S(2)}, u32[]{:S(2)}) collective-permute-start(bf16[256,768]{1,0:T(8,128)(2,1)S(1)} %collective-permute-done.2.refs_0_), channel_id=1, source_target_pairs={{0,2},{1,3},{2,4},{3,5},{4,6},{5,7},{6,8},{7,9},{8,10},{9,11},{10,... | collective-permute-start | bytes 1179656 | tf_op jit(solution)/shard_map/ppermute | solution.py:302
  68.8 2.2 %copy-start = (bf16[256,8192]{1,0:T(8,128)(2,1)S(1)}, bf16[256,8192]{1,0:T(8,128)(2,1)}, u32[]{:S(2)}) copy-start(bf16[256,8192]{1,0:T(8,128)(2,1)} %refs_2_.1) | copy-start | bytes 12582916
  73.0 4.9 %copy-start.1 = (bf16[256,8192]{1,0:T(8,128)(2,1)S(1)}, bf16[256,8192]{1,0:T(8,128)(2,1)}, u32[]{:S(2)}) copy-start(bf16[256,8192]{1,0:T(8,128)(2,1)} %refs_2_.1) | copy-start | bytes 12582916
  82.9 4.4 %copy-start.4 = (f32[128,128]{1,0:T(8,128)S(1)}, f32[128,128]{1,0:T(8,128)}, u32[]{:S(2)}) copy-start(f32[128,128]{1,0:T(8,128)} %constant.10.clone.cosine_ref) | copy-start | bytes 196612
  82.9 4.4 %copy-start.5 = (f32[128,128]{1,0:T(8,128)S(1)}, f32[128,128]{1,0:T(8,128)}, u32[]{:S(2)}) copy-start(f32[128,128]{1,0:T(8,128)} %constant.11.clone.sine_ref) | copy-start | bytes 196612
  82.9 4.4 %copy-start.6 = (s32[4]{0:T(128)S(1)}, s32[4]{0:T(128)}, u32[]{:S(2)}) copy-start(s32[4]{0:T(128)} %lengths_ref.1) | copy-start | bytes 52
  83.0 4.3 %copy-start.7 = (s32[4]{0:T(128)S(1)}, s32[4]{0:T(128)}, u32[]{:S(2)}) copy-start(s32[4]{0:T(128)} %learner_ref.1) | copy-start | bytes 52
  83.0 4.3 %copy-start.8 = (s32[4]{0:T(128)S(1)}, s32[4]{0:T(128)}, u32[]{:S(2)}) copy-start(s32[4]{0:T(128)} %offset_ref.1) | copy-start | bytes 52
  83.0 4.3 %collective-permute-start.15 = (f32[256,768]{1,0:T(8,128)S(1)}, f32[256,768]{1,0:T(8,128)S(1)}, u32[]{:S(2)}, u32[]{:S(2)}) collective-permute-start(f32[256,768]{1,0:T(8,128)S(1)} %partial_sums.7), channel_id=1, source_target_pairs={{0,1},{1,0},{2,3},{3,2},{4,5},{5,4},{6,7},{7,6},{8,9},{9,8},{10,11... | collective-permute-start | bytes 2359304 | tf_op jit(solution)/shard_map/ppermute | solution.py:302
  113.9 16.2 %all-to-all-start.1 = ((bf16[32,8,512]{2,1,0:T(8,128)(2,1)}), bf16[32,8,512]{2,1,0:T(8,128)(2,1)S(1)}, u32[]{:S(2)}, u32[]{:S(2)}) async-start(bf16[32,8,512]{2,1,0:T(8,128)(2,1)} %bitcast.3), calls=%async_computation.1 | async-start | bytes 524288 | tf_op jit(solution)/shard_map/all_to_all | solution.py:290
  (2 other events, 2.0 us)

commit v8 on v7

--- a/solution.py
+++ b/solution.py
@@ -46,6 +46,7 @@
         out_shape=[half] * 2,
         in_specs=[VMEM] * 3,
         out_specs=[VMEM] * 2,
+        compiler_params=pltpu.CompilerParams(vmem_limit_bytes=16 << 20),
         name="fold_gain",
     )(gain, query_weight, keyval_weight)
 
@@ -306,18 +307,25 @@
 
     held = fold(norm_gain, query_weight, keyval_weight)
     got = send(hidden, swap)
+    both = (hidden, got)
     above, below = list(held), list(held)
-    blocks = [(0, held)]
     for step in range(1, ring // 2):
+        near = (above, below)
         above = [send(w, up) for w in above]
         below = [send(w, down) for w in below]
-        blocks += [(-step, list(above)), (step, list(below))]
+        if step == 1:
+            sums = partial([(0, (held[0], after(held[1], above[0])))], both, None)
+            inverse = inverses(after(hidden, above[0]))
+            above[1] = after(above[1], *sums, inverse)
+        else:
+            blocks = [(1 - step, near[0]), (step - 1, near[1])]
+            sums = partial(blocks, both, sums)
+            if step == 2:
+                above[1] = after(above[1], *sums)
     far = [send(above[0], up), send(below[1], down)]
-    both = (hidden, got)
-    sums = partial(blocks[:-2], both, None)
-    sums = partial([(d, (a, after(b, *sums))) for d, (a, b) in blocks[-2:]], both, sums)
-    inverse = inverses(after(hidden, sums[0]))
-    far[1] = after(far[1], *sums, inverse)
+    last = step
+    sums = partial([(-last, (above[0], after(above[1], *sums))), (last, below)], both, sums)
+    far[1] = after(far[1], *sums)
     [other] = partial([(ring // 2, far)], (got,), sums[1:])
     other = send(other, swap)
     [mine] = partial([(ring // 2, far)], (hidden,), sums[:1])

time: 132 us -> 130 us (0.985)
  Pallas kernels: 16 us -> 13.7 us
  local copies, waits for them, and re-layouts: 4.21 us -> 5.61 us
    pallas_call x1, Pallas kernels: 2.31 us -> 0.37 us  [fold(): pl.pallas_call(fold_kernel, out_shape=[half] * 2, in_specs=[VMEM] * 3, ou...]
    unnamed x18 -> x20, local copies, waits for them, and re-layouts: 4.21 us -> 5.61 us
    pallas_call x4 -> x6, Pallas kernels: 8.84 us -> 8.53 us  [partial(): pl.pallas_call(functools.partial(partial_kernel, [d for d, _ in blocks],...]
  transfers between devices with their start and end apart: 17 -> 17, of which waited for: 6 -> 8; matrix products, arithmetic and copies ran while one was open for 0% -> 0% of each run, Pallas kernels for 9% -> 8%
where the time goes in v8:
time: 130 us; the launch traced here: 129 us
  starting transfers between devices  62.1 us (48%)
  blocking collectives  23.7 us (18%)
  waiting for transfers between devices  23.1 us (18%)
  Pallas kernels  13.7 us (11%)
  local copies, waits for them, and re-layouts  5.61 us (4%)
    ppermute x16, starting transfers between devices, send(): return lax.ppermute(values, 'fsdp', pairs)  57.3 us
    all_to_all x1, blocking collectives, exchange(): lax.all_to_all(blocks, 'dp', split_axis=0, concat_axis=0, tiled=True)  23.7 us
    ppermute x16, waiting for transfers between devices, send(): return lax.ppermute(values, 'fsdp', pairs)  12.1 us
    all_to_all x1, waiting for transfers between devices, exchange(): lax.all_to_all(blocks, 'dp', split_axis=0, concat_axis=0, tiled=True)  11 us
    pallas_call x6, Pallas kernels, partial(): pl.pallas_call(functools.partial(partial_kernel, [d for d, _ in blocks],...  8.53 us
    unnamed x20, local copies, waits for them, and re-layouts  5.61 us
    all_to_all x1, starting transfers between devices, exchange(): lax.all_to_all(blocks, 'dp', split_axis=0, concat_axis=0, tiled=True)  4.76 us
  transfers between devices with their start and end apart: 17, of which 8 were waited for; matrix products, arithmetic and copies ran while one was open for 0% of the time, Pallas kernels for 8%

profile of v8, /device:TPU:8, one launch (start us, length us, event | category | flops | bytes accessed | tf_op | source)
XLA Modules:
  0.0 129.4 jit_solution(14968538932914100413)
XLA Ops:
  0.0 1.9 %collective-permute-start.9 = (bf16[256,8192]{1,0:T(8,128)(2,1)}, bf16[256,8192]{1,0:T(8,128)(2,1)S(1)}, u32[]{:S(2)}, u32[]{:S(2)}) collective-permute-start(bf16[256,8192]{1,0:T(8,128)(2,1)} %refs_2_.3), channel_id=1, source_target_pairs={{0,1},{1,0},{2,3},{3,2},{4,5},{5,4},{6,7},{7,6},{8,9},{9,8},{10,11... | collective-permute-start | bytes 12582920 | tf_op jit(solution)/shard_map/ppermute | solution.py:303
  5.0 10.9 %collective-permute-start.4 = (bf16[256,768]{1,0:T(8,128)(2,1)S(1)}, bf16[256,768]{1,0:T(8,128)(2,1)S(1)}, u32[]{:S(2)}, u32[]{:S(2)}) collective-permute-start(bf16[256,768]{1,0:T(8,128)(2,1)S(1)} %get-tuple-element.23.refs_1_), channel_id=1, source_target_pairs={{0,14},{1,15},{2,0},{3,1},{4,2},{5,3},{6,4},{7,5},{8,6},{9,7},{10,... | collective-permute-start | bytes 1179656 | tf_op jit(solution)/shard_map/ppermute | solution.py:303
  15.9 1.9 %collective-permute-start = (bf16[256,768]{1,0:T(8,128)(2,1)S(1)}, bf16[256,768]{1,0:T(8,128)(2,1)S(1)}, u32[]{:S(2)}, u32[]{:S(2)}) collective-permute-start(bf16[256,768]{1,0:T(8,128)(2,1)S(1)} %get-tuple-element.21.refs_0_), channel_id=1, source_target_pairs={{0,2},{1,3},{2,4},{3,5},{4,6},{5,7},{6,8},{7,9},{8,10},{9,11},{10,... | collective-permute-start | bytes 1179656 | tf_op jit(solution)/shard_map/ppermute | solution.py:303
  17.8 1.9 %collective-permute-start.8 = (bf16[256,768]{1,0:T(8,128)(2,1)S(1)}, bf16[256,768]{1,0:T(8,128)(2,1)S(1)}, u32[]{:S(2)}, u32[]{:S(2)}) collective-permute-start(bf16[256,768]{1,0:T(8,128)(2,1)S(1)} %get-tuple-element.23.refs_1_), channel_id=1, source_target_pairs={{0,2},{1,3},{2,4},{3,5},{4,6},{5,7},{6,8},{7,9},{8,10},{9,11},{10,... | collective-permute-start | bytes 1179656 | tf_op jit(solution)/shard_map/ppermute | solution.py:303
  19.8 5.1 %collective-permute-start.11 = (bf16[256,768]{1,0:T(8,128)(2,1)S(1)}, bf16[256,768]{1,0:T(8,128)(2,1)S(1)}, u32[]{:S(2)}, u32[]{:S(2)}) collective-permute-start(bf16[256,768]{1,0:T(8,128)(2,1)S(1)} %get-tuple-element.21.refs_0_), channel_id=1, source_target_pairs={{0,14},{1,15},{2,0},{3,1},{4,2},{5,3},{6,4},{7,5},{8,6},{9,7},{10,... | collective-permute-start | bytes 1179656 | tf_op jit(solution)/shard_map/ppermute | solution.py:303
  24.9 5.6 %collective-permute-start.5 = (bf16[256,768]{1,0:T(8,128)(2,1)S(1)}, bf16[256,768]{1,0:T(8,128)(2,1)S(1)}, u32[]{:S(2)}, u32[]{:S(2)}) collective-permute-start(bf16[256,768]{1,0:T(8,128)(2,1)S(1)} %collective-permute-done.4.refs_3_), channel_id=1, source_target_pairs={{0,14},{1,15},{2,0},{3,1},{4,2},{5,3},{6,4},{7,5},{8,6},{9,7},{10,... | collective-permute-start | bytes 1179656 | tf_op jit(solution)/shard_map/ppermute | solution.py:303
  32.9 2.2 %copy-done = bf16[256,8192]{1,0:T(8,128)(2,1)S(1)} copy-done((bf16[256,8192]{1,0:T(8,128)(2,1)S(1)}, bf16[256,8192]{1,0:T(8,128)(2,1)}, u32[]{:S(2)}) %copy-start) | copy-done | bytes 4194328
  39.4 1.9 %collective-permute-start.10 = (bf16[256,768]{1,0:T(8,128)(2,1)S(1)}, bf16[256,768]{1,0:T(8,128)(2,1)S(1)}, u32[]{:S(2)}, u32[]{:S(2)}) collective-permute-start(bf16[256,768]{1,0:T(8,128)(2,1)S(1)} %collective-permute-done.8.refs_1_), channel_id=1, source_target_pairs={{0,2},{1,3},{2,4},{3,5},{4,6},{5,7},{6,8},{7,9},{8,10},{9,11},{10,... | collective-permute-start | bytes 1179656 | tf_op jit(solution)/shard_map/ppermute | solution.py:303
  41.3 5.1 %collective-permute-start.13 = (bf16[256,768]{1,0:T(8,128)(2,1)S(1)}, bf16[256,768]{1,0:T(8,128)(2,1)S(1)}, u32[]{:S(2)}, u32[]{:S(2)}) collective-permute-start(bf16[256,768]{1,0:T(8,128)(2,1)S(1)} %collective-permute-done.11.refs_2_), channel_id=1, source_target_pairs={{0,14},{1,15},{2,0},{3,1},{4,2},{5,3},{6,4},{7,5},{8,6},{9,7},{10,... | collective-permute-start | bytes 1179656 | tf_op jit(solution)/shard_map/ppermute | solution.py:303
  46.5 2.8 %collective-permute-start.6 = (bf16[256,768]{1,0:T(8,128)(2,1)S(1)}, bf16[256,768]{1,0:T(8,128)(2,1)S(1)}, u32[]{:S(2)}, u32[]{:S(2)}) collective-permute-start(bf16[256,768]{1,0:T(8,128)(2,1)S(1)} %collective-permute-done.5.refs_3_), channel_id=1, source_target_pairs={{0,14},{1,15},{2,0},{3,1},{4,2},{5,3},{6,4},{7,5},{8,6},{9,7},{10,... | collective-permute-start | bytes 1179656 | tf_op jit(solution)/shard_map/ppermute | solution.py:303
  49.3 3.1 %collective-permute-start.2 = (bf16[256,768]{1,0:T(8,128)(2,1)S(1)}, bf16[256,768]{1,0:T(8,128)(2,1)S(1)}, u32[]{:S(2)}, u32[]{:S(2)}) collective-permute-start(bf16[256,768]{1,0:T(8,128)(2,1)S(1)} %collective-permute-done.1.refs_0_), channel_id=1, source_target_pairs={{0,2},{1,3},{2,4},{3,5},{4,6},{5,7},{6,8},{7,9},{8,10},{9,11},{10,... | collective-permute-start | bytes 1179656 | tf_op jit(solution)/shard_map/ppermute | solution.py:303
  52.3 2.2 %partial_sums.7 = (f32[256,768]{1,0:T(8,128)S(1)}, f32[256,768]{1,0:T(8,128)S(1)}) custom-call(bf16[256,768]{1,0:T(8,128)(2,1)S(1)} %collective-permute-done.refs_0_, bf16[256,768]{1,0:T(8,128)(2,1)S(1)} %collective-permute-done.8.refs_1_, bf16[256,768]{1,0:T(8,128)(2,1)S(1)} %collective-permute-done.11.refs_2_, ...), custom_call_target="tpu_custom_call" | custom-call | flops 805306368 | bytes 5767168 | tf_op jit(solution)/shard_map/partial_sums/pallas_call | solution.py:127
  56.3 1.9 %collective-permute-start.12 = (bf16[256,768]{1,0:T(8,128)(2,1)S(1)}, bf16[256,768]{1,0:T(8,128)(2,1)S(1)}, u32[]{:S(2)}, u32[]{:S(2)}) collective-permute-start(bf16[256,768]{1,0:T(8,128)(2,1)S(1)} %collective-permute-done.10.refs_1_), channel_id=1, source_target_pairs={{0,2},{1,3},{2,4},{3,5},{4,6},{5,7},{6,8},{7,9},{8,10},{9,11},{10,... | collective-permute-start | bytes 1179656 | tf_op jit(solution)/shard_map/ppermute | solution.py:303
  58.2 5.1 %collective-permute-start.14 = (bf16[256,768]{1,0:T(8,128)(2,1)S(1)}, bf16[256,768]{1,0:T(8,128)(2,1)S(1)}, u32[]{:S(2)}, u32[]{:S(2)}) collective-permute-start(bf16[256,768]{1,0:T(8,128)(2,1)S(1)} %collective-permute-done.13.refs_2_), channel_id=1, source_target_pairs={{0,14},{1,15},{2,0},{3,1},{4,2},{5,3},{6,4},{7,5},{8,6},{9,7},{10,... | collective-permute-start | bytes 1179656 | tf_op jit(solution)/shard_map/ppermute | solution.py:303
  63.3 4.1 %collective-permute-start.7 = (bf16[256,768]{1,0:T(8,128)(2,1)S(1)}, bf16[256,768]{1,0:T(8,128)(2,1)S(1)}, u32[]{:S(2)}, u32[]{:S(2)}) collective-permute-start(bf16[256,768]{1,0:T(8,128)(2,1)S(1)} %collective-permute-done.6.refs_3_), channel_id=1, source_target_pairs={{0,14},{1,15},{2,0},{3,1},{4,2},{5,3},{6,4},{7,5},{8,6},{9,7},{10,... | collective-permute-start | bytes 1179656 | tf_op jit(solution)/shard_map/ppermute | solution.py:303
  67.4 1.9 %collective-permute-start.3 = (bf16[256,768]{1,0:T(8,128)(2,1)S(1)}, bf16[256,768]{1,0:T(8,128)(2,1)S(1)}, u32[]{:S(2)}, u32[]{:S(2)}) collective-permute-start(bf16[256,768]{1,0:T(8,128)(2,1)S(1)} %collective-permute-done.2.refs_0_), channel_id=1, source_target_pairs={{0,2},{1,3},{2,4},{3,5},{4,6},{5,7},{6,8},{7,9},{8,10},{9,11},{10,... | collective-permute-start | bytes 1179656 | tf_op jit(solution)/shard_map/ppermute | solution.py:303
  69.4 2.2 %partial_sums.8 = (f32[256,768]{1,0:T(8,128)S(1)}, f32[256,768]{1,0:T(8,128)S(1)}) custom-call(bf16[256,768]{1,0:T(8,128)(2,1)S(1)} %collective-permute-done.1.refs_0_, bf16[256,768]{1,0:T(8,128)(2,1)S(1)} %collective-permute-done.10.refs_1_, bf16[256,768]{1,0:T(8,128)(2,1)S(1)} %collective-permute-done.13.refs_2_, ...), custom_call_target="tpu_custom_call" | custom-call | flops 805306368 | bytes 5767168 | tf_op jit(solution)/shard_map/partial_sums/pallas_call | solution.py:127
  73.1 2.2 %partial_sums.9 = (f32[256,768]{1,0:T(8,128)S(1)}, f32[256,768]{1,0:T(8,128)S(1)}) custom-call(bf16[256,768]{1,0:T(8,128)(2,1)S(1)} %collective-permute-done.2.refs_0_, bf16[256,768]{1,0:T(8,128)(2,1)S(1)} %collective-permute-done.12.refs_1_, bf16[256,768]{1,0:T(8,128)(2,1)S(1)} %collective-permute-done.14.refs_2_, ...), custom_call_target="tpu_custom_call" | custom-call | flops 805306368 | bytes 5767168 | tf_op jit(solution)/shard_map/partial_sums/pallas_call | solution.py:127
  75.3 3.4 %collective-permute-done.7.refs_1_ = bf16[256,768]{1,0:T(8,128)(2,1)S(1)} collective-permute-done((bf16[256,768]{1,0:T(8,128)(2,1)S(1)}, bf16[256,768]{1,0:T(8,128)(2,1)S(1)}, u32[]{:S(2)}, u32[]{:S(2)}) %collective-permute-start.7) | collective-permute-done | bytes 393248 | tf_op jit(solution)/shard_map/ppermute | solution.py:303
  78.7 2.1 %collective-permute-done.3.refs_0_ = bf16[256,768]{1,0:T(8,128)(2,1)S(1)} collective-permute-done((bf16[256,768]{1,0:T(8,128)(2,1)S(1)}, bf16[256,768]{1,0:T(8,128)(2,1)S(1)}, u32[]{:S(2)}, u32[]{:S(2)}) %collective-permute-start.3) | collective-permute-done | bytes 393248 | tf_op jit(solution)/shard_map/ppermute | solution.py:303
  81.3 2.1 %collective-permute-start.15 = (f32[256,768]{1,0:T(8,128)S(1)}, f32[256,768]{1,0:T(8,128)S(1)}, u32[]{:S(2)}, u32[]{:S(2)}) collective-permute-start(f32[256,768]{1,0:T(8,128)S(1)} %partial_sums.11), channel_id=1, source_target_pairs={{0,1},{1,0},{2,3},{3,2},{4,5},{5,4},{6,7},{7,6},{8,9},{9,8},{10,11... | collective-permute-start | bytes 2359304 | tf_op jit(solution)/shard_map/ppermute | solution.py:303
  87.4 23.7 %all_to_all.10 = bf16[32,8,640]{2,1,0:T(8,128)(2,1)S(1)} all-to-all(bf16[32,8,640]{2,1,0:T(8,128)(2,1)S(1)} %bitcast.10), channel_id=1, replica_groups=mesh['dp'=32,'fsdp'=16] {'dp'}, dimensions={0} | all-to-all | bytes 655360 | tf_op jit(solution)/shard_map/all_to_all | solution.py:291
  112.3 4.8 %all-to-all-start.1 = ((bf16[32,8,512]{2,1,0:T(8,128)(2,1)}), bf16[32,8,512]{2,1,0:T(8,128)(2,1)S(1)}, u32[]{:S(2)}, u32[]{:S(2)}) async-start(bf16[32,8,512]{2,1,0:T(8,128)(2,1)} %bitcast.3), calls=%async_computation.1 | async-start | bytes 524288 | tf_op jit(solution)/shard_map/all_to_all | solution.py:291
  117.5 11.0 %all-to-all-done.1 = bf16[32,8,512]{2,1,0:T(8,128)(2,1)S(1)} async-done(((bf16[32,8,512]{2,1,0:T(8,128)(2,1)}), bf16[32,8,512]{2,1,0:T(8,128)(2,1)S(1)}, u32[]{:S(2)}, u32[]{:S(2)}) %all-to-all-start.1) | async-done | bytes 262176 | tf_op jit(solution)/shard_map/all_to_all | solution.py:291
  (43 shorter events, 19.9 us)
Async XLA Ops:
  0.0 36.5 %collective-permute-start.9 = (bf16[256,8192]{1,0:T(8,128)(2,1)}, bf16[256,8192]{1,0:T(8,128)(2,1)S(1)}, u32[]{:S(2)}, u32[]{:S(2)}) collective-permute-start(bf16[256,8192]{1,0:T(8,128)(2,1)} %refs_2_.3), channel_id=1, source_target_pairs={{0,1},{1,0},{2,3},{3,2},{4,5},{5,4},{6,7},{7,6},{8,9},{9,8},{10,11... | collective-permute-start | bytes 12582920 | tf_op jit(solution)/shard_map/ppermute | solution.py:303
  5.0 20.0 %collective-permute-start.4 = (bf16[256,768]{1,0:T(8,128)(2,1)S(1)}, bf16[256,768]{1,0:T(8,128)(2,1)S(1)}, u32[]{:S(2)}, u32[]{:S(2)}) collective-permute-start(bf16[256,768]{1,0:T(8,128)(2,1)S(1)} %get-tuple-element.23.refs_1_), channel_id=1, source_target_pairs={{0,14},{1,15},{2,0},{3,1},{4,2},{5,3},{6,4},{7,5},{8,6},{9,7},{10,... | collective-permute-start | bytes 1179656 | tf_op jit(solution)/shard_map/ppermute | solution.py:303
  15.9 15.1 %collective-permute-start = (bf16[256,768]{1,0:T(8,128)(2,1)S(1)}, bf16[256,768]{1,0:T(8,128)(2,1)S(1)}, u32[]{:S(2)}, u32[]{:S(2)}) collective-permute-start(bf16[256,768]{1,0:T(8,128)(2,1)S(1)} %get-tuple-element.21.refs_0_), channel_id=1, source_target_pairs={{0,2},{1,3},{2,4},{3,5},{4,6},{5,7},{6,8},{7,9},{8,10},{9,11},{10,... | collective-permute-start | bytes 1179656 | tf_op jit(solution)/shard_map/ppermute | solution.py:303
  17.8 21.5 %collective-permute-start.8 = (bf16[256,768]{1,0:T(8,128)(2,1)S(1)}, bf16[256,768]{1,0:T(8,128)(2,1)S(1)}, u32[]{:S(2)}, u32[]{:S(2)}) collective-permute-start(bf16[256,768]{1,0:T(8,128)(2,1)S(1)} %get-tuple-element.23.refs_1_), channel_id=1, source_target_pairs={{0,2},{1,3},{2,4},{3,5},{4,6},{5,7},{6,8},{7,9},{8,10},{9,11},{10,... | collective-permute-start | bytes 1179656 | tf_op jit(solution)/shard_map/ppermute | solution.py:303
  19.8 21.5 %collective-permute-start.11 = (bf16[256,768]{1,0:T(8,128)(2,1)S(1)}, bf16[256,768]{1,0:T(8,128)(2,1)S(1)}, u32[]{:S(2)}, u32[]{:S(2)}) collective-permute-start(bf16[256,768]{1,0:T(8,128)(2,1)S(1)} %get-tuple-element.21.refs_0_), channel_id=1, source_target_pairs={{0,14},{1,15},{2,0},{3,1},{4,2},{5,3},{6,4},{7,5},{8,6},{9,7},{10,... | collective-permute-start | bytes 1179656 | tf_op jit(solution)/shard_map/ppermute | solution.py:303
  24.9 21.5 %collective-permute-start.5 = (bf16[256,768]{1,0:T(8,128)(2,1)S(1)}, bf16[256,768]{1,0:T(8,128)(2,1)S(1)}, u32[]{:S(2)}, u32[]{:S(2)}) collective-permute-start(bf16[256,768]{1,0:T(8,128)(2,1)S(1)} %collective-permute-done.4.refs_3_), channel_id=1, source_target_pairs={{0,14},{1,15},{2,0},{3,1},{4,2},{5,3},{6,4},{7,5},{8,6},{9,7},{10,... | collective-permute-start | bytes 1179656 | tf_op jit(solution)/shard_map/ppermute | solution.py:303
  31.0 18.3 %collective-permute-start.1 = (bf16[256,768]{1,0:T(8,128)(2,1)S(1)}, bf16[256,768]{1,0:T(8,128)(2,1)S(1)}, u32[]{:S(2)}, u32[]{:S(2)}) collective-permute-start(bf16[256,768]{1,0:T(8,128)(2,1)S(1)} %collective-permute-done.refs_0_), channel_id=1, source_target_pairs={{0,2},{1,3},{2,4},{3,5},{4,6},{5,7},{6,8},{7,9},{8,10},{9,11},{10,... | collective-permute-start | bytes 1179656 | tf_op jit(solution)/shard_map/ppermute | solution.py:303
  32.9 2.2 %copy-start = (bf16[256,8192]{1,0:T(8,128)(2,1)S(1)}, bf16[256,8192]{1,0:T(8,128)(2,1)}, u32[]{:S(2)}) copy-start(bf16[256,8192]{1,0:T(8,128)(2,1)} %refs_2_.3) | copy-start | bytes 12582916
  35.1 2.2 %copy-start.1 = (bf16[256,8192]{1,0:T(8,128)(2,1)S(1)}, bf16[256,8192]{1,0:T(8,128)(2,1)}, u32[]{:S(2)}) copy-start(bf16[256,8192]{1,0:T(8,128)(2,1)} %refs_2_.3) | copy-start | bytes 12582916
  39.4 16.9 %collective-permute-start.10 = (bf16[256,768]{1,0:T(8,128)(2,1)S(1)}, bf16[256,768]{1,0:T(8,128)(2,1)S(1)}, u32[]{:S(2)}, u32[]{:S(2)}) collective-permute-start(bf16[256,768]{1,0:T(8,128)(2,1)S(1)} %collective-permute-done.8.refs_1_), channel_id=1, source_target_pairs={{0,2},{1,3},{2,4},{3,5},{4,6},{5,7},{6,8},{7,9},{8,10},{9,11},{10,... | collective-permute-start | bytes 1179656 | tf_op jit(solution)/shard_map/ppermute | solution.py:303
  41.3 16.8 %collective-permute-start.13 = (bf16[256,768]{1,0:T(8,128)(2,1)S(1)}, bf16[256,768]{1,0:T(8,128)(2,1)S(1)}, u32[]{:S(2)}, u32[]{:S(2)}) collective-permute-start(bf16[256,768]{1,0:T(8,128)(2,1)S(1)} %collective-permute-done.11.refs_2_), channel_id=1, source_target_pairs={{0,14},{1,15},{2,0},{3,1},{4,2},{5,3},{6,4},{7,5},{8,6},{9,7},{10,... | collective-permute-start | bytes 1179656 | tf_op jit(solution)/shard_map/ppermute | solution.py:303
  46.5 16.8 %collective-permute-start.6 = (bf16[256,768]{1,0:T(8,128)(2,1)S(1)}, bf16[256,768]{1,0:T(8,128)(2,1)S(1)}, u32[]{:S(2)}, u32[]{:S(2)}) collective-permute-start(bf16[256,768]{1,0:T(8,128)(2,1)S(1)} %collective-permute-done.5.refs_3_), channel_id=1, source_target_pairs={{0,14},{1,15},{2,0},{3,1},{4,2},{5,3},{6,4},{7,5},{8,6},{9,7},{10,... | collective-permute-start | bytes 1179656 | tf_op jit(solution)/shard_map/ppermute | solution.py:303
  49.3 18.2 %collective-permute-start.2 = (bf16[256,768]{1,0:T(8,128)(2,1)S(1)}, bf16[256,768]{1,0:T(8,128)(2,1)S(1)}, u32[]{:S(2)}, u32[]{:S(2)}) collective-permute-start(bf16[256,768]{1,0:T(8,128)(2,1)S(1)} %collective-permute-done.1.refs_0_), channel_id=1, source_target_pairs={{0,2},{1,3},{2,4},{3,5},{4,6},{5,7},{6,8},{7,9},{8,10},{9,11},{10,... | collective-permute-start | bytes 1179656 | tf_op jit(solution)/shard_map/ppermute | solution.py:303
  56.3 16.9 %collective-permute-start.12 = (bf16[256,768]{1,0:T(8,128)(2,1)S(1)}, bf16[256,768]{1,0:T(8,128)(2,1)S(1)}, u32[]{:S(2)}, u32[]{:S(2)}) collective-permute-start(bf16[256,768]{1,0:T(8,128)(2,1)S(1)} %collective-permute-done.10.refs_1_), channel_id=1, source_target_pairs={{0,2},{1,3},{2,4},{3,5},{4,6},{5,7},{6,8},{7,9},{8,10},{9,11},{10,... | collective-permute-start | bytes 1179656 | tf_op jit(solution)/shard_map/ppermute | solution.py:303
  58.2 14.9 %collective-permute-start.14 = (bf16[256,768]{1,0:T(8,128)(2,1)S(1)}, bf16[256,768]{1,0:T(8,128)(2,1)S(1)}, u32[]{:S(2)}, u32[]{:S(2)}) collective-permute-start(bf16[256,768]{1,0:T(8,128)(2,1)S(1)} %collective-permute-done.13.refs_2_), channel_id=1, source_target_pairs={{0,14},{1,15},{2,0},{3,1},{4,2},{5,3},{6,4},{7,5},{8,6},{9,7},{10,... | collective-permute-start | bytes 1179656 | tf_op jit(solution)/shard_map/ppermute | solution.py:303
  63.3 15.3 %collective-permute-start.7 = (bf16[256,768]{1,0:T(8,128)(2,1)S(1)}, bf16[256,768]{1,0:T(8,128)(2,1)S(1)}, u32[]{:S(2)}, u32[]{:S(2)}) collective-permute-start(bf16[256,768]{1,0:T(8,128)(2,1)S(1)} %collective-permute-done.6.refs_3_), channel_id=1, source_target_pairs={{0,14},{1,15},{2,0},{3,1},{4,2},{5,3},{6,4},{7,5},{8,6},{9,7},{10,... | collective-permute-start | bytes 1179656 | tf_op jit(solution)/shard_map/ppermute | solution.py:303
  67.4 13.4 %collective-permute-start.3 = (bf16[256,768]{1,0:T(8,128)(2,1)S(1)}, bf16[256,768]{1,0:T(8,128)(2,1)S(1)}, u32[]{:S(2)}, u32[]{:S(2)}) collective-permute-start(bf16[256,768]{1,0:T(8,128)(2,1)S(1)} %collective-permute-done.2.refs_0_), channel_id=1, source_target_pairs={{0,2},{1,3},{2,4},{3,5},{4,6},{5,7},{6,8},{7,9},{8,10},{9,11},{10,... | collective-permute-start | bytes 1179656 | tf_op jit(solution)/shard_map/ppermute | solution.py:303
  81.3 4.4 %copy-start.4 = (f32[128,128]{1,0:T(8,128)S(1)}, f32[128,128]{1,0:T(8,128)}, u32[]{:S(2)}) copy-start(f32[128,128]{1,0:T(8,128)} %constant.10.clone.cosine_ref) | copy-start | bytes 196612
  81.3 4.4 %copy-start.5 = (f32[128,128]{1,0:T(8,128)S(1)}, f32[128,128]{1,0:T(8,128)}, u32[]{:S(2)}) copy-start(f32[128,128]{1,0:T(8,128)} %constant.11.clone.sine_ref) | copy-start | bytes 196612
  81.3 4.4 %copy-start.7 = (s32[4]{0:T(128)S(1)}, s32[4]{0:T(128)}, u32[]{:S(2)}) copy-start(s32[4]{0:T(128)} %lengths_ref.1) | copy-start | bytes 52
  81.3 4.3 %copy-start.8 = (s32[4]{0:T(128)S(1)}, s32[4]{0:T(128)}, u32[]{:S(2)}) copy-start(s32[4]{0:T(128)} %learner_ref.1) | copy-start | bytes 52
  81.3 4.3 %copy-start.9 = (s32[4]{0:T(128)S(1)}, s32[4]{0:T(128)}, u32[]{:S(2)}) copy-start(s32[4]{0:T(128)} %offset_ref.1) | copy-start | bytes 52
  81.3 4.3 %collective-permute-start.15 = (f32[256,768]{1,0:T(8,128)S(1)}, f32[256,768]{1,0:T(8,128)S(1)}, u32[]{:S(2)}, u32[]{:S(2)}) collective-permute-start(f32[256,768]{1,0:T(8,128)S(1)} %partial_sums.11), channel_id=1, source_target_pairs={{0,1},{1,0},{2,3},{3,2},{4,5},{5,4},{6,7},{7,6},{8,9},{9,8},{10,11... | collective-permute-start | bytes 2359304 | tf_op jit(solution)/shard_map/ppermute | solution.py:303
  112.3 16.2 %all-to-all-start.1 = ((bf16[32,8,512]{2,1,0:T(8,128)(2,1)}), bf16[32,8,512]{2,1,0:T(8,128)(2,1)S(1)}, u32[]{:S(2)}, u32[]{:S(2)}) async-start(bf16[32,8,512]{2,1,0:T(8,128)(2,1)} %bitcast.3), calls=%async_computation.1 | async-start | bytes 524288 | tf_op jit(solution)/shard_map/all_to_all | solution.py:291
  (3 other events, 2.7 us)

commit v9 on v8

--- a/solution.py
+++ b/solution.py
@@ -25,28 +25,54 @@
 SMEM = pl.BlockSpec(memory_space=pltpu.SMEM)
 
 
-def fold_kernel(gain_ref, query_ref, keyval_ref, *out_refs):
-    rows = out_refs[0].shape[0]
+def fold_kernel(gain_hbm, query_hbm, keyval_hbm, *refs):
+    (*outs_hbm, gain_ref, query_ref, keyval_ref, folded, arrived, left) = refs
+    copies = [
+        pltpu.make_async_copy(source, target, arrived.at[i])
+        for i, (source, target) in enumerate(
+            zip((gain_hbm, query_hbm, keyval_hbm), (gain_ref, query_ref, keyval_ref))
+        )
+    ]
+    for copy in copies:
+        copy.start()
+    for copy in copies:
+        copy.wait()
+    rows = folded.shape[1]
     row = lax.broadcasted_iota(jnp.int32, (rows, rows), 0)
     column = lax.broadcasted_iota(jnp.int32, (rows, rows), 1)
-    for i, out_ref in enumerate(out_refs):
+    copies = []
+    for i, out_hbm in enumerate(outs_hbm):
         own = slice(i * rows, (i + 1) * rows)
         gain = gain_ref[own].astype(f32).reshape(1, rows)
         gain = jnp.where(row == column, gain, 0.0).astype(bf16)
         query = jnp.dot(gain, query_ref[own, :], preferred_element_type=f32)
         keyval = jnp.dot(gain, keyval_ref[own, :], preferred_element_type=f32)
-        out_ref[:, : QH * HD] = query.astype(bf16)
-        out_ref[:, QH * HD :] = keyval.astype(bf16)
+        folded[i, :, : QH * HD] = query.astype(bf16)
+        folded[i, :, QH * HD :] = keyval.astype(bf16)
+        copies.append(pltpu.make_async_copy(folded.at[i], out_hbm, left.at[i]))
+        copies[-1].start()
+    for copy in copies:
+        copy.wait()
 
 
 def fold(gain, query_weight, keyval_weight):
-    half = jax.ShapeDtypeStruct((gain.shape[0] // 2, WIDE), bf16)
+    depth = gain.shape[0]
+    half = jax.ShapeDtypeStruct((depth // 2, WIDE), bf16)
+    anywhere = pl.BlockSpec(memory_space=pl.ANY)
     return pl.pallas_call(
         fold_kernel,
         out_shape=[half] * 2,
-        in_specs=[VMEM] * 3,
-        out_specs=[VMEM] * 2,
-        compiler_params=pltpu.CompilerParams(vmem_limit_bytes=16 << 20),
+        in_specs=[anywhere] * 3,
+        out_specs=[anywhere] * 2,
+        scratch_shapes=[
+            pltpu.VMEM(gain.shape, bf16),
+            pltpu.VMEM(query_weight.shape, bf16),
+            pltpu.VMEM(keyval_weight.shape, bf16),
+            pltpu.VMEM((2, depth // 2, WIDE), bf16),
+            pltpu.SemaphoreType.DMA((3,)),
+            pltpu.SemaphoreType.DMA((2,)),
+        ],
+        compiler_params=pltpu.CompilerParams(vmem_limit_bytes=60 << 20),
         name="fold_gain",
     )(gain, query_weight, keyval_weight)
 
@@ -306,29 +332,28 @@
         return lax.optimization_barrier((value, *others))[0]
 
     held = fold(norm_gain, query_weight, keyval_weight)
-    got = send(hidden, swap)
-    both = (hidden, got)
+    both = (hidden, send(hidden, swap))
     above, below = list(held), list(held)
+    sums = None
     for step in range(1, ring // 2):
         near = (above, below)
         above = [send(w, up) for w in above]
         below = [send(w, down) for w in below]
         if step == 1:
-            sums = partial([(0, (held[0], after(held[1], above[0])))], both, None)
             inverse = inverses(after(hidden, above[0]))
-            above[1] = after(above[1], *sums, inverse)
+            above[1] = after(above[1], inverse)
         else:
             blocks = [(1 - step, near[0]), (step - 1, near[1])]
             sums = partial(blocks, both, sums)
             if step == 2:
                 above[1] = after(above[1], *sums)
     far = [send(above[0], up), send(below[1], down)]
-    last = step
-    sums = partial([(-last, (above[0], after(above[1], *sums))), (last, below)], both, sums)
+    blocks = [(-step, (above[0], after(above[1], *sums))), (step, below), (0, held)]
+    sums = partial(blocks, both, sums)
     far[1] = after(far[1], *sums)
-    [other] = partial([(ring // 2, far)], (got,), sums[1:])
+    [other] = partial([(ring // 2, far)], both[1:], sums[1:])
     other = send(other, swap)
-    [mine] = partial([(ring // 2, far)], (hidden,), sums[:1])
+    [mine] = partial([(ring // 2, far)], both[:1], sums[:1])
     mixed = attend(lengths, learner, slot_offset, mine, other, inverse, *rotary())
     spread = exchange(mixed)
     landed = exchange(arrange(spread))

time: 130 us -> 131 us (level)
  local copies, waits for them, and re-layouts: 5.61 us -> 2.23 us
  Pallas kernels: 13.7 us -> 16.4 us
    unnamed x20 -> x18, local copies, waits for them, and re-layouts: 5.61 us -> 2.23 us
    pallas_call x1, Pallas kernels: 0.37 us -> 2.36 us  [fold(): pl.pallas_call(fold_kernel, out_shape=[half] * 2, in_specs=[anywhere] * 3...]
    pallas_call x6 -> x5, Pallas kernels: 8.53 us -> 9.2 us  [partial(): pl.pallas_call(functools.partial(partial_kernel, [d for d, _ in blocks],...]
  transfers between devices with their start and end apart: 17 -> 17, of which waited for: 8 -> 9; matrix products, arithmetic and copies ran while one was open for 0% -> 0% of each run, Pallas kernels for 8% -> 9%
where the time goes in v9:
time: 131 us; the launch traced here: 130 us
  starting transfers between devices  62 us (47%)
  waiting for transfers between devices  24.3 us (19%)
  blocking collectives  23.7 us (18%)
  Pallas kernels  16.4 us (13%)
  local copies, waits for them, and re-layouts  2.23 us (2%)
    ppermute x16, starting transfers between devices, send(): return lax.ppermute(values, 'fsdp', pairs)  57.2 us
    all_to_all x1, blocking collectives, exchange(): lax.all_to_all(blocks, 'dp', split_axis=0, concat_axis=0, tiled=True)  23.7 us
    ppermute x16, waiting for transfers between devices, send(): return lax.ppermute(values, 'fsdp', pairs)  13.4 us
    all_to_all x1, waiting for transfers between devices, exchange(): lax.all_to_all(blocks, 'dp', split_axis=0, concat_axis=0, tiled=True)  10.9 us
    pallas_call x5, Pallas kernels, partial(): pl.pallas_call(functools.partial(partial_kernel, [d for d, _ in blocks],...  9.2 us
    all_to_all x1, starting transfers between devices, exchange(): lax.all_to_all(blocks, 'dp', split_axis=0, concat_axis=0, tiled=True)  4.77 us
  transfers between devices with their start and end apart: 17, of which 9 were waited for; matrix products, arithmetic and copies ran while one was open for 0% of the time, Pallas kernels for 9%

profile of v9, /device:TPU:8, one launch (start us, length us, event | category | flops | bytes accessed | tf_op | source)
XLA Modules:
  0.0 129.8 jit_solution(13760944172606901649)
XLA Ops:
  1.9 2.4 %fold_gain.1 = (bf16[256,768]{1,0:T(8,128)(2,1)}, bf16[256,768]{1,0:T(8,128)(2,1)}) custom-call(bf16[512]{0:T(512)(128)(2,1)} %gain_hbm.1, bf16[512,512]{1,0:T(8,128)(2,1)} %query_hbm.1, bf16[512,256]{1,0:T(8,128)(2,1)} %keyval_hbm.1), custom_call_target="tpu_custom_call" | custom-call | tf_op jit(solution)/shard_map/fold_gain/pallas_call | solution.py:62
  4.3 10.9 %collective-permute-start.4 = (bf16[256,768]{1,0:T(8,128)(2,1)}, bf16[256,768]{1,0:T(8,128)(2,1)S(1)}, u32[]{:S(2)}, u32[]{:S(2)}) collective-permute-start(bf16[256,768]{1,0:T(8,128)(2,1)} %get-tuple-element.19.refs_5_), channel_id=1, source_target_pairs={{0,14},{1,15},{2,0},{3,1},{4,2},{5,3},{6,4},{7,5},{8,6},{9,7},{10,... | collective-permute-start | bytes 1179656 | tf_op jit(solution)/shard_map/ppermute | solution.py:329
  15.2 1.9 %collective-permute-start = (bf16[256,768]{1,0:T(8,128)(2,1)}, bf16[256,768]{1,0:T(8,128)(2,1)S(1)}, u32[]{:S(2)}, u32[]{:S(2)}) collective-permute-start(bf16[256,768]{1,0:T(8,128)(2,1)} %get-tuple-element.18.refs_4_), channel_id=1, source_target_pairs={{0,2},{1,3},{2,4},{3,5},{4,6},{5,7},{6,8},{7,9},{8,10},{9,11},{10,... | collective-permute-start | bytes 1179656 | tf_op jit(solution)/shard_map/ppermute | solution.py:329
  17.2 1.9 %collective-permute-start.8 = (bf16[256,768]{1,0:T(8,128)(2,1)}, bf16[256,768]{1,0:T(8,128)(2,1)S(1)}, u32[]{:S(2)}, u32[]{:S(2)}) collective-permute-start(bf16[256,768]{1,0:T(8,128)(2,1)} %get-tuple-element.19.refs_5_), channel_id=1, source_target_pairs={{0,2},{1,3},{2,4},{3,5},{4,6},{5,7},{6,8},{7,9},{8,10},{9,11},{10,... | collective-permute-start | bytes 1179656 | tf_op jit(solution)/shard_map/ppermute | solution.py:329
  19.1 5.1 %collective-permute-start.10 = (bf16[256,768]{1,0:T(8,128)(2,1)}, bf16[256,768]{1,0:T(8,128)(2,1)S(1)}, u32[]{:S(2)}, u32[]{:S(2)}) collective-permute-start(bf16[256,768]{1,0:T(8,128)(2,1)} %get-tuple-element.18.refs_4_), channel_id=1, source_target_pairs={{0,14},{1,15},{2,0},{3,1},{4,2},{5,3},{6,4},{7,5},{8,6},{9,7},{10,... | collective-permute-start | bytes 1179656 | tf_op jit(solution)/shard_map/ppermute | solution.py:329
  24.6 5.5 %collective-permute-start.5 = (bf16[256,768]{1,0:T(8,128)(2,1)S(1)}, bf16[256,768]{1,0:T(8,128)(2,1)S(1)}, u32[]{:S(2)}, u32[]{:S(2)}) collective-permute-start(bf16[256,768]{1,0:T(8,128)(2,1)S(1)} %collective-permute-done.4.refs_3_), channel_id=1, source_target_pairs={{0,14},{1,15},{2,0},{3,1},{4,2},{5,3},{6,4},{7,5},{8,6},{9,7},{10,... | collective-permute-start | bytes 1179656 | tf_op jit(solution)/shard_map/ppermute | solution.py:329
  32.4 2.2 %copy-done = bf16[256,8192]{1,0:T(8,128)(2,1)S(1)} copy-done((bf16[256,8192]{1,0:T(8,128)(2,1)S(1)}, bf16[256,8192]{1,0:T(8,128)(2,1)}, u32[]{:S(2)}) %copy-start) | copy-done | bytes 4194328
  36.1 2.9 %collective-permute-done.8.refs_1_ = bf16[256,768]{1,0:T(8,128)(2,1)S(1)} collective-permute-done((bf16[256,768]{1,0:T(8,128)(2,1)}, bf16[256,768]{1,0:T(8,128)(2,1)S(1)}, u32[]{:S(2)}, u32[]{:S(2)}) %collective-permute-start.8) | collective-permute-done | bytes 393248 | tf_op jit(solution)/shard_map/ppermute | solution.py:329
  40.9 5.1 %collective-permute-start.13 = (bf16[256,768]{1,0:T(8,128)(2,1)S(1)}, bf16[256,768]{1,0:T(8,128)(2,1)S(1)}, u32[]{:S(2)}, u32[]{:S(2)}) collective-permute-start(bf16[256,768]{1,0:T(8,128)(2,1)S(1)} %collective-permute-done.10.refs_2_), channel_id=1, source_target_pairs={{0,14},{1,15},{2,0},{3,1},{4,2},{5,3},{6,4},{7,5},{8,6},{9,7},{10,... | collective-permute-start | bytes 1179656 | tf_op jit(solution)/shard_map/ppermute | solution.py:329
  46.0 1.9 %collective-permute-start.6 = (bf16[256,768]{1,0:T(8,128)(2,1)S(1)}, bf16[256,768]{1,0:T(8,128)(2,1)S(1)}, u32[]{:S(2)}, u32[]{:S(2)}) collective-permute-start(bf16[256,768]{1,0:T(8,128)(2,1)S(1)} %collective-permute-done.5.refs_3_), channel_id=1, source_target_pairs={{0,14},{1,15},{2,0},{3,1},{4,2},{5,3},{6,4},{7,5},{8,6},{9,7},{10,... | collective-permute-start | bytes 1179656 | tf_op jit(solution)/shard_map/ppermute | solution.py:329
  48.0 3.9 %collective-permute-start.2 = (bf16[256,768]{1,0:T(8,128)(2,1)S(1)}, bf16[256,768]{1,0:T(8,128)(2,1)S(1)}, u32[]{:S(2)}, u32[]{:S(2)}) collective-permute-start(bf16[256,768]{1,0:T(8,128)(2,1)S(1)} %collective-permute-done.1.refs_0_), channel_id=1, source_target_pairs={{0,2},{1,3},{2,4},{3,5},{4,6},{5,7},{6,8},{7,9},{8,10},{9,11},{10,... | collective-permute-start | bytes 1179656 | tf_op jit(solution)/shard_map/ppermute | solution.py:329
  51.9 2.1 %partial_sums.5 = (f32[256,768]{1,0:T(8,128)S(1)}, f32[256,768]{1,0:T(8,128)S(1)}) custom-call(bf16[256,768]{1,0:T(8,128)(2,1)S(1)} %collective-permute-done.refs_0_, bf16[256,768]{1,0:T(8,128)(2,1)S(1)} %collective-permute-done.8.refs_1_, bf16[256,768]{1,0:T(8,128)(2,1)S(1)} %collective-permute-done.10.refs_2_, ...), custom_call_target="tpu_custom_call" | custom-call | flops 805306368 | bytes 5767168 | tf_op jit(solution)/shard_map/partial_sums/pallas_call | solution.py:153
  55.8 2.0 %collective-permute-start.12 = (bf16[256,768]{1,0:T(8,128)(2,1)S(1)}, bf16[256,768]{1,0:T(8,128)(2,1)S(1)}, u32[]{:S(2)}, u32[]{:S(2)}) collective-permute-start(bf16[256,768]{1,0:T(8,128)(2,1)S(1)} %collective-permute-done.9.refs_1_), channel_id=1, source_target_pairs={{0,2},{1,3},{2,4},{3,5},{4,6},{5,7},{6,8},{7,9},{8,10},{9,11},{10,... | collective-permute-start | bytes 1179656 | tf_op jit(solution)/shard_map/ppermute | solution.py:329
  57.9 5.1 %collective-permute-start.14 = (bf16[256,768]{1,0:T(8,128)(2,1)S(1)}, bf16[256,768]{1,0:T(8,128)(2,1)S(1)}, u32[]{:S(2)}, u32[]{:S(2)}) collective-permute-start(bf16[256,768]{1,0:T(8,128)(2,1)S(1)} %collective-permute-done.13.refs_2_), channel_id=1, source_target_pairs={{0,14},{1,15},{2,0},{3,1},{4,2},{5,3},{6,4},{7,5},{8,6},{9,7},{10,... | collective-permute-start | bytes 1179656 | tf_op jit(solution)/shard_map/ppermute | solution.py:329
  63.0 3.9 %collective-permute-start.7 = (bf16[256,768]{1,0:T(8,128)(2,1)S(1)}, bf16[256,768]{1,0:T(8,128)(2,1)S(1)}, u32[]{:S(2)}, u32[]{:S(2)}) collective-permute-start(bf16[256,768]{1,0:T(8,128)(2,1)S(1)} %collective-permute-done.6.refs_3_), channel_id=1, source_target_pairs={{0,14},{1,15},{2,0},{3,1},{4,2},{5,3},{6,4},{7,5},{8,6},{9,7},{10,... | collective-permute-start | bytes 1179656 | tf_op jit(solution)/shard_map/ppermute | solution.py:329
  67.0 1.9 %collective-permute-start.3 = (bf16[256,768]{1,0:T(8,128)(2,1)S(1)}, bf16[256,768]{1,0:T(8,128)(2,1)S(1)}, u32[]{:S(2)}, u32[]{:S(2)}) collective-permute-start(bf16[256,768]{1,0:T(8,128)(2,1)S(1)} %collective-permute-done.2.refs_0_), channel_id=1, source_target_pairs={{0,2},{1,3},{2,4},{3,5},{4,6},{5,7},{6,8},{7,9},{8,10},{9,11},{10,... | collective-permute-start | bytes 1179656 | tf_op jit(solution)/shard_map/ppermute | solution.py:329
  68.9 2.2 %partial_sums.6 = (f32[256,768]{1,0:T(8,128)S(1)}, f32[256,768]{1,0:T(8,128)S(1)}) custom-call(bf16[256,768]{1,0:T(8,128)(2,1)S(1)} %collective-permute-done.1.refs_0_, bf16[256,768]{1,0:T(8,128)(2,1)S(1)} %collective-permute-done.9.refs_1_, bf16[256,768]{1,0:T(8,128)(2,1)S(1)} %collective-permute-done.13.refs_2_, ...), custom_call_target="tpu_custom_call" | custom-call | flops 805306368 | bytes 5767168 | tf_op jit(solution)/shard_map/partial_sums/pallas_call | solution.py:153
  72.7 3.1 %partial_sums.7 = (f32[256,768]{1,0:T(8,128)S(1)}, f32[256,768]{1,0:T(8,128)S(1)}) custom-call(bf16[256,768]{1,0:T(8,128)(2,1)S(1)} %collective-permute-done.2.refs_0_, bf16[256,768]{1,0:T(8,128)(2,1)S(1)} %collective-permute-done.12.refs_1_, bf16[256,768]{1,0:T(8,128)(2,1)S(1)} %collective-permute-done.14.refs_2_, ...), custom_call_target="tpu_custom_call" | custom-call | flops 1207959552 | bytes 7077888 | tf_op jit(solution)/shard_map/partial_sums/pallas_call | solution.py:153
  75.8 2.6 %collective-permute-done.7.refs_1_ = bf16[256,768]{1,0:T(8,128)(2,1)S(1)} collective-permute-done((bf16[256,768]{1,0:T(8,128)(2,1)S(1)}, bf16[256,768]{1,0:T(8,128)(2,1)S(1)}, u32[]{:S(2)}, u32[]{:S(2)}) %collective-permute-start.7) | collective-permute-done | bytes 393248 | tf_op jit(solution)/shard_map/ppermute | solution.py:329
  78.3 2.0 %collective-permute-done.3.refs_0_ = bf16[256,768]{1,0:T(8,128)(2,1)S(1)} collective-permute-done((bf16[256,768]{1,0:T(8,128)(2,1)S(1)}, bf16[256,768]{1,0:T(8,128)(2,1)S(1)}, u32[]{:S(2)}, u32[]{:S(2)}) %collective-permute-start.3) | collective-permute-done | bytes 393248 | tf_op jit(solution)/shard_map/ppermute | solution.py:329
  81.8 2.1 %collective-permute-start.15 = (f32[256,768]{1,0:T(8,128)S(1)}, f32[256,768]{1,0:T(8,128)S(1)}, u32[]{:S(2)}, u32[]{:S(2)}) collective-permute-start(f32[256,768]{1,0:T(8,128)S(1)} %partial_sums.9), channel_id=1, source_target_pairs={{0,1},{1,0},{2,3},{3,2},{4,5},{5,4},{6,7},{7,6},{8,9},{9,8},{10,11... | collective-permute-start | bytes 2359304 | tf_op jit(solution)/shard_map/ppermute | solution.py:329
  87.9 23.7 %all_to_all.10 = bf16[32,8,640]{2,1,0:T(8,128)(2,1)S(1)} all-to-all(bf16[32,8,640]{2,1,0:T(8,128)(2,1)S(1)} %bitcast.10), channel_id=1, replica_groups=mesh['dp'=32,'fsdp'=16] {'dp'}, dimensions={0} | all-to-all | bytes 655360 | tf_op jit(solution)/shard_map/all_to_all | solution.py:317
  112.7 4.8 %all-to-all-start.1 = ((bf16[32,8,512]{2,1,0:T(8,128)(2,1)}), bf16[32,8,512]{2,1,0:T(8,128)(2,1)S(1)}, u32[]{:S(2)}, u32[]{:S(2)}) async-start(bf16[32,8,512]{2,1,0:T(8,128)(2,1)} %bitcast.3), calls=%async_computation.1 | async-start | bytes 524288 | tf_op jit(solution)/shard_map/all_to_all | solution.py:317
  118.0 10.9 %all-to-all-done.1 = bf16[32,8,512]{2,1,0:T(8,128)(2,1)S(1)} async-done(((bf16[32,8,512]{2,1,0:T(8,128)(2,1)}), bf16[32,8,512]{2,1,0:T(8,128)(2,1)S(1)}, u32[]{:S(2)}, u32[]{:S(2)}) %all-to-all-start.1) | async-done | bytes 262176 | tf_op jit(solution)/shard_map/all_to_all | solution.py:317
  (40 shorter events, 19.2 us)
Async XLA Ops:
  0.0 51.9 %collective-permute-start.11 = (bf16[256,8192]{1,0:T(8,128)(2,1)}, bf16[256,8192]{1,0:T(8,128)(2,1)}, u32[]{:S(2)}, u32[]{:S(2)}) collective-permute-start(bf16[256,8192]{1,0:T(8,128)(2,1)} %refs_2_.1), channel_id=1, source_target_pairs={{0,1},{1,0},{2,3},{3,2},{4,5},{5,4},{6,7},{7,6},{8,9},{9,8},{10,11... | collective-permute-start | bytes 12582920 | tf_op jit(solution)/shard_map/ppermute | solution.py:329
  4.3 20.3 %collective-permute-start.4 = (bf16[256,768]{1,0:T(8,128)(2,1)}, bf16[256,768]{1,0:T(8,128)(2,1)S(1)}, u32[]{:S(2)}, u32[]{:S(2)}) collective-permute-start(bf16[256,768]{1,0:T(8,128)(2,1)} %get-tuple-element.19.refs_5_), channel_id=1, source_target_pairs={{0,14},{1,15},{2,0},{3,1},{4,2},{5,3},{6,4},{7,5},{8,6},{9,7},{10,... | collective-permute-start | bytes 1179656 | tf_op jit(solution)/shard_map/ppermute | solution.py:329
  15.2 15.3 %collective-permute-start = (bf16[256,768]{1,0:T(8,128)(2,1)}, bf16[256,768]{1,0:T(8,128)(2,1)S(1)}, u32[]{:S(2)}, u32[]{:S(2)}) collective-permute-start(bf16[256,768]{1,0:T(8,128)(2,1)} %get-tuple-element.18.refs_4_), channel_id=1, source_target_pairs={{0,2},{1,3},{2,4},{3,5},{4,6},{5,7},{6,8},{7,9},{8,10},{9,11},{10,... | collective-permute-start | bytes 1179656 | tf_op jit(solution)/shard_map/ppermute | solution.py:329
  17.2 21.8 %collective-permute-start.8 = (bf16[256,768]{1,0:T(8,128)(2,1)}, bf16[256,768]{1,0:T(8,128)(2,1)S(1)}, u32[]{:S(2)}, u32[]{:S(2)}) collective-permute-start(bf16[256,768]{1,0:T(8,128)(2,1)} %get-tuple-element.19.refs_5_), channel_id=1, source_target_pairs={{0,2},{1,3},{2,4},{3,5},{4,6},{5,7},{6,8},{7,9},{8,10},{9,11},{10,... | collective-permute-start | bytes 1179656 | tf_op jit(solution)/shard_map/ppermute | solution.py:329
  19.1 21.8 %collective-permute-start.10 = (bf16[256,768]{1,0:T(8,128)(2,1)}, bf16[256,768]{1,0:T(8,128)(2,1)S(1)}, u32[]{:S(2)}, u32[]{:S(2)}) collective-permute-start(bf16[256,768]{1,0:T(8,128)(2,1)} %get-tuple-element.18.refs_4_), channel_id=1, source_target_pairs={{0,14},{1,15},{2,0},{3,1},{4,2},{5,3},{6,4},{7,5},{8,6},{9,7},{10,... | collective-permute-start | bytes 1179656 | tf_op jit(solution)/shard_map/ppermute | solution.py:329
  24.6 21.4 %collective-permute-start.5 = (bf16[256,768]{1,0:T(8,128)(2,1)S(1)}, bf16[256,768]{1,0:T(8,128)(2,1)S(1)}, u32[]{:S(2)}, u32[]{:S(2)}) collective-permute-start(bf16[256,768]{1,0:T(8,128)(2,1)S(1)} %collective-permute-done.4.refs_3_), channel_id=1, source_target_pairs={{0,14},{1,15},{2,0},{3,1},{4,2},{5,3},{6,4},{7,5},{8,6},{9,7},{10,... | collective-permute-start | bytes 1179656 | tf_op jit(solution)/shard_map/ppermute | solution.py:329
  30.5 17.4 %collective-permute-start.1 = (bf16[256,768]{1,0:T(8,128)(2,1)S(1)}, bf16[256,768]{1,0:T(8,128)(2,1)S(1)}, u32[]{:S(2)}, u32[]{:S(2)}) collective-permute-start(bf16[256,768]{1,0:T(8,128)(2,1)S(1)} %collective-permute-done.refs_0_), channel_id=1, source_target_pairs={{0,2},{1,3},{2,4},{3,5},{4,6},{5,7},{6,8},{7,9},{8,10},{9,11},{10,... | collective-permute-start | bytes 1179656 | tf_op jit(solution)/shard_map/ppermute | solution.py:329
  34.6 17.3 %copy-start.1 = (bf16[256,8192]{1,0:T(8,128)(2,1)S(1)}, bf16[256,8192]{1,0:T(8,128)(2,1)}, u32[]{:S(2)}) copy-start(bf16[256,8192]{1,0:T(8,128)(2,1)} %refs_2_.1) | copy-start | bytes 12582916
  38.9 16.9 %collective-permute-start.9 = (bf16[256,768]{1,0:T(8,128)(2,1)S(1)}, bf16[256,768]{1,0:T(8,128)(2,1)S(1)}, u32[]{:S(2)}, u32[]{:S(2)}) collective-permute-start(bf16[256,768]{1,0:T(8,128)(2,1)S(1)} %collective-permute-done.8.refs_1_), channel_id=1, source_target_pairs={{0,2},{1,3},{2,4},{3,5},{4,6},{5,7},{6,8},{7,9},{8,10},{9,11},{10,... | collective-permute-start | bytes 1179656 | tf_op jit(solution)/shard_map/ppermute | solution.py:329
  40.9 17.0 %collective-permute-start.13 = (bf16[256,768]{1,0:T(8,128)(2,1)S(1)}, bf16[256,768]{1,0:T(8,128)(2,1)S(1)}, u32[]{:S(2)}, u32[]{:S(2)}) collective-permute-start(bf16[256,768]{1,0:T(8,128)(2,1)S(1)} %collective-permute-done.10.refs_2_), channel_id=1, source_target_pairs={{0,14},{1,15},{2,0},{3,1},{4,2},{5,3},{6,4},{7,5},{8,6},{9,7},{10,... | collective-permute-start | bytes 1179656 | tf_op jit(solution)/shard_map/ppermute | solution.py:329
  46.0 17.0 %collective-permute-start.6 = (bf16[256,768]{1,0:T(8,128)(2,1)S(1)}, bf16[256,768]{1,0:T(8,128)(2,1)S(1)}, u32[]{:S(2)}, u32[]{:S(2)}) collective-permute-start(bf16[256,768]{1,0:T(8,128)(2,1)S(1)} %collective-permute-done.5.refs_3_), channel_id=1, source_target_pairs={{0,14},{1,15},{2,0},{3,1},{4,2},{5,3},{6,4},{7,5},{8,6},{9,7},{10,... | collective-permute-start | bytes 1179656 | tf_op jit(solution)/shard_map/ppermute | solution.py:329
  48.0 19.0 %collective-permute-start.2 = (bf16[256,768]{1,0:T(8,128)(2,1)S(1)}, bf16[256,768]{1,0:T(8,128)(2,1)S(1)}, u32[]{:S(2)}, u32[]{:S(2)}) collective-permute-start(bf16[256,768]{1,0:T(8,128)(2,1)S(1)} %collective-permute-done.1.refs_0_), channel_id=1, source_target_pairs={{0,2},{1,3},{2,4},{3,5},{4,6},{5,7},{6,8},{7,9},{8,10},{9,11},{10,... | collective-permute-start | bytes 1179656 | tf_op jit(solution)/shard_map/ppermute | solution.py:329
  55.8 16.9 %copy-start.2 = (bf16[256,768]{1,0:T(8,128)(2,1)S(1)}, bf16[256,768]{1,0:T(8,128)(2,1)}, u32[]{:S(2)}) copy-start(bf16[256,768]{1,0:T(8,128)(2,1)} %get-tuple-element.18.refs_4_) | copy-start | bytes 1179652
  55.8 16.9 %copy-start.3 = (bf16[256,768]{1,0:T(8,128)(2,1)S(1)}, bf16[256,768]{1,0:T(8,128)(2,1)}, u32[]{:S(2)}) copy-start(bf16[256,768]{1,0:T(8,128)(2,1)} %get-tuple-element.19.refs_5_) | copy-start | bytes 1179652
  55.8 16.8 %collective-permute-start.12 = (bf16[256,768]{1,0:T(8,128)(2,1)S(1)}, bf16[256,768]{1,0:T(8,128)(2,1)S(1)}, u32[]{:S(2)}, u32[]{:S(2)}) collective-permute-start(bf16[256,768]{1,0:T(8,128)(2,1)S(1)} %collective-permute-done.9.refs_1_), channel_id=1, source_target_pairs={{0,2},{1,3},{2,4},{3,5},{4,6},{5,7},{6,8},{7,9},{8,10},{9,11},{10,... | collective-permute-start | bytes 1179656 | tf_op jit(solution)/shard_map/ppermute | solution.py:329
  57.9 14.8 %collective-permute-start.14 = (bf16[256,768]{1,0:T(8,128)(2,1)S(1)}, bf16[256,768]{1,0:T(8,128)(2,1)S(1)}, u32[]{:S(2)}, u32[]{:S(2)}) collective-permute-start(bf16[256,768]{1,0:T(8,128)(2,1)S(1)} %collective-permute-done.13.refs_2_), channel_id=1, source_target_pairs={{0,14},{1,15},{2,0},{3,1},{4,2},{5,3},{6,4},{7,5},{8,6},{9,7},{10,... | collective-permute-start | bytes 1179656 | tf_op jit(solution)/shard_map/ppermute | solution.py:329
  63.0 15.3 %collective-permute-start.7 = (bf16[256,768]{1,0:T(8,128)(2,1)S(1)}, bf16[256,768]{1,0:T(8,128)(2,1)S(1)}, u32[]{:S(2)}, u32[]{:S(2)}) collective-permute-start(bf16[256,768]{1,0:T(8,128)(2,1)S(1)} %collective-permute-done.6.refs_3_), channel_id=1, source_target_pairs={{0,14},{1,15},{2,0},{3,1},{4,2},{5,3},{6,4},{7,5},{8,6},{9,7},{10,... | collective-permute-start | bytes 1179656 | tf_op jit(solution)/shard_map/ppermute | solution.py:329
  67.0 13.4 %collective-permute-start.3 = (bf16[256,768]{1,0:T(8,128)(2,1)S(1)}, bf16[256,768]{1,0:T(8,128)(2,1)S(1)}, u32[]{:S(2)}, u32[]{:S(2)}) collective-permute-start(bf16[256,768]{1,0:T(8,128)(2,1)S(1)} %collective-permute-done.2.refs_0_), channel_id=1, source_target_pairs={{0,2},{1,3},{2,4},{3,5},{4,6},{5,7},{6,8},{7,9},{8,10},{9,11},{10,... | collective-permute-start | bytes 1179656 | tf_op jit(solution)/shard_map/ppermute | solution.py:329
  81.7 4.4 %copy-start.4 = (f32[128,128]{1,0:T(8,128)S(1)}, f32[128,128]{1,0:T(8,128)}, u32[]{:S(2)}) copy-start(f32[128,128]{1,0:T(8,128)} %constant.10.clone.cosine_ref) | copy-start | bytes 196612
  81.7 4.4 %copy-start.5 = (f32[128,128]{1,0:T(8,128)S(1)}, f32[128,128]{1,0:T(8,128)}, u32[]{:S(2)}) copy-start(f32[128,128]{1,0:T(8,128)} %constant.11.clone.sine_ref) | copy-start | bytes 196612
  81.7 4.4 %copy-start.6 = (s32[4]{0:T(128)S(1)}, s32[4]{0:T(128)}, u32[]{:S(2)}) copy-start(s32[4]{0:T(128)} %lengths_ref.1) | copy-start | bytes 52
  81.8 4.3 %copy-start.7 = (s32[4]{0:T(128)S(1)}, s32[4]{0:T(128)}, u32[]{:S(2)}) copy-start(s32[4]{0:T(128)} %learner_ref.1) | copy-start | bytes 52
  81.8 4.3 %collective-permute-start.15 = (f32[256,768]{1,0:T(8,128)S(1)}, f32[256,768]{1,0:T(8,128)S(1)}, u32[]{:S(2)}, u32[]{:S(2)}) collective-permute-start(f32[256,768]{1,0:T(8,128)S(1)} %partial_sums.9), channel_id=1, source_target_pairs={{0,1},{1,0},{2,3},{3,2},{4,5},{5,4},{6,7},{7,6},{8,9},{9,8},{10,11... | collective-permute-start | bytes 2359304 | tf_op jit(solution)/shard_map/ppermute | solution.py:329
  112.7 16.2 %all-to-all-start.1 = ((bf16[32,8,512]{2,1,0:T(8,128)(2,1)}), bf16[32,8,512]{2,1,0:T(8,128)(2,1)S(1)}, u32[]{:S(2)}, u32[]{:S(2)}) async-start(bf16[32,8,512]{2,1,0:T(8,128)(2,1)} %bitcast.3), calls=%async_computation.1 | async-start | bytes 524288 | tf_op jit(solution)/shard_map/all_to_all | solution.py:317
  (2 other events, 6.5 us)

commit v10 on v8

--- a/solution.py
+++ b/solution.py
@@ -115,10 +115,10 @@
                     preferred_element_type=f32,
                 )
                 total = part if total is None else total + part
-        out_refs[side][...] = total
-
-
-def partial(blocks, rows, before):
+        out_refs[side][...] = total.astype(out_refs[side].dtype)
+
+
+def partial(blocks, rows, before, kind=f32):
     count, sides = len(blocks), len(rows)
     halves = [w for _, pair in blocks for w in pair]
     tokens, depth = rows[0].shape[0], 2 * halves[0].shape[0]
@@ -126,7 +126,7 @@
     operands = [*halves, *rows, *(before or [])]
     return pl.pallas_call(
         functools.partial(partial_kernel, [d for d, _ in blocks], sides, carried),
-        out_shape=[jax.ShapeDtypeStruct((tokens, WIDE), f32)] * sides,
+        out_shape=[jax.ShapeDtypeStruct((tokens, WIDE), kind)] * sides,
         in_specs=[VMEM] * len(halves)
         + [pl.BlockSpec(memory_space=pl.ANY)] * sides
         + [VMEM] * (sides * carried),
@@ -162,7 +162,7 @@
 
     def product(head):
         own = slice(head * HD, (head + 1) * HD)
-        return mine_ref[:, own] + other_ref[:, own]
+        return mine_ref[:, own] + other_ref[:, own].astype(f32)
 
     def rotated(head):
         values = product(head)
@@ -326,7 +326,7 @@
     last = step
     sums = partial([(-last, (above[0], after(above[1], *sums))), (last, below)], both, sums)
     far[1] = after(far[1], *sums)
-    [other] = partial([(ring // 2, far)], (got,), sums[1:])
+    [other] = partial([(ring // 2, far)], (got,), sums[1:], bf16)
     other = send(other, swap)
     [mine] = partial([(ring // 2, far)], (hidden,), sums[:1])
     mixed = attend(lengths, learner, slot_offset, mine, other, inverse, *rotary())

time: 130 us -> 130 us (level)
  no operation moved by 1% of the time
where the time goes in v10:
time: 130 us; the launch traced here: 129 us
  starting transfers between devices  62.1 us (48%)
  blocking collectives  23.7 us (18%)
  waiting for transfers between devices  22.5 us (17%)
  Pallas kernels  13.7 us (11%)
  local copies, waits for them, and re-layouts  5.61 us (4%)
    ppermute x16, starting transfers between devices, send(): return lax.ppermute(values, 'fsdp', pairs)  57.3 us
    all_to_all x1, blocking collectives, exchange(): lax.all_to_all(blocks, 'dp', split_axis=0, concat_axis=0, tiled=True)  23.7 us
    ppermute x16, waiting for transfers between devices, send(): return lax.ppermute(values, 'fsdp', pairs)  11.5 us
    all_to_all x1, waiting for transfers between devices, exchange(): lax.all_to_all(blocks, 'dp', split_axis=0, concat_axis=0, tiled=True)  11 us
    pallas_call x6, Pallas kernels, partial(): pl.pallas_call(functools.partial(partial_kernel, [d for d, _ in blocks],...  8.53 us
    unnamed x20, local copies, waits for them, and re-layouts  5.61 us
    all_to_all x1, starting transfers between devices, exchange(): lax.all_to_all(blocks, 'dp', split_axis=0, concat_axis=0, tiled=True)  4.75 us
  transfers between devices with their start and end apart: 17, of which 8 were waited for; matrix products, arithmetic and copies ran while one was open for 0% of the time, Pallas kernels for 8%

profile of v10, /device:TPU:8, one launch (start us, length us, event | category | flops | bytes accessed | tf_op | source)
XLA Modules:
  0.0 128.9 jit_solution(10431512302008278038)
XLA Ops:
  0.0 1.9 %collective-permute-start.9 = (bf16[256,8192]{1,0:T(8,128)(2,1)}, bf16[256,8192]{1,0:T(8,128)(2,1)S(1)}, u32[]{:S(2)}, u32[]{:S(2)}) collective-permute-start(bf16[256,8192]{1,0:T(8,128)(2,1)} %refs_2_.3), channel_id=1, source_target_pairs={{0,1},{1,0},{2,3},{3,2},{4,5},{5,4},{6,7},{7,6},{8,9},{9,8},{10,11... | collective-permute-start | bytes 12582920 | tf_op jit(solution)/shard_map/ppermute | solution.py:303
  5.0 10.9 %collective-permute-start.4 = (bf16[256,768]{1,0:T(8,128)(2,1)S(1)}, bf16[256,768]{1,0:T(8,128)(2,1)S(1)}, u32[]{:S(2)}, u32[]{:S(2)}) collective-permute-start(bf16[256,768]{1,0:T(8,128)(2,1)S(1)} %get-tuple-element.23.refs_1_), channel_id=1, source_target_pairs={{0,14},{1,15},{2,0},{3,1},{4,2},{5,3},{6,4},{7,5},{8,6},{9,7},{10,... | collective-permute-start | bytes 1179656 | tf_op jit(solution)/shard_map/ppermute | solution.py:303
  15.9 1.9 %collective-permute-start = (bf16[256,768]{1,0:T(8,128)(2,1)S(1)}, bf16[256,768]{1,0:T(8,128)(2,1)S(1)}, u32[]{:S(2)}, u32[]{:S(2)}) collective-permute-start(bf16[256,768]{1,0:T(8,128)(2,1)S(1)} %get-tuple-element.21.refs_0_), channel_id=1, source_target_pairs={{0,2},{1,3},{2,4},{3,5},{4,6},{5,7},{6,8},{7,9},{8,10},{9,11},{10,... | collective-permute-start | bytes 1179656 | tf_op jit(solution)/shard_map/ppermute | solution.py:303
  17.8 1.9 %collective-permute-start.8 = (bf16[256,768]{1,0:T(8,128)(2,1)S(1)}, bf16[256,768]{1,0:T(8,128)(2,1)S(1)}, u32[]{:S(2)}, u32[]{:S(2)}) collective-permute-start(bf16[256,768]{1,0:T(8,128)(2,1)S(1)} %get-tuple-element.23.refs_1_), channel_id=1, source_target_pairs={{0,2},{1,3},{2,4},{3,5},{4,6},{5,7},{6,8},{7,9},{8,10},{9,11},{10,... | collective-permute-start | bytes 1179656 | tf_op jit(solution)/shard_map/ppermute | solution.py:303
  19.8 5.1 %collective-permute-start.11 = (bf16[256,768]{1,0:T(8,128)(2,1)S(1)}, bf16[256,768]{1,0:T(8,128)(2,1)S(1)}, u32[]{:S(2)}, u32[]{:S(2)}) collective-permute-start(bf16[256,768]{1,0:T(8,128)(2,1)S(1)} %get-tuple-element.21.refs_0_), channel_id=1, source_target_pairs={{0,14},{1,15},{2,0},{3,1},{4,2},{5,3},{6,4},{7,5},{8,6},{9,7},{10,... | collective-permute-start | bytes 1179656 | tf_op jit(solution)/shard_map/ppermute | solution.py:303
  24.9 5.6 %collective-permute-start.5 = (bf16[256,768]{1,0:T(8,128)(2,1)S(1)}, bf16[256,768]{1,0:T(8,128)(2,1)S(1)}, u32[]{:S(2)}, u32[]{:S(2)}) collective-permute-start(bf16[256,768]{1,0:T(8,128)(2,1)S(1)} %collective-permute-done.4.refs_3_), channel_id=1, source_target_pairs={{0,14},{1,15},{2,0},{3,1},{4,2},{5,3},{6,4},{7,5},{8,6},{9,7},{10,... | collective-permute-start | bytes 1179656 | tf_op jit(solution)/shard_map/ppermute | solution.py:303
  32.9 2.2 %copy-done = bf16[256,8192]{1,0:T(8,128)(2,1)S(1)} copy-done((bf16[256,8192]{1,0:T(8,128)(2,1)S(1)}, bf16[256,8192]{1,0:T(8,128)(2,1)}, u32[]{:S(2)}) %copy-start) | copy-done | bytes 4194328
  39.4 1.9 %collective-permute-start.10 = (bf16[256,768]{1,0:T(8,128)(2,1)S(1)}, bf16[256,768]{1,0:T(8,128)(2,1)S(1)}, u32[]{:S(2)}, u32[]{:S(2)}) collective-permute-start(bf16[256,768]{1,0:T(8,128)(2,1)S(1)} %collective-permute-done.8.refs_1_), channel_id=1, source_target_pairs={{0,2},{1,3},{2,4},{3,5},{4,6},{5,7},{6,8},{7,9},{8,10},{9,11},{10,... | collective-permute-start | bytes 1179656 | tf_op jit(solution)/shard_map/ppermute | solution.py:303
  41.3 5.1 %collective-permute-start.13 = (bf16[256,768]{1,0:T(8,128)(2,1)S(1)}, bf16[256,768]{1,0:T(8,128)(2,1)S(1)}, u32[]{:S(2)}, u32[]{:S(2)}) collective-permute-start(bf16[256,768]{1,0:T(8,128)(2,1)S(1)} %collective-permute-done.11.refs_2_), channel_id=1, source_target_pairs={{0,14},{1,15},{2,0},{3,1},{4,2},{5,3},{6,4},{7,5},{8,6},{9,7},{10,... | collective-permute-start | bytes 1179656 | tf_op jit(solution)/shard_map/ppermute | solution.py:303
  46.5 2.8 %collective-permute-start.6 = (bf16[256,768]{1,0:T(8,128)(2,1)S(1)}, bf16[256,768]{1,0:T(8,128)(2,1)S(1)}, u32[]{:S(2)}, u32[]{:S(2)}) collective-permute-start(bf16[256,768]{1,0:T(8,128)(2,1)S(1)} %collective-permute-done.5.refs_3_), channel_id=1, source_target_pairs={{0,14},{1,15},{2,0},{3,1},{4,2},{5,3},{6,4},{7,5},{8,6},{9,7},{10,... | collective-permute-start | bytes 1179656 | tf_op jit(solution)/shard_map/ppermute | solution.py:303
  49.3 3.1 %collective-permute-start.2 = (bf16[256,768]{1,0:T(8,128)(2,1)S(1)}, bf16[256,768]{1,0:T(8,128)(2,1)S(1)}, u32[]{:S(2)}, u32[]{:S(2)}) collective-permute-start(bf16[256,768]{1,0:T(8,128)(2,1)S(1)} %collective-permute-done.1.refs_0_), channel_id=1, source_target_pairs={{0,2},{1,3},{2,4},{3,5},{4,6},{5,7},{6,8},{7,9},{8,10},{9,11},{10,... | collective-permute-start | bytes 1179656 | tf_op jit(solution)/shard_map/ppermute | solution.py:303
  52.3 2.2 %partial_sums.7 = (f32[256,768]{1,0:T(8,128)S(1)}, f32[256,768]{1,0:T(8,128)S(1)}) custom-call(bf16[256,768]{1,0:T(8,128)(2,1)S(1)} %collective-permute-done.refs_0_, bf16[256,768]{1,0:T(8,128)(2,1)S(1)} %collective-permute-done.8.refs_1_, bf16[256,768]{1,0:T(8,128)(2,1)S(1)} %collective-permute-done.11.refs_2_, ...), custom_call_target="tpu_custom_call" | custom-call | flops 805306368 | bytes 5767168 | tf_op jit(solution)/shard_map/partial_sums/pallas_call | solution.py:127
  56.3 1.9 %collective-permute-start.12 = (bf16[256,768]{1,0:T(8,128)(2,1)S(1)}, bf16[256,768]{1,0:T(8,128)(2,1)S(1)}, u32[]{:S(2)}, u32[]{:S(2)}) collective-permute-start(bf16[256,768]{1,0:T(8,128)(2,1)S(1)} %collective-permute-done.10.refs_1_), channel_id=1, source_target_pairs={{0,2},{1,3},{2,4},{3,5},{4,6},{5,7},{6,8},{7,9},{8,10},{9,11},{10,... | collective-permute-start | bytes 1179656 | tf_op jit(solution)/shard_map/ppermute | solution.py:303
  58.2 5.1 %collective-permute-start.14 = (bf16[256,768]{1,0:T(8,128)(2,1)S(1)}, bf16[256,768]{1,0:T(8,128)(2,1)S(1)}, u32[]{:S(2)}, u32[]{:S(2)}) collective-permute-start(bf16[256,768]{1,0:T(8,128)(2,1)S(1)} %collective-permute-done.13.refs_2_), channel_id=1, source_target_pairs={{0,14},{1,15},{2,0},{3,1},{4,2},{5,3},{6,4},{7,5},{8,6},{9,7},{10,... | collective-permute-start | bytes 1179656 | tf_op jit(solution)/shard_map/ppermute | solution.py:303
  63.3 4.1 %collective-permute-start.7 = (bf16[256,768]{1,0:T(8,128)(2,1)S(1)}, bf16[256,768]{1,0:T(8,128)(2,1)S(1)}, u32[]{:S(2)}, u32[]{:S(2)}) collective-permute-start(bf16[256,768]{1,0:T(8,128)(2,1)S(1)} %collective-permute-done.6.refs_3_), channel_id=1, source_target_pairs={{0,14},{1,15},{2,0},{3,1},{4,2},{5,3},{6,4},{7,5},{8,6},{9,7},{10,... | collective-permute-start | bytes 1179656 | tf_op jit(solution)/shard_map/ppermute | solution.py:303
  67.4 1.9 %collective-permute-start.3 = (bf16[256,768]{1,0:T(8,128)(2,1)S(1)}, bf16[256,768]{1,0:T(8,128)(2,1)S(1)}, u32[]{:S(2)}, u32[]{:S(2)}) collective-permute-start(bf16[256,768]{1,0:T(8,128)(2,1)S(1)} %collective-permute-done.2.refs_0_), channel_id=1, source_target_pairs={{0,2},{1,3},{2,4},{3,5},{4,6},{5,7},{6,8},{7,9},{8,10},{9,11},{10,... | collective-permute-start | bytes 1179656 | tf_op jit(solution)/shard_map/ppermute | solution.py:303
  69.4 2.2 %partial_sums.8 = (f32[256,768]{1,0:T(8,128)S(1)}, f32[256,768]{1,0:T(8,128)S(1)}) custom-call(bf16[256,768]{1,0:T(8,128)(2,1)S(1)} %collective-permute-done.1.refs_0_, bf16[256,768]{1,0:T(8,128)(2,1)S(1)} %collective-permute-done.10.refs_1_, bf16[256,768]{1,0:T(8,128)(2,1)S(1)} %collective-permute-done.13.refs_2_, ...), custom_call_target="tpu_custom_call" | custom-call | flops 805306368 | bytes 5767168 | tf_op jit(solution)/shard_map/partial_sums/pallas_call | solution.py:127
  73.1 2.2 %partial_sums.9 = (f32[256,768]{1,0:T(8,128)S(1)}, f32[256,768]{1,0:T(8,128)S(1)}) custom-call(bf16[256,768]{1,0:T(8,128)(2,1)S(1)} %collective-permute-done.2.refs_0_, bf16[256,768]{1,0:T(8,128)(2,1)S(1)} %collective-permute-done.12.refs_1_, bf16[256,768]{1,0:T(8,128)(2,1)S(1)} %collective-permute-done.14.refs_2_, ...), custom_call_target="tpu_custom_call" | custom-call | flops 805306368 | bytes 5767168 | tf_op jit(solution)/shard_map/partial_sums/pallas_call | solution.py:127
  75.3 3.4 %collective-permute-done.7.refs_1_ = bf16[256,768]{1,0:T(8,128)(2,1)S(1)} collective-permute-done((bf16[256,768]{1,0:T(8,128)(2,1)S(1)}, bf16[256,768]{1,0:T(8,128)(2,1)S(1)}, u32[]{:S(2)}, u32[]{:S(2)}) %collective-permute-start.7) | collective-permute-done | bytes 393248 | tf_op jit(solution)/shard_map/ppermute | solution.py:303
  78.7 2.1 %collective-permute-done.3.refs_0_ = bf16[256,768]{1,0:T(8,128)(2,1)S(1)} collective-permute-done((bf16[256,768]{1,0:T(8,128)(2,1)S(1)}, bf16[256,768]{1,0:T(8,128)(2,1)S(1)}, u32[]{:S(2)}, u32[]{:S(2)}) %collective-permute-start.3) | collective-permute-done | bytes 393248 | tf_op jit(solution)/shard_map/ppermute | solution.py:303
  81.3 2.1 %collective-permute-start.15 = (bf16[256,768]{1,0:T(8,128)(2,1)S(1)}, bf16[256,768]{1,0:T(8,128)(2,1)S(1)}, u32[]{:S(2)}, u32[]{:S(2)}) collective-permute-start(bf16[256,768]{1,0:T(8,128)(2,1)S(1)} %partial_sums.11), channel_id=1, source_target_pairs={{0,1},{1,0},{2,3},{3,2},{4,5},{5,4},{6,7},{7,6},{8,9},{9,8},{10,11... | collective-permute-start | bytes 1179656 | tf_op jit(solution)/shard_map/ppermute | solution.py:303
  86.9 23.7 %all_to_all.10 = bf16[32,8,640]{2,1,0:T(8,128)(2,1)S(1)} all-to-all(bf16[32,8,640]{2,1,0:T(8,128)(2,1)S(1)} %bitcast.10), channel_id=1, replica_groups=mesh['dp'=32,'fsdp'=16] {'dp'}, dimensions={0} | all-to-all | bytes 655360 | tf_op jit(solution)/shard_map/all_to_all | solution.py:291
  111.7 4.8 %all-to-all-start.1 = ((bf16[32,8,512]{2,1,0:T(8,128)(2,1)}), bf16[32,8,512]{2,1,0:T(8,128)(2,1)S(1)}, u32[]{:S(2)}, u32[]{:S(2)}) async-start(bf16[32,8,512]{2,1,0:T(8,128)(2,1)} %bitcast.3), calls=%async_computation.1 | async-start | bytes 524288 | tf_op jit(solution)/shard_map/all_to_all | solution.py:291
  117.0 11.0 %all-to-all-done.1 = bf16[32,8,512]{2,1,0:T(8,128)(2,1)S(1)} async-done(((bf16[32,8,512]{2,1,0:T(8,128)(2,1)}), bf16[32,8,512]{2,1,0:T(8,128)(2,1)S(1)}, u32[]{:S(2)}, u32[]{:S(2)}) %all-to-all-start.1) | async-done | bytes 262176 | tf_op jit(solution)/shard_map/all_to_all | solution.py:291
  (43 shorter events, 19.4 us)
Async XLA Ops:
  0.0 36.5 %collective-permute-start.9 = (bf16[256,8192]{1,0:T(8,128)(2,1)}, bf16[256,8192]{1,0:T(8,128)(2,1)S(1)}, u32[]{:S(2)}, u32[]{:S(2)}) collective-permute-start(bf16[256,8192]{1,0:T(8,128)(2,1)} %refs_2_.3), channel_id=1, source_target_pairs={{0,1},{1,0},{2,3},{3,2},{4,5},{5,4},{6,7},{7,6},{8,9},{9,8},{10,11... | collective-permute-start | bytes 12582920 | tf_op jit(solution)/shard_map/ppermute | solution.py:303
  5.0 20.0 %collective-permute-start.4 = (bf16[256,768]{1,0:T(8,128)(2,1)S(1)}, bf16[256,768]{1,0:T(8,128)(2,1)S(1)}, u32[]{:S(2)}, u32[]{:S(2)}) collective-permute-start(bf16[256,768]{1,0:T(8,128)(2,1)S(1)} %get-tuple-element.23.refs_1_), channel_id=1, source_target_pairs={{0,14},{1,15},{2,0},{3,1},{4,2},{5,3},{6,4},{7,5},{8,6},{9,7},{10,... | collective-permute-start | bytes 1179656 | tf_op jit(solution)/shard_map/ppermute | solution.py:303
  15.9 15.1 %collective-permute-start = (bf16[256,768]{1,0:T(8,128)(2,1)S(1)}, bf16[256,768]{1,0:T(8,128)(2,1)S(1)}, u32[]{:S(2)}, u32[]{:S(2)}) collective-permute-start(bf16[256,768]{1,0:T(8,128)(2,1)S(1)} %get-tuple-element.21.refs_0_), channel_id=1, source_target_pairs={{0,2},{1,3},{2,4},{3,5},{4,6},{5,7},{6,8},{7,9},{8,10},{9,11},{10,... | collective-permute-start | bytes 1179656 | tf_op jit(solution)/shard_map/ppermute | solution.py:303
  17.8 21.5 %collective-permute-start.8 = (bf16[256,768]{1,0:T(8,128)(2,1)S(1)}, bf16[256,768]{1,0:T(8,128)(2,1)S(1)}, u32[]{:S(2)}, u32[]{:S(2)}) collective-permute-start(bf16[256,768]{1,0:T(8,128)(2,1)S(1)} %get-tuple-element.23.refs_1_), channel_id=1, source_target_pairs={{0,2},{1,3},{2,4},{3,5},{4,6},{5,7},{6,8},{7,9},{8,10},{9,11},{10,... | collective-permute-start | bytes 1179656 | tf_op jit(solution)/shard_map/ppermute | solution.py:303
  19.8 21.5 %collective-permute-start.11 = (bf16[256,768]{1,0:T(8,128)(2,1)S(1)}, bf16[256,768]{1,0:T(8,128)(2,1)S(1)}, u32[]{:S(2)}, u32[]{:S(2)}) collective-permute-start(bf16[256,768]{1,0:T(8,128)(2,1)S(1)} %get-tuple-element.21.refs_0_), channel_id=1, source_target_pairs={{0,14},{1,15},{2,0},{3,1},{4,2},{5,3},{6,4},{7,5},{8,6},{9,7},{10,... | collective-permute-start | bytes 1179656 | tf_op jit(solution)/shard_map/ppermute | solution.py:303
  24.9 21.5 %collective-permute-start.5 = (bf16[256,768]{1,0:T(8,128)(2,1)S(1)}, bf16[256,768]{1,0:T(8,128)(2,1)S(1)}, u32[]{:S(2)}, u32[]{:S(2)}) collective-permute-start(bf16[256,768]{1,0:T(8,128)(2,1)S(1)} %collective-permute-done.4.refs_3_), channel_id=1, source_target_pairs={{0,14},{1,15},{2,0},{3,1},{4,2},{5,3},{6,4},{7,5},{8,6},{9,7},{10,... | collective-permute-start | bytes 1179656 | tf_op jit(solution)/shard_map/ppermute | solution.py:303
  31.0 18.3 %collective-permute-start.1 = (bf16[256,768]{1,0:T(8,128)(2,1)S(1)}, bf16[256,768]{1,0:T(8,128)(2,1)S(1)}, u32[]{:S(2)}, u32[]{:S(2)}) collective-permute-start(bf16[256,768]{1,0:T(8,128)(2,1)S(1)} %collective-permute-done.refs_0_), channel_id=1, source_target_pairs={{0,2},{1,3},{2,4},{3,5},{4,6},{5,7},{6,8},{7,9},{8,10},{9,11},{10,... | collective-permute-start | bytes 1179656 | tf_op jit(solution)/shard_map/ppermute | solution.py:303
  32.9 2.2 %copy-start = (bf16[256,8192]{1,0:T(8,128)(2,1)S(1)}, bf16[256,8192]{1,0:T(8,128)(2,1)}, u32[]{:S(2)}) copy-start(bf16[256,8192]{1,0:T(8,128)(2,1)} %refs_2_.3) | copy-start | bytes 12582916
  35.1 2.2 %copy-start.1 = (bf16[256,8192]{1,0:T(8,128)(2,1)S(1)}, bf16[256,8192]{1,0:T(8,128)(2,1)}, u32[]{:S(2)}) copy-start(bf16[256,8192]{1,0:T(8,128)(2,1)} %refs_2_.3) | copy-start | bytes 12582916
  39.4 16.9 %collective-permute-start.10 = (bf16[256,768]{1,0:T(8,128)(2,1)S(1)}, bf16[256,768]{1,0:T(8,128)(2,1)S(1)}, u32[]{:S(2)}, u32[]{:S(2)}) collective-permute-start(bf16[256,768]{1,0:T(8,128)(2,1)S(1)} %collective-permute-done.8.refs_1_), channel_id=1, source_target_pairs={{0,2},{1,3},{2,4},{3,5},{4,6},{5,7},{6,8},{7,9},{8,10},{9,11},{10,... | collective-permute-start | bytes 1179656 | tf_op jit(solution)/shard_map/ppermute | solution.py:303
  41.3 16.8 %collective-permute-start.13 = (bf16[256,768]{1,0:T(8,128)(2,1)S(1)}, bf16[256,768]{1,0:T(8,128)(2,1)S(1)}, u32[]{:S(2)}, u32[]{:S(2)}) collective-permute-start(bf16[256,768]{1,0:T(8,128)(2,1)S(1)} %collective-permute-done.11.refs_2_), channel_id=1, source_target_pairs={{0,14},{1,15},{2,0},{3,1},{4,2},{5,3},{6,4},{7,5},{8,6},{9,7},{10,... | collective-permute-start | bytes 1179656 | tf_op jit(solution)/shard_map/ppermute | solution.py:303
  46.5 16.8 %collective-permute-start.6 = (bf16[256,768]{1,0:T(8,128)(2,1)S(1)}, bf16[256,768]{1,0:T(8,128)(2,1)S(1)}, u32[]{:S(2)}, u32[]{:S(2)}) collective-permute-start(bf16[256,768]{1,0:T(8,128)(2,1)S(1)} %collective-permute-done.5.refs_3_), channel_id=1, source_target_pairs={{0,14},{1,15},{2,0},{3,1},{4,2},{5,3},{6,4},{7,5},{8,6},{9,7},{10,... | collective-permute-start | bytes 1179656 | tf_op jit(solution)/shard_map/ppermute | solution.py:303
  49.3 18.2 %collective-permute-start.2 = (bf16[256,768]{1,0:T(8,128)(2,1)S(1)}, bf16[256,768]{1,0:T(8,128)(2,1)S(1)}, u32[]{:S(2)}, u32[]{:S(2)}) collective-permute-start(bf16[256,768]{1,0:T(8,128)(2,1)S(1)} %collective-permute-done.1.refs_0_), channel_id=1, source_target_pairs={{0,2},{1,3},{2,4},{3,5},{4,6},{5,7},{6,8},{7,9},{8,10},{9,11},{10,... | collective-permute-start | bytes 1179656 | tf_op jit(solution)/shard_map/ppermute | solution.py:303
  56.3 16.9 %collective-permute-start.12 = (bf16[256,768]{1,0:T(8,128)(2,1)S(1)}, bf16[256,768]{1,0:T(8,128)(2,1)S(1)}, u32[]{:S(2)}, u32[]{:S(2)}) collective-permute-start(bf16[256,768]{1,0:T(8,128)(2,1)S(1)} %collective-permute-done.10.refs_1_), channel_id=1, source_target_pairs={{0,2},{1,3},{2,4},{3,5},{4,6},{5,7},{6,8},{7,9},{8,10},{9,11},{10,... | collective-permute-start | bytes 1179656 | tf_op jit(solution)/shard_map/ppermute | solution.py:303
  58.2 14.9 %collective-permute-start.14 = (bf16[256,768]{1,0:T(8,128)(2,1)S(1)}, bf16[256,768]{1,0:T(8,128)(2,1)S(1)}, u32[]{:S(2)}, u32[]{:S(2)}) collective-permute-start(bf16[256,768]{1,0:T(8,128)(2,1)S(1)} %collective-permute-done.13.refs_2_), channel_id=1, source_target_pairs={{0,14},{1,15},{2,0},{3,1},{4,2},{5,3},{6,4},{7,5},{8,6},{9,7},{10,... | collective-permute-start | bytes 1179656 | tf_op jit(solution)/shard_map/ppermute | solution.py:303
  63.3 15.3 %collective-permute-start.7 = (bf16[256,768]{1,0:T(8,128)(2,1)S(1)}, bf16[256,768]{1,0:T(8,128)(2,1)S(1)}, u32[]{:S(2)}, u32[]{:S(2)}) collective-permute-start(bf16[256,768]{1,0:T(8,128)(2,1)S(1)} %collective-permute-done.6.refs_3_), channel_id=1, source_target_pairs={{0,14},{1,15},{2,0},{3,1},{4,2},{5,3},{6,4},{7,5},{8,6},{9,7},{10,... | collective-permute-start | bytes 1179656 | tf_op jit(solution)/shard_map/ppermute | solution.py:303
  67.4 13.4 %collective-permute-start.3 = (bf16[256,768]{1,0:T(8,128)(2,1)S(1)}, bf16[256,768]{1,0:T(8,128)(2,1)S(1)}, u32[]{:S(2)}, u32[]{:S(2)}) collective-permute-start(bf16[256,768]{1,0:T(8,128)(2,1)S(1)} %collective-permute-done.2.refs_0_), channel_id=1, source_target_pairs={{0,2},{1,3},{2,4},{3,5},{4,6},{5,7},{6,8},{7,9},{8,10},{9,11},{10,... | collective-permute-start | bytes 1179656 | tf_op jit(solution)/shard_map/ppermute | solution.py:303
  81.3 3.8 %copy-start.4 = (f32[128,128]{1,0:T(8,128)S(1)}, f32[128,128]{1,0:T(8,128)}, u32[]{:S(2)}) copy-start(f32[128,128]{1,0:T(8,128)} %constant.10.clone.cosine_ref) | copy-start | bytes 196612
  81.3 3.8 %copy-start.5 = (f32[128,128]{1,0:T(8,128)S(1)}, f32[128,128]{1,0:T(8,128)}, u32[]{:S(2)}) copy-start(f32[128,128]{1,0:T(8,128)} %constant.11.clone.sine_ref) | copy-start | bytes 196612
  81.3 3.8 %copy-start.7 = (s32[4]{0:T(128)S(1)}, s32[4]{0:T(128)}, u32[]{:S(2)}) copy-start(s32[4]{0:T(128)} %lengths_ref.1) | copy-start | bytes 52
  81.3 3.8 %copy-start.8 = (s32[4]{0:T(128)S(1)}, s32[4]{0:T(128)}, u32[]{:S(2)}) copy-start(s32[4]{0:T(128)} %learner_ref.1) | copy-start | bytes 52
  81.3 3.8 %copy-start.9 = (s32[4]{0:T(128)S(1)}, s32[4]{0:T(128)}, u32[]{:S(2)}) copy-start(s32[4]{0:T(128)} %offset_ref.1) | copy-start | bytes 52
  81.3 3.7 %collective-permute-start.15 = (bf16[256,768]{1,0:T(8,128)(2,1)S(1)}, bf16[256,768]{1,0:T(8,128)(2,1)S(1)}, u32[]{:S(2)}, u32[]{:S(2)}) collective-permute-start(bf16[256,768]{1,0:T(8,128)(2,1)S(1)} %partial_sums.11), channel_id=1, source_target_pairs={{0,1},{1,0},{2,3},{3,2},{4,5},{5,4},{6,7},{7,6},{8,9},{9,8},{10,11... | collective-permute-start | bytes 1179656 | tf_op jit(solution)/shard_map/ppermute | solution.py:303
  111.7 16.2 %all-to-all-start.1 = ((bf16[32,8,512]{2,1,0:T(8,128)(2,1)}), bf16[32,8,512]{2,1,0:T(8,128)(2,1)S(1)}, u32[]{:S(2)}, u32[]{:S(2)}) async-start(bf16[32,8,512]{2,1,0:T(8,128)(2,1)} %bitcast.3), calls=%async_computation.1 | async-start | bytes 524288 | tf_op jit(solution)/shard_map/all_to_all | solution.py:291
  (3 other events, 2.7 us)
